TPU v7x, 256 devices: a whole 4x4x8 slice. The times are simulated.
256 devices in a mesh: row: 2 (over core), col: 8 (over z), layer: 16 (over y, x).
Axes of the slice: x: 4, y: 4, z: 8, core: 2. Of those that a mesh axis runs over, the one named last changes fastest.
Arguments:
- panel_top: float32 [16, 1024, 1024], P('layer', 'row', 'col'), as said below
- panel_win: float32 [16, 2048, 1024], P('layer', 'col', 'row'), may hold values from -0.375 to 0.375
- panel_rest: float32 [16, 2688, 1024], P('layer', 'row', 'col'), may hold values from -0.375 to 0.375
- trail_rest: float32 [16, 2688, 2048], P('layer', 'row', 'col'), may hold values from -2 to 2
Outputs:
- factor_top: float32 [1024, 1024], P('row', 'col')
- factor_win: float32 [2048, 1024], P('col', 'row')
- factor_rest: float32 [2688, 1024], P(('row', 'layer'), 'col')
- schur: float32 [2688, 2048], P(('row', 'layer'), 'col')
Inputs may be any that keep to these rules, and one draw needn't show every extreme that they name: `panel_top`: each layer's block is symmetric, and the sum over the layers is positive definite with no eigenvalue under 0.25.
All inputs are finite; a program needn't handle non-finite values.
Results may differ from a plain program's by a relative error of at most 0.00021.
Values sent between devices are 32-bit elements; how exact they have to be, the bound alone decides.
No kernel may reach another device: no remote copies, remote signals or barrier semaphores. Data moves between devices by JAX's collectives and lax.ppermute only.
A program may use at most 128 MiB of HBM per device.

v0:
```python
import jax
import jax.numpy as jnp
from jax import lax
from jax.sharding import PartitionSpec as P


def solve_right(factor, values):
    return jax.scipy.linalg.solve_triangular(factor, values.T, lower=True).T


def per_device(panel_top, panel_win, panel_rest, trail_rest):
    top_sum, win_sum = lax.psum((panel_top[0], panel_win[0]), "layer")
    rows_here, cols_here = top_sum.shape
    n_row = lax.axis_size("row")
    top_rows = lax.all_gather(top_sum, "row", axis=0, tiled=True)
    top_full = lax.all_gather(top_rows, "col", axis=1, tiled=True)
    factor_top = jnp.linalg.cholesky(top_full)
    window = lax.all_gather(win_sum, "row", axis=1, tiled=True)
    factor_win = solve_right(factor_top, window)
    rest_part = lax.psum_scatter(panel_rest[0], "layer", scatter_dimension=0, tiled=True)
    rest_full = lax.all_gather(rest_part, "col", axis=1, tiled=True)
    factor_rest = solve_right(factor_top, rest_full)
    panel_cols = factor_top.shape[1]
    shares = lax.all_to_all(factor_rest, "layer", split_axis=1, concat_axis=0, tiled=True)
    share_cols = panel_cols // lax.axis_size("layer")
    win_share = lax.dynamic_slice_in_dim(
        factor_win, lax.axis_index("layer") * share_cols, share_cols, 1
    )
    partial_trail = trail_rest[0]
    schur = lax.psum_scatter(
        partial_trail
        - jnp.dot(
            shares, win_share.T, precision=lax.Precision.HIGHEST, preferred_element_type=jnp.float32
        ),
        "layer",
        scatter_dimension=0,
        tiled=True,
    )
    top_block = lax.dynamic_slice(
        factor_top,
        (lax.axis_index("row") * rows_here, lax.axis_index("col") * cols_here),
        (rows_here, cols_here),
    )
    row_cols = panel_cols // n_row
    win_block = lax.dynamic_slice_in_dim(factor_win, lax.axis_index("row") * row_cols, row_cols, 1)
    rest_block = lax.dynamic_slice_in_dim(
        factor_rest, lax.axis_index("col") * cols_here, cols_here, 1
    )
    return (top_block, win_block, rest_block, schur)


def solution(mesh):
    return jax.shard_map(
        per_device,
        mesh=mesh,
        in_specs=(
            P("layer", "row", "col"),
            P("layer", "col", "row"),
            P("layer", "row", "col"),
            P("layer", "row", "col"),
        ),
        out_specs=(
            P("row", "col"),
            P("col", "row"),
            P(("row", "layer"), "col"),
            P(("row", "layer"), "col"),
        ),
        check_vma=False,
    )
```

profile of v0, /device:TPU:1, one launch (start us, length us, event | category | flops | bytes accessed | tf_op | source)
XLA Modules:
  0.0 615.6 jit_solution(10585900240212755345)
XLA Ops:
  9.0 2.0 copy.18
  11.1 99.5 %all-reduce.8.cloned.1.call-done = (f32[512,128]{0,1:T(8,128)}, f32[256,512]{0,1:T(8,128)}) async-done(((f32[512,128]{0,1:T(8,128)}, f32[256,512]{0,1:T(8,128)}), (f32[512,128]{0,1:T(8,128)}, f32[256,512]{0,1:T(8,128)})) %all-reduce.8.cloned.1.call-update) | async-done | bytes 786448 | tf_op jit(solution)/shard_map/psum | solution.py:12
  110.7 5.7 all_gather.12
  116.5 42.7 %fusion = f32[96,128]{1,0:T(8,128)S(1)} fusion(f32[1344,128]{1,0:T(8,128)} %bitcast.168), kind=kCustom, calls=%all-reduce-scatter | all-reduce-scatter fusion | flops 196609 | bytes 738304
  161.0 3.9 collective-permute-start.1
  166.7 21.0 %all_gather.15 = f32[84,1024]{1,0:T(8,128)S(1)} all-gather(f32[84,128]{1,0:T(8,128)S(1)} %constant_dynamic-slice_fusion.2), channel_id=1, replica_groups=mesh['row'=2,'col'=8,'layer'=16] {'col'}, dimensions={1}, use_global_device_ids=true | all-gather | bytes 387072 | tf_op jit(solution)/shard_map/all_gather | solution.py:21
  187.7 5.5 copy.17
  193.2 4.4 fusion.2
  197.7 1.9 copy-done.1
  199.6 11.7 %cholesky.223 = f32[128,128]{1,0:T(8,128)S(1)} custom-call(f32[128,128]{1,0:T(8,128)S(1)} %cholesky.580), custom_call_target="Cholesky" | custom-call | tf_op jit(solution)/shard_map/jit(cholesky)/cholesky | solution.py:17
  211.3 2.5 cholesky.255
  213.8 9.8 %custom-call.66 = f32[1,128,128]{1,2,0:T(8,128)S(1)} custom-call(f32[1,128,128]{2,1,0:T(8,128)S(1)} %get-tuple-element.84), custom_call_target="InvertDiagBlocksLowerTriangular" | custom-call | tf_op jit(solution)/shard_map/jit(cholesky)/cholesky | solution.py:17
  223.7 2.3 constant_dynamic-update-slice_fusion.54
  227.6 11.9 %cholesky.244 = f32[128,128]{1,0:T(8,128)S(1)} custom-call(f32[128,128]{1,0:T(8,128)S(1)} %cholesky.584), custom_call_target="Cholesky" | custom-call | tf_op jit(solution)/shard_map/jit(cholesky)/cholesky | solution.py:17
  240.1 9.8 %custom-call.67 = f32[1,128,128]{1,2,0:T(8,128)S(1)} custom-call(f32[1,128,128]{2,1,0:T(8,128)S(1)} %get-tuple-element.81), custom_call_target="InvertDiagBlocksLowerTriangular" | custom-call | tf_op jit(solution)/shard_map/jit(cholesky)/cholesky | solution.py:17
  251.2 2.1 convolution_subtract_fusion.2
  253.3 11.7 %cholesky.468 = f32[128,128]{1,0:T(8,128)S(1)} custom-call(f32[128,128]{1,0:T(8,128)S(1)} %cholesky.589), custom_call_target="Cholesky" | custom-call | tf_op jit(solution)/shard_map/jit(cholesky)/cholesky | solution.py:17
  265.6 9.8 %custom-call.68 = f32[1,128,128]{1,2,0:T(8,128)S(1)} custom-call(f32[1,128,128]{2,1,0:T(8,128)S(1)} %get-tuple-element.78), custom_call_target="InvertDiagBlocksLowerTriangular" | custom-call | tf_op jit(solution)/shard_map/jit(cholesky)/cholesky | solution.py:17
  276.6 2.3 convolution_subtract_fusion.3
  279.0 12.1 %cholesky.487 = f32[128,128]{1,0:T(8,128)S(1)} custom-call(f32[128,128]{1,0:T(8,128)S(1)} %cholesky.594), custom_call_target="Cholesky" | custom-call | tf_op jit(solution)/shard_map/jit(cholesky)/cholesky | solution.py:17
  291.7 9.8 %custom-call.69 = f32[1,128,128]{1,2,0:T(8,128)S(1)} custom-call(f32[1,128,128]{2,1,0:T(8,128)S(1)} %get-tuple-element.75), custom_call_target="InvertDiagBlocksLowerTriangular" | custom-call | tf_op jit(solution)/shard_map/jit(cholesky)/cholesky | solution.py:17
  302.6 2.3 convolution_subtract_fusion.4
  305.0 11.7 %cholesky.506 = f32[128,128]{1,0:T(8,128)S(1)} custom-call(f32[128,128]{1,0:T(8,128)S(1)} %cholesky.599), custom_call_target="Cholesky" | custom-call | tf_op jit(solution)/shard_map/jit(cholesky)/cholesky | solution.py:17
  317.4 10.0 %custom-call.70 = f32[1,128,128]{1,2,0:T(8,128)S(1)} custom-call(f32[1,128,128]{2,1,0:T(8,128)S(1)} %get-tuple-element.72), custom_call_target="InvertDiagBlocksLowerTriangular" | custom-call | tf_op jit(solution)/shard_map/jit(cholesky)/cholesky | solution.py:17
  328.3 2.3 convolution_subtract_fusion.5
  330.6 11.7 %cholesky.526 = f32[128,128]{1,0:T(8,128)S(1)} custom-call(f32[128,128]{1,0:T(8,128)S(1)} %cholesky.604), custom_call_target="Cholesky" | custom-call | tf_op jit(solution)/shard_map/jit(cholesky)/cholesky | solution.py:17
  343.0 9.8 %custom-call.71 = f32[1,128,128]{1,2,0:T(8,128)S(1)} custom-call(f32[1,128,128]{2,1,0:T(8,128)S(1)} %get-tuple-element.69), custom_call_target="InvertDiagBlocksLowerTriangular" | custom-call | tf_op jit(solution)/shard_map/jit(cholesky)/cholesky | solution.py:17
  353.8 2.0 convolution_subtract_fusion.12
  355.8 11.7 %cholesky.546 = f32[128,128]{1,0:T(8,128)S(1)} custom-call(f32[128,128]{1,0:T(8,128)S(1)} %cholesky.609), custom_call_target="Cholesky" | custom-call | tf_op jit(solution)/shard_map/jit(cholesky)/cholesky | solution.py:17
  368.2 9.8 %custom-call.72 = f32[1,128,128]{1,2,0:T(8,128)S(1)} custom-call(f32[1,128,128]{2,1,0:T(8,128)S(1)} %get-tuple-element.66), custom_call_target="InvertDiagBlocksLowerTriangular" | custom-call | tf_op jit(solution)/shard_map/jit(cholesky)/cholesky | solution.py:17
  380.6 11.7 %cholesky.564 = f32[128,128]{1,0:T(8,128)S(1)} custom-call(f32[128,128]{1,0:T(8,128)S(1)} %convolution_subtract_fusion.14), custom_call_target="Cholesky" | custom-call | tf_op jit(solution)/shard_map/jit(cholesky)/cholesky | solution.py:17
  402.7 6.6 %fusion.3 = (f32[1024,1024]{1,0:T(8,128)}, f32[1024,1024]{1,0:T(8,128)}) fusion(f32[1024,1024]{1,0:T(8,128)} %get-tuple-element.64, pred[]{:T(512)S(6)} %cholesky.579), kind=kLoop, calls=%fused_computation.6 | loop fusion | flops 4194304 | bytes 12582913 | tf_op jit(solution)/shard_map/jit(_solve_triangular)/triangular_solve | solution.py:8
  409.3 23.2 %while.1 = (s32[]{:T(128)}, f32[1024,1024]{1,0:T(8,128)}, s32[8,2]{0,1:T(2,128)S(1)}, f32[8,128,128]{2,1,0:T(8,128)S(1)}, s32[]{:T(128)}) while((s32[]{:T(128)}, f32[1024,1024]{1,0:T(8,128)}, s32[8,2]{0,1:T(2,128)S(1)}, f32[8,128,128]{2,1,0:T(8,128)S(1)}, s32[]{:T(128)}) %tuple.87), condition=%wide.while_cond, body=%wide.while_body.sunk | while | flops 2 | bytes 131189 | solution.py:8
  409.9 2.3 bitcast_dynamic-update-slice_fusion.2
  412.8 2.3 bitcast_dynamic-update-slice_fusion.2
  415.7 2.3 bitcast_dynamic-update-slice_fusion.2
  418.6 2.3 bitcast_dynamic-update-slice_fusion.2
  421.5 2.3 bitcast_dynamic-update-slice_fusion.2
  424.4 2.3 bitcast_dynamic-update-slice_fusion.2
  427.3 2.3 bitcast_dynamic-update-slice_fusion.2
  430.2 2.2 bitcast_dynamic-update-slice_fusion.2
  432.5 78.8 %custom-call.73 = f32[8,128,128]{1,2,0:T(8,128)S(1)} custom-call(f32[8,128,128]{2,1,0:T(8,128)S(1)} %get-tuple-element.11), custom_call_target="InvertDiagBlocksLowerTriangular" | custom-call | tf_op jit(solution)/shard_map/jit(_solve_triangular)/triangular_solve | solution.py:8
  526.9 7.0 %all-to-all-start = ((f32[84,16,64]{0,2,1:T(8,128)}), f32[84,16,64]{0,2,1:T(8,128)S(1)}, u32[]{:S(2)}, u32[]{:S(2)}) async-start(f32[84,16,64]{0,2,1:T(8,128)} %bitcast.32), calls=%async_computation | async-start | bytes 1048576 | tf_op jit(solution)/shard_map/all_to_all | solution.py:24
  538.6 4.3 all-to-all-done
  543.5 2.1 convolution_subtract_fusion
  545.6 53.0 %fusion.1 = f32[96,256]{1,0:T(8,128)S(1)} fusion(f32[1344,256]{1,0:T(8,128)S(1)} %convolution_subtract_fusion), kind=kCustom, calls=%all-reduce-scatter.1 | all-reduce-scatter fusion | flops 393217 | bytes 1475584
  598.6 2.7 collective-permute-start.2
  601.3 4.3 collective-permute-start.3
  (118 shorter events, 52.0 us)
Async XLA Ops:
  7.2 157.8 %copy-start.5 = (u32[256]{0:T(256)S(1)}, u32[256]{0:T(256)}, u32[]{:S(2)}) copy-start(u32[256]{0:T(256)} %constant.330) | copy-start | bytes 3076
  7.2 103.5 %all-reduce.8.cloned.1.call-start = ((), (), s32[]{:S(2)}) async-start(), calls=%async_computation.3 | async-start | bytes 1572864 | tf_op jit(solution)/shard_map/psum | solution.py:12
  11.1 176.6 %all-gather.3.cloned.1.call-start = ((), (), s32[]{:S(2)}) async-start(), calls=%async_computation.1 | async-start | bytes 4718592 | tf_op jit(solution)/shard_map/all_gather | solution.py:16
  116.4 395.0 %all-gather.5.cloned.1.call-start = ((), (), s32[]{:S(2)}) async-start(), calls=%async_computation.2 | async-start | bytes 1572864 | tf_op jit(solution)/shard_map/all_gather | solution.py:18
  159.2 7.0 %collective-permute-start = (f32[96,128]{1,0:T(8,128)S(1)}, f32[96,128]{1,0:T(8,128)S(1)}, u32[]{:S(2)}, u32[]{:S(2)}) collective-permute-start(f32[96,128]{1,0:T(8,128)S(1)} %fusion), channel_id=1, source_target_pairs={{0,1},{1,2},{2,3},{3,4},{4,5},{5,6},{6,7},{7,8},{8,9},{9,10},{10,1... | collective-permute-start | bytes 147464
  161.0 5.2 collective-permute-start.1
  197.7 1.9 copy-start.1
  511.4 6.5 %copy-start = (f32[1024,1024]{1,0:T(8,128)S(1)}, f32[1024,1024]{1,0:T(8,128)}, u32[]{:S(2)}) copy-start(f32[1024,1024]{1,0:T(8,128)} %get-tuple-element.173) | copy-start | bytes 12582916
  511.4 6.5 %copy-start.3 = (f32[256,1024]{0,1:T(8,128)S(1)}, f32[256,1024]{0,1:T(8,128)}, u32[]{:S(2)}) copy-start(f32[256,1024]{0,1:T(8,128)} %all-gather.5.cloned.1.call-done) | copy-start | bytes 3145732
  520.3 5.6 copy-start.4
  524.7 18.7 %copy-start.2 = (f32[1,1344,256]{2,1,0:T(8,128)S(1)}, f32[1,1344,256]{2,1,0:T(8,128)}, u32[]{:S(2)}) copy-start(f32[1,1344,256]{2,1,0:T(8,128)} %param.7) | copy-start | bytes 4128772
  526.9 16.0 %all-to-all-start = ((f32[84,16,64]{0,2,1:T(8,128)}), f32[84,16,64]{0,2,1:T(8,128)S(1)}, u32[]{:S(2)}, u32[]{:S(2)}) async-start(f32[84,16,64]{0,2,1:T(8,128)} %bitcast.32), calls=%async_computation | async-start | bytes 1048576 | tf_op jit(solution)/shard_map/all_to_all | solution.py:24
  598.6 8.9 %collective-permute-start.2 = (f32[96,256]{1,0:T(8,128)S(1)}, f32[96,256]{1,0:T(8,128)S(1)}, u32[]{:S(2)}, u32[]{:S(2)}) collective-permute-start(f32[96,256]{1,0:T(8,128)S(1)} %fusion.1), channel_id=1, source_target_pairs={{0,1},{1,2},{2,3},{3,4},{4,5},{5,6},{6,7},{7,8},{8,9},{9,10},{10,1... | collective-permute-start | bytes 294920
  601.3 6.2 %collective-permute-start.3 = (f32[84,256]{1,0:T(8,128)S(1)}, f32[84,256]{1,0:T(8,128)S(1)}, u32[]{:S(2)}, u32[]{:S(2)}) collective-permute-start(f32[84,256]{1,0:T(8,128)S(1)} %slice.327), channel_id=1, source_target_pairs={{0,2},{1,3},{2,4},{3,5},{4,6},{5,7},{6,8},{7,9},{8,10},{9,11},{10,... | collective-permute-start | bytes 258056
Sparse Core Ops, SparseCore 0:
  11.9 98.7 all-reduce.7
  116.5 53.6 all-gather.2
  187.8 25.0 all-gather.4
where the time goes:
time: 623 us; the launch traced here: 616 us
  other arithmetic  262 us (42%)
  blocking collectives  122 us (20%)
  waiting for transfers between devices  105 us (17%)
  local copies, waits for them, and re-layouts  44.9 us (7%)
  matrix products  40.4 us (6%)
  between operations  20.6 us (3%)
  starting transfers between devices  19.8 us (3%)
    another operation x30, other arithmetic, per_device(): factor_top = jnp.linalg.cholesky(top_full)  172 us
    psum x1, waiting for transfers between devices, per_device(): top_sum, win_sum = lax.psum((panel_top[0], panel_win[0]), 'layer')  99.5 us
    unnamed x2, blocking collectives  95.7 us
    another operation x3, other arithmetic, solve_right(): return jax.scipy.linalg.solve_triangular(factor, values.T, lower=True).T  85.5 us
    another operation x14, matrix products, per_device(): factor_top = jnp.linalg.cholesky(top_full)  23.1 us
    another operation x24, local copies, waits for them, and re-layouts  23 us
    all_gather x1, blocking collectives, per_device(): rest_full = lax.all_gather(rest_part, 'col', axis=1, tiled=True)  21 us
    another operation x30, matrix products, solve_right(): return jax.scipy.linalg.solve_triangular(factor, values.T, lower=True).T  15.2 us
  transfers between devices with their start and end apart: 8, of which 3 were waited for; matrix products, arithmetic and copies ran while one was open for 59% of the time, Pallas kernels for 0%

commit v1 on v0

v1 whole, which is shorter than its diff:
```python
import jax, jax.numpy as jnp
from jax import lax
from jax.sharding import PartitionSpec as P
from jax.experimental import pallas as pl
from jax.experimental.pallas import tpu as pltpu
HALF = 512
f32=jnp.float32; bf16=jnp.bfloat16
NN=(((1,),(0,)),((),())); NT=(((1,),(1,)),((),())); TN=(((0,),(0,)),((),()))

def split(a):
    hi=a.astype(bf16); lo=(a-hi.astype(f32)).astype(bf16)
    return hi,lo

def mm(a,b,dims=NN):
    ah,al=split(a); bh,bl=split(b)
    d=lambda x,y: lax.dot_general(x,y,dims,preferred_element_type=f32)
    return d(ah,bh)+(d(ah,bl)+d(al,bh))

def chol128(groups):
    lane=lax.broadcasted_iota(jnp.int32,(8,128),1)
    sub=lax.broadcasted_iota(jnp.int32,(8,128),0)
    bc=lambda x: jnp.broadcast_to(x,(8,128))
    S=list(groups); U=[]; W=[]
    for t in range(16):
        o=8*t
        St=S[t]
        inblk=(lane>=o)&(lane<o+8)
        P=[bc(St[i:i+1,:]) for i in range(8)]
        a=[[bc(P[i][:,o+j:o+j+1]) for j in range(i+1)] for i in range(8)]
        C={g:[bc(S[g][:,o+m:o+m+1]) for m in range(8)] for g in range(t+1,16)}
        P=[jnp.where(inblk,jnp.where(lane==o+i,1.0,0.0),P[i]) for i in range(8)]
        r=[None]*8; R=[None]*8
        for m in range(8):
            r[m]=lax.rsqrt(a[m][m])
            for i in range(m+1,8): a[i][m]=a[i][m]*r[m]
            a[m][m]=a[m][m]*r[m]
            for i in range(m+1,8):
                for j in range(m+1,i+1):
                    a[i][j]=a[i][j]-a[i][m]*a[j][m]
            R[m]=P[m]*r[m]
            for i in range(m+1,8): P[i]=P[i]-a[i][m]*R[m]
        V=[None]*8
        for m in range(7,-1,-1):
            acc=R[m]
            for j in range(7,m,-1): acc=acc-a[j][m]*V[j]
            V[m]=acc*r[m]
        for g in range(t+1,16):
            x=jnp.where(inblk,0.0,S[g])
            for m in range(8): x=x-C[g][m]*V[m]
            S[g]=x
        ut=jnp.zeros((8,128),f32); wt=ut
        for m in range(8):
            row=R[m]
            wt=jnp.where(sub==m,row,wt)
            for i in range(m,8): row=jnp.where(lane==o+i,a[i][m],row)
            if m: row=jnp.where((lane>=o)&(lane<o+m),0.0,row)
            ut=jnp.where(sub==m,row,ut)
        U.append(jnp.where(lane>=o,ut,0.0)); W.append(jnp.where(lane<o+8,wt,0.0))
    return U,W


def factor_loop(a_ref, u_ref, w_ref):
    n = a_ref.shape[0]

    def body(k, _):
        o = pl.multiple_of(k * 128, 128)
        rows = [pl.ds(pl.multiple_of(o + 8 * g, 8), 8) for g in range(16)]
        upper, inverse = chol128([a_ref[rows[g], pl.ds(o, 128)] for g in range(16)])
        for g in range(16):
            w_ref[k, 8 * g : 8 * g + 8, :] = inverse[g]
        panel = mm(w_ref[k], a_ref[pl.ds(o, 128), :])
        col = lax.broadcasted_iota(jnp.int32, (128, n), 1)
        panel = jnp.where(col >= o + 128, panel, 0.0)
        u_ref[pl.ds(o, 128), :] = panel
        for g in range(16):
            u_ref[rows[g], pl.ds(o, 128)] = upper[g]
        a_ref[...] = a_ref[...] - mm(panel, panel, TN)
        return 0

    lax.fori_loop(0, n // 128, body, 0)


def solve_half(x_ref, lanes, u_ref, w_ref):
    for k in range(HALF // 128):
        o = lanes + 128 * k
        value = x_ref[:, o : o + 128]
        if k:
            value = value - mm(x_ref[:, lanes:o], u_ref[0 : 128 * k, 128 * k : 128 * k + 128])
        x_ref[:, o : o + 128] = mm(value, w_ref[k], NT)


def place_strips(dst_ref, own_ref, other_ref, n_cols):
    q = lax.axis_index("row")
    for which, src in ((q, own_ref), (1 - q, other_ref)):
        for strip in range(src.shape[0]):
            start = pl.multiple_of(32 * strip + 16 * which, 16)
            for c in range(n_cols):
                dst_ref[pl.ds(start, 16), 128 * c : 128 * c + 128] = src[strip, c]


def first_kernel(own_ref, other_ref, u_ref, w_ref, a_ref):
    place_strips(a_ref, own_ref, other_ref, 4)
    factor_loop(a_ref, u_ref, w_ref)


def second_kernel(own_ref, other_ref, u1_ref, w1_ref, l21_ref, u_ref, w_ref, x_ref, a_ref):
    place_strips(x_ref, own_ref, other_ref, 8)
    solve_half(x_ref, 0, u1_ref, w1_ref)
    l21 = x_ref[:, :HALF]
    l21_ref[...] = l21
    a_ref[...] = x_ref[:, HALF:] - mm(l21, l21, NT)
    factor_loop(a_ref, u_ref, w_ref)


def third_kernel(
    own_ref, other_ref, rest_ref, trail_ref, u1_ref, w1_ref, l21_ref, u2_ref, w2_ref,
    top_out, win_out, rest_out, schur_out, x_ref,
):
    q = lax.axis_index("row")
    c = lax.axis_index("col")
    n_win = own_ref.shape[0]
    n_rest = rest_ref.shape[1]
    x_ref[n_win:, :] = jnp.zeros((x_ref.shape[0] - n_win, x_ref.shape[1]), f32)
    x_ref[0:n_win, pl.ds(pl.multiple_of(HALF * q, HALF), HALF)] = own_ref[...]
    x_ref[0:n_win, pl.ds(pl.multiple_of(HALF * (1 - q), HALF), HALF)] = other_ref[...]
    for j in range(rest_ref.shape[0]):
        x_ref[n_win : n_win + n_rest, 128 * j : 128 * j + 128] = rest_ref[j]
    solve_half(x_ref, 0, u1_ref, w1_ref)
    x_ref[:, HALF:] = x_ref[:, HALF:] - mm(x_ref[:, :HALF], l21_ref[...], NT)
    solve_half(x_ref, HALF, u2_ref, w2_ref)
    win_out[...] = x_ref[0:n_win, pl.ds(pl.multiple_of(HALF * q, HALF), HALF)]
    rest_out[...] = x_ref[n_win : n_win + n_rest, pl.ds(pl.multiple_of(128 * c, 128), 128)]
    product = mm(x_ref[n_win:, :], x_ref[0:n_win, :], NT)
    schur_out[...] = trail_ref[...] - product[0:n_rest]

    left = c < 4

    @pl.when(left & (q == 0))
    def _():
        top_out[...] = u1_ref[pl.ds(pl.multiple_of(128 * c, 128), 128), :].T

    @pl.when(jnp.logical_not(left) & (q == 0))
    def _():
        top_out[...] = jnp.zeros(top_out.shape, f32)

    @pl.when(left & (q == 1))
    def _():
        top_out[...] = l21_ref[:, pl.ds(pl.multiple_of(128 * c, 128), 128)]

    @pl.when(jnp.logical_not(left) & (q == 1))
    def _():
        top_out[...] = u2_ref[pl.ds(pl.multiple_of(128 * (c - 4), 128), 128), :].T


def call(kernel, outs, scratch, *args):
    shape = lambda s: jax.ShapeDtypeStruct(s, f32)
    return pl.pallas_call(
        kernel,
        out_shape=tuple(shape(s) for s in outs),
        scratch_shapes=[pltpu.VMEM(s, f32) for s in scratch],
        compiler_params=pltpu.CompilerParams(vmem_limit_bytes=48 << 20),
    )(*args)


def swap_rows(value):
    return lax.ppermute(value, "row", [(0, 1), (1, 0)])


def spread(value, axis):
    n = lax.axis_size(axis)
    return lax.all_to_all(jnp.broadcast_to(value, (n,) + value.shape), axis, 0, 0)


def reduce_pieces(value, axis):
    return lax.all_to_all(value, axis, 0, 0)


def per_device(panel_top, panel_win, panel_rest, trail_rest):
    top_parts = lax.all_to_all(panel_top[0].reshape(32, 16, 128), ("layer", "row"), 0, 0)
    top_piece = jnp.sum(top_parts.reshape(16, 2, 16, 128), axis=0)
    strips = spread(top_piece, "col")
    first_own = spread(strips[:4, 0], "layer")
    first_other = swap_rows(first_own)
    first_own, first_other, strips, panel_win, panel_rest, trail_rest = lax.optimization_barrier(
        (first_own, first_other, strips, panel_win, panel_rest, trail_rest)
    )
    second_own = spread(strips[:, 1], "layer")
    second_other = swap_rows(second_own)
    win_parts = lax.all_to_all(panel_win[0].reshape(16, 16, HALF), "layer", 0, 0)
    lower = jnp.concatenate(
        [panel_rest[0].reshape(16, 84, 128), trail_rest[0].reshape(16, 84, 256)], axis=2
    )
    lower_parts = lax.all_to_all(lower, "layer", 0, 0)
    u1, w1 = call(first_kernel, [(HALF, HALF), (4, 128, 128)], [(HALF, HALF)], first_own, first_other)
    win_own = spread(jnp.sum(win_parts, axis=0), "layer").reshape(256, HALF)
    win_other = swap_rows(win_own)
    lower_sum = jnp.sum(lower_parts, axis=0)
    rest_strips = spread(lower_sum[:, :128], "col")
    l21, u2, w2 = call(
        second_kernel,
        [(HALF, HALF), (HALF, HALF), (4, 128, 128)],
        [(HALF, 2 * HALF), (HALF, HALF)],
        second_own, second_other, u1, w1,
    )
    return call(
        third_kernel,
        [(HALF, 128), (256, HALF), (84, 128), (84, 256)],
        [(344, 2 * HALF)],
        win_own, win_other, rest_strips, lower_sum[:, 128:], u1, w1, l21, u2, w2,
    )


def solution(mesh):
    return jax.shard_map(
        per_device,
        mesh=mesh,
        in_specs=(
            P("layer", "row", "col"),
            P("layer", "col", "row"),
            P("layer", "row", "col"),
            P("layer", "row", "col"),
        ),
        out_specs=(
            P("row", "col"),
            P("col", "row"),
            P(("row", "layer"), "col"),
            P(("row", "layer"), "col"),
        ),
        check_vma=False,
    )
```

time: 623 us -> 215 us (0.35)
  other arithmetic: 262 us -> 4.39 us
  blocking collectives: 122 us -> 47.3 us
  Pallas kernels: 0 us -> 57.2 us
  waiting for transfers between devices: 105 us -> 54.4 us
  matrix products: 40.4 us -> 0 us
  local copies, waits for them, and re-layouts: 44.9 us -> 19.4 us
  between operations: 20.6 us -> 0.79 us
  starting transfers between devices: 19.8 us -> 29.8 us
    another operation x33 -> x0, other arithmetic: 258 us -> none  [the longest x30 172 us: per_device(): factor_top = jnp.linalg.cholesky(top_full)]
    psum x1 -> x0, waiting for transfers between devices: 99.5 us -> none  [per_device(): top_sum, win_sum = lax.psum((panel_top[0], panel_win[0]), 'layer')]
    unnamed x2 -> x0, blocking collectives: 95.7 us -> none
    pallas_call x0 -> x3, Pallas kernels: none -> 57.2 us  [call(): pl.pallas_call(kernel, out_shape=tuple((shape(s) for s in outs)), scratch...]
    all_to_all x1 -> x5, waiting for transfers between devices: 4.28 us -> 52.9 us  [the longest x1 26 us: per_device(): lower_parts = lax.all_to_all(lower, 'layer', 0, 0)]
    all_to_all x0 -> x3, blocking collectives: none -> 47.3 us  [the longest x2 29.8 us: spread(): lax.all_to_all(jnp.broadcast_to(value, (n,) + value.shape), axis, 0, 0)]
    another operation x44 -> x0, matrix products: 38.3 us -> none  [the longest x14 23.1 us: per_device(): factor_top = jnp.linalg.cholesky(top_full)]
    all_gather x2 -> x0, blocking collectives: 26.7 us -> none  [the longest x1 21 us: per_device(): rest_full = lax.all_gather(rest_part, 'col', axis=1, tiled=True)]
  transfers between devices with their start and end apart: 8 -> 8, of which waited for: 3 -> 5; matrix products, arithmetic and copies ran while one was open for 59% -> 5% of each run, Pallas kernels for 0% -> 24%
where the time goes in v1:
time: 215 us; the launch traced here: 213 us
  Pallas kernels  57.2 us (27%)
  waiting for transfers between devices  54.4 us (25%)
  blocking collectives  47.3 us (22%)
  starting transfers between devices  29.8 us (14%)
  local copies, waits for them, and re-layouts  19.4 us (9%)
  other arithmetic  4.39 us (2%)
    pallas_call x3, Pallas kernels, call(): pl.pallas_call(kernel, out_shape=tuple((shape(s) for s in outs)), scratch...  57.2 us
    all_to_all x2, blocking collectives, spread(): lax.all_to_all(jnp.broadcast_to(value, (n,) + value.shape), axis, 0, 0)  29.8 us
    all_to_all x1, waiting for transfers between devices, per_device(): lower_parts = lax.all_to_all(lower, 'layer', 0, 0)  26 us
    all_to_all x1, blocking collectives, per_device(): lax.all_to_all(panel_top[0].reshape(32, 16, 128), ('layer', 'row'), 0, 0)  17.5 us
    all_to_all x3, waiting for transfers between devices, spread(): lax.all_to_all(jnp.broadcast_to(value, (n,) + value.shape), axis, 0, 0)  15.9 us
    all_to_all x3, starting transfers between devices, spread(): lax.all_to_all(jnp.broadcast_to(value, (n,) + value.shape), axis, 0, 0)  14.9 us
    unnamed x28, local copies, waits for them, and re-layouts  11.6 us
    all_to_all x1, waiting for transfers between devices, per_device(): lax.all_to_all(panel_win[0].reshape(16, 16, HALF), 'layer', 0, 0)  10.9 us
  transfers between devices with their start and end apart: 8, of which 5 were waited for; matrix products, arithmetic and copies ran while one was open for 5% of the time, Pallas kernels for 24%

profile of v1, /device:TPU:1, one launch (start us, length us, event | category | flops | bytes accessed | tf_op | source)
XLA Modules:
  0.0 213.4 jit_solution(10997268820921126806)
XLA Ops:
  0.6 17.5 %all_to_all.40 = f32[32,16,128]{2,1,0:T(8,128)S(1)} all-to-all(f32[32,16,128]{2,1,0:T(8,128)} %bitcast.11), channel_id=1, replica_groups=mesh['row'=2,'col'=8,'layer'=16] {'layer','row'}, dimensions={0} | all-to-all | bytes 524288 | tf_op jit(solution)/shard_map/all_to_all | solution.py:179
  18.2 16.2 %all_to_all.41 = f32[8,2,16,128]{3,2,1,0:T(8,128)S(1)} all-to-all(f32[8,2,16,128]{3,2,1,0:T(8,128)S(1)} %broadcast_in_dim.15), channel_id=1, replica_groups=mesh['row'=2,'col'=8,'layer'=16] {'col'}, dimensions={0} | all-to-all | bytes 262144 | tf_op jit(solution)/shard_map/all_to_all | solution.py:171
  34.4 13.6 %all_to_all.42.own_ref = f32[16,4,16,128]{3,2,1,0:T(8,128)S(1)} all-to-all(f32[16,4,16,128]{3,2,1,0:T(8,128)S(1)} %broadcast_in_dim.16), channel_id=1, replica_groups=mesh['row'=2,'col'=8,'layer'=16] {'layer'}, dimensions={0} | all-to-all | bytes 1048576 | tf_op jit(solution)/shard_map/all_to_all | solution.py:171
  48.0 2.4 %collective-permute-start = (f32[16,4,16,128]{3,2,1,0:T(8,128)S(1)}, f32[16,4,16,128]{3,2,1,0:T(8,128)S(1)}, u32[]{:S(2)}, u32[]{:S(2)}) collective-permute-start(f32[16,4,16,128]{3,2,1,0:T(8,128)S(1)} %all_to_all.42.own_ref), channel_id=1, source_target_pairs={{0,128},{128,0},{1,129},{129,1},{2,130},{130,2},{3,131},{131,3},{4... | collective-permute-start | bytes 1572872 | tf_op jit(solution)/shard_map/ppermute | solution.py:166
  50.4 1.5 collective-permute-done.other_ref
  51.9 0.0 copy-start.8
  51.9 0.8 copy-done.8
  52.8 3.6 %all-to-all-start.3 = ((f32[16,16,512]{2,1,0:T(8,128)}), f32[16,16,512]{2,1,0:T(8,128)S(1)}, u32[]{:S(2)}, u32[]{:S(2)}) async-start(f32[16,16,512]{2,1,0:T(8,128)} %bitcast.3), calls=%async_computation.3 | async-start | bytes 1048576 | tf_op jit(solution)/shard_map/all_to_all | solution.py:189
  56.4 10.9 %all-to-all-done.3 = f32[16,16,512]{2,1,0:T(8,128)S(1)} async-done(((f32[16,16,512]{2,1,0:T(8,128)}), f32[16,16,512]{2,1,0:T(8,128)S(1)}, u32[]{:S(2)}, u32[]{:S(2)}) %all-to-all-start.3) | async-done | bytes 524320 | tf_op jit(solution)/shard_map/all_to_all | solution.py:189
  67.3 1.1 broadcast_in_dim.19
  68.4 3.7 %all-to-all-start.7 = ((f32[16,8,16,128]{3,2,1,0:T(8,128)}), f32[16,8,16,128]{3,2,1,0:T(8,128)S(1)}, u32[]{:S(2)}, u32[]{:S(2)}) async-start(f32[16,8,16,128]{3,2,1,0:T(8,128)} %broadcast_in_dim.19), calls=%async_computation.7 | async-start | bytes 2097152 | tf_op jit(solution)/shard_map/all_to_all | solution.py:171
  72.0 1.4 reshape_squeeze.15
  73.5 2.0 reshape_squeeze.14
  75.5 2.6 %pad_maximum_fusion = f32[16,84,384]{2,1,0:T(8,128)} fusion(f32[16,84,256]{2,1,0:T(8,128)S(1)} %reshape_squeeze.15, f32[16,84,128]{2,1,0:T(8,128)} %reshape_squeeze.14), kind=kLoop, calls=%fused_computation | loop fusion | flops 516096 | bytes 4128768 | tf_op jit(solution)/shard_map/concatenate | solution.py:190
  78.1 9.4 %all-to-all-done.7.own_ref = f32[16,8,16,128]{3,2,1,0:T(8,128)S(1)} async-done(((f32[16,8,16,128]{3,2,1,0:T(8,128)}), f32[16,8,16,128]{3,2,1,0:T(8,128)S(1)}, u32[]{:S(2)}, u32[]{:S(2)}) %all-to-all-start.7) | async-done | bytes 1048608 | tf_op jit(solution)/shard_map/all_to_all | solution.py:171
  87.5 4.5 %all-to-all-start.5 = ((f32[16,84,384]{2,1,0:T(8,128)}), f32[16,84,384]{2,1,0:T(8,128)}, u32[]{:S(2)}, u32[]{:S(2)}) async-start(f32[16,84,384]{2,1,0:T(8,128)} %pad_maximum_fusion), calls=%async_computation.5 | async-start | bytes 4325376 | tf_op jit(solution)/shard_map/all_to_all | solution.py:193
  92.0 26.0 %all-to-all-done.5 = f32[16,84,384]{2,1,0:T(8,128)} async-done(((f32[16,84,384]{2,1,0:T(8,128)}), f32[16,84,384]{2,1,0:T(8,128)}, u32[]{:S(2)}, u32[]{:S(2)}) %all-to-all-start.5) | async-done | bytes 2064416 | tf_op jit(solution)/shard_map/all_to_all | solution.py:193
  118.0 0.9 broadcast_in_dim.17
  118.9 7.9 %all-to-all-start.4 = ((f32[16,16,512]{2,1,0:T(8,128)}), f32[16,16,512]{2,1,0:T(8,128)S(1)}, u32[]{:S(2)}, u32[]{:S(2)}) async-start(f32[16,16,512]{2,1,0:T(8,128)} %broadcast_in_dim.17), calls=%async_computation.4 | async-start | bytes 1048576 | tf_op jit(solution)/shard_map/all_to_all | solution.py:171
  126.7 1.8 collective-permute-start.2
  128.5 1.7 reduce_sum.29
  130.2 0.0 copy-start.13
  130.3 6.6 %all-to-all-done.4 = f32[16,16,512]{2,1,0:T(8,128)S(1)} async-done(((f32[16,16,512]{2,1,0:T(8,128)}), f32[16,16,512]{2,1,0:T(8,128)S(1)}, u32[]{:S(2)}, u32[]{:S(2)}) %all-to-all-start.4) | async-done | bytes 524320 | tf_op jit(solution)/shard_map/all_to_all | solution.py:171
  136.8 0.8 broadcast_in_dim.18
  137.6 0.0 copy-done.13
  137.6 3.4 %all-to-all-start.6 = ((f32[8,84,128]{2,1,0:T(8,128)}), f32[8,84,128]{2,1,0:T(8,128)S(1)}, u32[]{:S(2)}, u32[]{:S(2)}) async-start(f32[8,84,128]{2,1,0:T(8,128)} %broadcast_in_dim.18), calls=%async_computation.6 | async-start | bytes 720896 | tf_op jit(solution)/shard_map/all_to_all | solution.py:171
  141.0 2.7 %collective-permute-start.1 = (f32[256,512]{1,0:T(8,128)S(1)}, f32[256,512]{1,0:T(8,128)S(1)}, u32[]{:S(2)}, u32[]{:S(2)}) collective-permute-start(f32[256,512]{1,0:T(8,128)S(1)} %bitcast.8), channel_id=1, source_target_pairs={{0,128},{128,0},{1,129},{129,1},{2,130},{130,2},{3,131},{131,3},{4... | collective-permute-start | bytes 1572872 | tf_op jit(solution)/shard_map/ppermute | solution.py:166
  143.7 1.0 copy-done.9
  144.8 23.3 %shard_map.75 = (f32[512,512]{1,0:T(8,128)S(1)}, f32[4,128,128]{2,1,0:T(8,128)S(1)}) custom-call(f32[16,4,16,128]{3,2,1,0:T(8,128)S(1)} %all_to_all.42.own_ref, f32[16,4,16,128]{3,2,1,0:T(8,128)S(1)} %copy-done.9), custom_call_target="tpu_custom_call" | custom-call | tf_op jit(solution)/shard_map/pallas_call | solution.py:157
  168.1 0.0 copy-start.4
  168.1 1.6 slice.18.trail_ref
  169.7 0.0 collective-permute-done.2.other_ref
  169.7 27.8 %shard_map.76 = (f32[512,512]{1,0:T(8,128)S(1)}, f32[512,512]{1,0:T(8,128)S(1)}, f32[4,128,128]{2,1,0:T(8,128)S(1)}) custom-call(f32[16,8,16,128]{3,2,1,0:T(8,128)S(1)} %all-to-all-done.7.own_ref, f32[16,8,16,128]{3,2,1,0:T(8,128)} %collective-permute-done.2.other_ref, f32[512,512]{1,0:T(8,128)S(1)} %get-tuple-element.20.u1_ref, ...), custom_call_target="tpu_custom_call" | custom-call | tf_op jit(solution)/shard_map/pallas_call | solution.py:157
  197.6 0.0 copy-done.4
  197.6 0.0 copy-start
  197.6 1.0 copy-done
  198.6 1.0 copy-done.2
  199.6 0.7 copy-done.11
  200.3 0.0 collective-permute-done.1.other_ref
  200.3 0.8 copy-done.6
  201.0 0.0 all-to-all-done.6.rest_ref
  201.1 1.2 copy-done.1
  202.3 1.2 copy-done.3
  203.5 0.9 copy-done.5
  204.5 1.0 copy-done.7
  205.5 0.9 copy-done.10
  206.4 0.9 copy-done.12
  207.3 6.0 %shard_map.77 = (f32[512,128]{1,0:T(8,128)}, f32[256,512]{1,0:T(8,128)}, f32[84,128]{1,0:T(8,128)}, f32[84,256]{1,0:T(8,128)}) custom-call(f32[256,512]{1,0:T(8,128)S(1)} %bitcast.9, f32[256,512]{1,0:T(8,128)S(1)} %copy-done.7, f32[8,84,128]{2,1,0:T(8,128)S(1)} %all-to-all-done.6.rest_ref, f32[84,256]{1,0:T(8,128)S(1)} %copy-done.10, ...), custom_call_target="tpu_custom_call" | custom-call | tf_op jit(solution)/shard_map/pallas_call | solution.py:157
  (17 shorter events, 0.1 us)
Async XLA Ops:
  48.0 3.9 %collective-permute-start = (f32[16,4,16,128]{3,2,1,0:T(8,128)S(1)}, f32[16,4,16,128]{3,2,1,0:T(8,128)S(1)}, u32[]{:S(2)}, u32[]{:S(2)}) collective-permute-start(f32[16,4,16,128]{3,2,1,0:T(8,128)S(1)} %all_to_all.42.own_ref), channel_id=1, source_target_pairs={{0,128},{128,0},{1,129},{129,1},{2,130},{130,2},{3,131},{131,3},{4... | collective-permute-start | bytes 1572872 | tf_op jit(solution)/shard_map/ppermute | solution.py:166
  51.9 0.8 copy-start.8
  52.8 14.5 %all-to-all-start.3 = ((f32[16,16,512]{2,1,0:T(8,128)}), f32[16,16,512]{2,1,0:T(8,128)S(1)}, u32[]{:S(2)}, u32[]{:S(2)}) async-start(f32[16,16,512]{2,1,0:T(8,128)} %bitcast.3), calls=%async_computation.3 | async-start | bytes 1048576 | tf_op jit(solution)/shard_map/all_to_all | solution.py:189
  68.4 19.1 %all-to-all-start.7 = ((f32[16,8,16,128]{3,2,1,0:T(8,128)}), f32[16,8,16,128]{3,2,1,0:T(8,128)S(1)}, u32[]{:S(2)}, u32[]{:S(2)}) async-start(f32[16,8,16,128]{3,2,1,0:T(8,128)} %broadcast_in_dim.19), calls=%async_computation.7 | async-start | bytes 2097152 | tf_op jit(solution)/shard_map/all_to_all | solution.py:171
  87.5 30.6 %all-to-all-start.5 = ((f32[16,84,384]{2,1,0:T(8,128)}), f32[16,84,384]{2,1,0:T(8,128)}, u32[]{:S(2)}, u32[]{:S(2)}) async-start(f32[16,84,384]{2,1,0:T(8,128)} %pad_maximum_fusion), calls=%async_computation.5 | async-start | bytes 4325376 | tf_op jit(solution)/shard_map/all_to_all | solution.py:193
  118.9 17.9 %all-to-all-start.4 = ((f32[16,16,512]{2,1,0:T(8,128)}), f32[16,16,512]{2,1,0:T(8,128)S(1)}, u32[]{:S(2)}, u32[]{:S(2)}) async-start(f32[16,16,512]{2,1,0:T(8,128)} %broadcast_in_dim.17), calls=%async_computation.4 | async-start | bytes 1048576 | tf_op jit(solution)/shard_map/all_to_all | solution.py:171
  126.7 43.0 %collective-permute-start.2 = (f32[16,8,16,128]{3,2,1,0:T(8,128)S(1)}, f32[16,8,16,128]{3,2,1,0:T(8,128)}, u32[]{:S(2)}, u32[]{:S(2)}) collective-permute-start(f32[16,8,16,128]{3,2,1,0:T(8,128)S(1)} %all-to-all-done.7.own_ref), channel_id=1, source_target_pairs={{0,128},{128,0},{1,129},{129,1},{2,130},{130,2},{3,131},{131,3},{4... | collective-permute-start | bytes 3145736 | tf_op jit(solution)/shard_map/ppermute | solution.py:166
  130.2 7.4 %copy-start.13 = (f32[84,384]{1,0:T(8,128)}, f32[84,384]{1,0:T(8,128)S(1)}, u32[]{:S(2)}) copy-start(f32[84,384]{1,0:T(8,128)S(1)} %reduce_sum.29) | copy-start | bytes 387076
  137.6 63.5 %all-to-all-start.6 = ((f32[8,84,128]{2,1,0:T(8,128)}), f32[8,84,128]{2,1,0:T(8,128)S(1)}, u32[]{:S(2)}, u32[]{:S(2)}) async-start(f32[8,84,128]{2,1,0:T(8,128)} %broadcast_in_dim.18), calls=%async_computation.6 | async-start | bytes 720896 | tf_op jit(solution)/shard_map/all_to_all | solution.py:171
  141.0 59.2 %collective-permute-start.1 = (f32[256,512]{1,0:T(8,128)S(1)}, f32[256,512]{1,0:T(8,128)S(1)}, u32[]{:S(2)}, u32[]{:S(2)}) collective-permute-start(f32[256,512]{1,0:T(8,128)S(1)} %bitcast.8), channel_id=1, source_target_pairs={{0,128},{128,0},{1,129},{129,1},{2,130},{130,2},{3,131},{131,3},{4... | collective-permute-start | bytes 1572872 | tf_op jit(solution)/shard_map/ppermute | solution.py:166
  143.7 1.0 copy-start.9
  168.1 29.5 %copy-start.4 = (f32[4,128,128]{2,1,0:T(8,128)}, f32[4,128,128]{2,1,0:T(8,128)S(1)}, u32[]{:S(2)}) copy-start(f32[4,128,128]{2,1,0:T(8,128)S(1)} %get-tuple-element.21.w1_ref) | copy-start | bytes 786436
  197.6 1.0 copy-start
  198.6 1.0 copy-start.2
  199.6 0.7 copy-start.11
  200.3 0.8 copy-start.6
  201.1 1.2 copy-start.1
  202.3 1.2 copy-start.3
  203.5 0.9 copy-start.5
  204.5 1.0 copy-start.7
  205.5 0.9 copy-start.10
  206.4 0.9 copy-start.12

commit v2 on v1

v2 whole, which is shorter than its diff:
```python
import jax, jax.numpy as jnp
from jax import lax
from jax.sharding import PartitionSpec as P
from jax.experimental import pallas as pl
from jax.experimental.pallas import tpu as pltpu
HALF = 512
f32=jnp.float32; bf16=jnp.bfloat16
NN=(((1,),(0,)),((),())); NT=(((1,),(1,)),((),())); TN=(((0,),(0,)),((),()))

def split(a):
    hi=a.astype(bf16); lo=(a-hi.astype(f32)).astype(bf16)
    return hi,lo

def mm(a,b,dims=NN):
    ah,al=split(a); bh,bl=split(b)
    d=lambda x,y: lax.dot_general(x,y,dims,preferred_element_type=f32)
    return d(ah,bh)+(d(ah,bl)+d(al,bh))

def chol128(groups):
    lane=lax.broadcasted_iota(jnp.int32,(8,128),1)
    sub=lax.broadcasted_iota(jnp.int32,(8,128),0)
    bc=lambda x: jnp.broadcast_to(x,(8,128))
    S=list(groups); U=[]; W=[]
    for t in range(16):
        o=8*t
        St=S[t]
        inblk=(lane>=o)&(lane<o+8)
        P=[bc(St[i:i+1,:]) for i in range(8)]
        a=[[bc(P[i][:,o+j:o+j+1]) for j in range(i+1)] for i in range(8)]
        C={g:[bc(S[g][:,o+m:o+m+1]) for m in range(8)] for g in range(t+1,16)}
        P=[jnp.where(inblk,jnp.where(lane==o+i,1.0,0.0),P[i]) for i in range(8)]
        r=[None]*8; R=[None]*8
        for m in range(8):
            r[m]=lax.rsqrt(a[m][m])
            for i in range(m+1,8): a[i][m]=a[i][m]*r[m]
            a[m][m]=a[m][m]*r[m]
            for i in range(m+1,8):
                for j in range(m+1,i+1):
                    a[i][j]=a[i][j]-a[i][m]*a[j][m]
            R[m]=P[m]*r[m]
            for i in range(m+1,8): P[i]=P[i]-a[i][m]*R[m]
        V=[None]*8
        for m in range(7,-1,-1):
            acc=R[m]
            for j in range(7,m,-1): acc=acc-a[j][m]*V[j]
            V[m]=acc*r[m]
        for g in range(t+1,16):
            x=jnp.where(inblk,0.0,S[g])
            for m in range(8): x=x-C[g][m]*V[m]
            S[g]=x
        ut=jnp.zeros((8,128),f32); wt=ut
        for m in range(8):
            row=R[m]
            wt=jnp.where(sub==m,row,wt)
            for i in range(m,8): row=jnp.where(lane==o+i,a[i][m],row)
            if m: row=jnp.where((lane>=o)&(lane<o+m),0.0,row)
            ut=jnp.where(sub==m,row,ut)
        U.append(jnp.where(lane>=o,ut,0.0)); W.append(jnp.where(lane<o+8,wt,0.0))
    return U,W


def factor_loop(a_ref, u_ref, w_ref):
    n = a_ref.shape[0]

    def body(k, _):
        o = pl.multiple_of(k * 128, 128)
        rows = [pl.ds(pl.multiple_of(o + 8 * g, 8), 8) for g in range(16)]
        upper, inverse = chol128([a_ref[rows[g], pl.ds(o, 128)] for g in range(16)])
        for g in range(16):
            w_ref[k, 8 * g : 8 * g + 8, :] = inverse[g]
        panel = mm(w_ref[k], a_ref[pl.ds(o, 128), :])
        col = lax.broadcasted_iota(jnp.int32, (128, n), 1)
        panel = jnp.where(col >= o + 128, panel, 0.0)
        u_ref[pl.ds(o, 128), :] = panel
        for g in range(16):
            u_ref[rows[g], pl.ds(o, 128)] = upper[g]
        a_ref[...] = a_ref[...] - mm(panel, panel, TN)
        return 0

    lax.fori_loop(0, n // 128, body, 0)


def solve_half(x_ref, first, lanes, u_ref, w_ref):
    for k in range(HALF // 128):
        o = lanes + 128 * k
        value = x_ref[first:, o : o + 128]
        if k:
            value = value - mm(
                x_ref[first:, lanes:o], u_ref[0 : 128 * k, 128 * k : 128 * k + 128]
            )
        x_ref[first:, o : o + 128] = mm(value, w_ref[k], NT)


def aligned(index, step):
    return pl.ds(pl.multiple_of(index * step, step), step)


def pack_kernel(top_ref, win_ref, rest_ref, out_ref):
    for piece in range(out_ref.shape[0]):
        for j in range(4):
            out_ref[piece, 16 * j : 16 * j + 16] = win_ref[
                16 * piece : 16 * piece + 16, 128 * j : 128 * j + 128
            ]
        out_ref[piece, 64:96] = top_ref[32 * piece : 32 * piece + 32]
        out_ref[piece, 96:180] = rest_ref[84 * piece : 84 * piece + 84]


def first_kernel(own_ref, other_ref, u_ref, w_ref, a_ref):
    q = lax.axis_index("row")
    for which, src in ((q, own_ref), (1 - q, other_ref)):
        for strip in range(src.shape[0]):
            for c in range(4):
                a_ref[aligned(2 * strip + which, 16), 128 * c : 128 * c + 128] = src[
                    strip, 16 * c : 16 * c + 16
                ]
    factor_loop(a_ref, u_ref, w_ref)


def second_kernel(
    own_ref, other_ref, own2_ref, other2_ref, strips_ref, u1_ref, w1_ref,
    top_out, win_out, rest_out, product_out, u2_ref, w2_ref, x_ref, a_ref,
):
    q = lax.axis_index("row")
    c = lax.axis_index("col")
    n_win = win_out.shape[0]
    n_rest = rest_out.shape[0]
    win = HALF
    rest = HALF + n_win
    x_ref[rest:, :] = jnp.zeros((x_ref.shape[0] - rest, x_ref.shape[1]), f32)
    for which, top_src, win_src in ((q, own2_ref, own_ref), (1 - q, other2_ref, other_ref)):
        for strip in range(top_src.shape[0]):
            for j in range(8):
                x_ref[aligned(2 * strip + which, 16), 128 * j : 128 * j + 128] = top_src[strip, j]
            for j in range(4):
                x_ref[win + 16 * strip : win + 16 * strip + 16, aligned(4 * which + j, 128)] = (
                    win_src[strip, 64 + 16 * j : 80 + 16 * j]
                )
    for j in range(8):
        x_ref[rest : rest + n_rest, 128 * j : 128 * j + 128] = strips_ref[j, 32 : 32 + n_rest]
    solve_half(x_ref, 0, 0, u1_ref, w1_ref)
    x_ref[:, HALF:] = x_ref[:, HALF:] - mm(x_ref[:, :HALF], x_ref[:HALF, :HALF], NT)
    a_ref[...] = x_ref[:HALF, HALF:]
    factor_loop(a_ref, u2_ref, w2_ref)
    solve_half(x_ref, HALF, HALF, u2_ref, w2_ref)
    win_out[...] = x_ref[win:rest, aligned(q, HALF)]
    rest_out[...] = x_ref[rest : rest + n_rest, aligned(c, 128)]
    product_out[...] = mm(x_ref[rest:, :], x_ref[win:rest, :], NT)[0:n_rest]
    left = c < 4

    @pl.when(left & (q == 0))
    def _():
        top_out[...] = u1_ref[aligned(c, 128), :].T

    @pl.when(jnp.logical_not(left) & (q == 0))
    def _():
        top_out[...] = jnp.zeros(top_out.shape, f32)

    @pl.when(left & (q == 1))
    def _():
        top_out[...] = x_ref[:HALF, aligned(c, 128)]

    @pl.when(jnp.logical_not(left) & (q == 1))
    def _():
        top_out[...] = u2_ref[aligned(c - 4, 128), :].T


def call(kernel, outs, scratch, micros, *args):
    shape = lambda s: jax.ShapeDtypeStruct(s, f32)
    return pl.pallas_call(
        kernel,
        out_shape=tuple(shape(s) for s in outs),
        scratch_shapes=[pltpu.VMEM(s, f32) for s in scratch],
        compiler_params=pltpu.CompilerParams(vmem_limit_bytes=48 << 20),
        cost_estimate=pl.CostEstimate(
            flops=int(micros * 1e9), transcendentals=0, bytes_accessed=int(micros * 3e6)
        ),
    )(*args)


def swap_rows(value):
    return lax.ppermute(value, "row", [(0, 1), (1, 0)])


def spread(value, axis):
    n = lax.axis_size(axis)
    return lax.all_to_all(jnp.broadcast_to(value, (n,) + value.shape), axis, 0, 0)


def per_device(panel_top, panel_win, panel_rest, trail_rest):
    q = lax.axis_index("row")
    (pieces,) = call(pack_kernel, [(16, 180, 128)], [], 2, panel_top[0], panel_win[0], panel_rest[0])
    sums = jnp.sum(lax.all_to_all(pieces, "layer", 0, 0), axis=0)
    strips = spread(sums[64:], "col")
    kept = lax.dynamic_slice_in_dim(strips, 16 * q, 16, 1)
    got = swap_rows(lax.dynamic_slice_in_dim(strips, 16 * (1 - q), 16, 1))
    half0 = jnp.where(q == 0, kept[:4], got[:4])
    half1 = jnp.where(q == 0, got, kept)
    own = spread(jnp.concatenate([half0.reshape(64, 128), sums[:64]], axis=0), "layer")
    other = swap_rows(own)
    own, other, half1, trail_rest = lax.optimization_barrier((own, other, half1, trail_rest))
    own2 = spread(half1, "layer")
    u1, w1 = call(first_kernel, [(HALF, HALF), (4, 128, 128)], [(HALF, HALF)], 24, own, other)
    own2, u1, trail_rest = lax.optimization_barrier((own2, u1, trail_rest))
    other2 = swap_rows(own2)
    trail_parts = lax.all_to_all(trail_rest[0].reshape(16, 84, 256), "layer", 0, 0)
    top_block, win_block, rest_block, product = call(
        second_kernel,
        [(HALF, 128), (256, HALF), (84, 128), (84, 256)],
        [(HALF, HALF), (4, 128, 128), (856, 2 * HALF), (HALF, HALF)],
        30, own, other, own2, other2, strips, u1, w1,
    )
    return top_block, win_block, rest_block, jnp.sum(trail_parts, axis=0) - product


def solution(mesh):
    return jax.shard_map(
        per_device,
        mesh=mesh,
        in_specs=(
            P("layer", "row", "col"),
            P("layer", "col", "row"),
            P("layer", "row", "col"),
            P("layer", "row", "col"),
        ),
        out_specs=(
            P("row", "col"),
            P("col", "row"),
            P(("row", "layer"), "col"),
            P(("row", "layer"), "col"),
        ),
        check_vma=False,
    )
```

time: 215 us -> 162 us (0.75)
  waiting for transfers between devices: 54.4 us -> 17.9 us
  local copies, waits for them, and re-layouts: 19.4 us -> 12.4 us
  starting transfers between devices: 29.8 us -> 24.1 us
  other arithmetic: 4.39 us -> 2.21 us
    all_to_all x2 -> x1, waiting for transfers between devices: 37 us -> 0.01 us  [per_device(): lax.all_to_all(trail_rest[0].reshape(16, 84, 256), 'layer', 0, 0)]
    all_to_all x1, blocking collectives: 17.5 us -> 28.6 us  [per_device(): sums = jnp.sum(lax.all_to_all(pieces, 'layer', 0, 0), axis=0)]
    all_to_all x2 -> x1, blocking collectives: 29.8 us -> 19.4 us  [spread(): lax.all_to_all(jnp.broadcast_to(value, (n,) + value.shape), axis, 0, 0)]
    unnamed x28 -> x16, local copies, waits for them, and re-layouts: 11.6 us -> 7.87 us
    all_to_all x3 -> x2, starting transfers between devices: 14.9 us -> 11.8 us  [spread(): lax.all_to_all(jnp.broadcast_to(value, (n,) + value.shape), axis, 0, 0)]
    concatenate x1, other arithmetic: 2.61 us -> 0.01 us  [per_device(): jnp.concatenate([half0.reshape(64, 128), sums[:64]], axis=0)]
    all_to_all x3 -> x2, waiting for transfers between devices: 15.9 us -> 14.7 us  [spread(): lax.all_to_all(jnp.broadcast_to(value, (n,) + value.shape), axis, 0, 0)]
    all_to_all x2 -> x1, starting transfers between devices: 8.09 us -> 6.93 us  [per_device(): lax.all_to_all(trail_rest[0].reshape(16, 84, 256), 'layer', 0, 0)]
  transfers between devices with their start and end apart: 8 -> 6, of which waited for: 5 -> 3; matrix products, arithmetic and copies ran while one was open for 5% -> 2% of each run, Pallas kernels for 24% -> 35%
where the time goes in v2:
time: 162 us
  Pallas kernels  56.4 us (35%)
  blocking collectives  48 us (30%)
  starting transfers between devices  24.1 us (15%)
  waiting for transfers between devices  17.9 us (11%)
  local copies, waits for them, and re-layouts  12.4 us (8%)
  other arithmetic  2.21 us (1%)
    pallas_call x3, Pallas kernels, call(): pl.pallas_call(kernel, out_shape=tuple((shape(s) for s in outs)), scratch...  56.4 us
    all_to_all x1, blocking collectives, per_device(): sums = jnp.sum(lax.all_to_all(pieces, 'layer', 0, 0), axis=0)  28.6 us
    all_to_all x1, blocking collectives, spread(): lax.all_to_all(jnp.broadcast_to(value, (n,) + value.shape), axis, 0, 0)  19.4 us
    all_to_all x2, waiting for transfers between devices, spread(): lax.all_to_all(jnp.broadcast_to(value, (n,) + value.shape), axis, 0, 0)  14.7 us
    all_to_all x2, starting transfers between devices, spread(): lax.all_to_all(jnp.broadcast_to(value, (n,) + value.shape), axis, 0, 0)  11.8 us
    unnamed x16, local copies, waits for them, and re-layouts  7.87 us
    all_to_all x1, starting transfers between devices, per_device(): lax.all_to_all(trail_rest[0].reshape(16, 84, 256), 'layer', 0, 0)  6.93 us
    ppermute x3, starting transfers between devices, swap_rows(): return lax.ppermute(value, 'row', [(0, 1), (1, 0)])  5.29 us
  transfers between devices with their start and end apart: 6, of which 3 were waited for; matrix products, arithmetic and copies ran while one was open for 2% of the time, Pallas kernels for 35%

profile of v2, /device:TPU:1, one launch (start us, length us, event | category | flops | bytes accessed | tf_op | source)
XLA Modules:
  0.0 161.6 jit_solution(3843060329899966274)
XLA Ops:
  0.6 0.0 copy-start.3
  0.6 1.1 copy-done.3
  1.7 0.0 copy-start.4
  1.7 1.0 copy-done.4
  2.8 0.0 copy-start.5
  2.8 0.9 copy-done.5
  3.7 0.1 shard_map.75
  3.8 28.6 %all_to_all.25 = f32[16,180,128]{2,1,0:T(8,128)S(1)} all-to-all(f32[16,180,128]{2,1,0:T(8,128)S(1)} %shard_map.75), channel_id=1, replica_groups=mesh['row'=2,'col'=8,'layer'=16] {'layer'}, dimensions={0} | all-to-all | bytes 2949120 | tf_op jit(solution)/shard_map/all_to_all | solution.py:192
  32.4 0.1 reduce_sum.18
  32.5 0.8 broadcast_in_dim.9
  33.3 8.2 %all-to-all-start.1 = ((f32[8,116,128]{2,1,0:T(8,128)}), f32[8,116,128]{2,1,0:T(8,128)S(1)}, u32[]{:S(2)}, u32[]{:S(2)}) async-start(f32[8,116,128]{2,1,0:T(8,128)} %broadcast_in_dim.9), calls=%async_computation.1 | async-start | bytes 983040 | tf_op jit(solution)/shard_map/all_to_all | solution.py:186
  41.5 14.7 %all-to-all-done.1.strips_ref = f32[8,116,128]{2,1,0:T(8,128)S(1)} async-done(((f32[8,116,128]{2,1,0:T(8,128)}), f32[8,116,128]{2,1,0:T(8,128)S(1)}, u32[]{:S(2)}, u32[]{:S(2)}) %all-to-all-start.1) | async-done | bytes 475168 | tf_op jit(solution)/shard_map/all_to_all | solution.py:186
  56.2 3.2 %collective-permute-start = (f32[8,16,128]{2,1,0:T(8,128)S(1)}, f32[8,16,128]{2,1,0:T(8,128)S(1)}, u32[]{:S(2)}, u32[]{:S(2)}) collective-permute-start(f32[8,16,128]{2,1,0:T(8,128)S(1)} %constant_dynamic-slice_fusion), channel_id=1, source_target_pairs={{0,128},{128,0},{1,129},{129,1},{2,130},{130,2},{3,131},{131,3},{4... | collective-permute-start | bytes 196616 | tf_op jit(solution)/shard_map/ppermute | solution.py:181
  59.4 0.9 collective-permute-done
  60.3 0.1 broadcast_in_dim.10
  60.4 19.4 %all_to_all.26.own_ref = f32[16,128,128]{2,1,0:T(8,128)S(1)} all-to-all(f32[16,128,128]{2,1,0:T(8,128)S(1)} %broadcast_in_dim.10), channel_id=1, replica_groups=mesh['row'=2,'col'=8,'layer'=16] {'layer'}, dimensions={0} | all-to-all | bytes 2097152 | tf_op jit(solution)/shard_map/all_to_all | solution.py:186
  79.8 1.8 %collective-permute-start.1 = (f32[16,128,128]{2,1,0:T(8,128)S(1)}, f32[16,128,128]{2,1,0:T(8,128)S(1)}, u32[]{:S(2)}, u32[]{:S(2)}) collective-permute-start(f32[16,128,128]{2,1,0:T(8,128)S(1)} %all_to_all.26.own_ref), channel_id=1, source_target_pairs={{0,128},{128,0},{1,129},{129,1},{2,130},{130,2},{3,131},{131,3},{4... | collective-permute-start | bytes 3145736 | tf_op jit(solution)/shard_map/ppermute | solution.py:181
  81.5 2.3 %collective-permute-done.1.other_ref = f32[16,128,128]{2,1,0:T(8,128)S(1)} collective-permute-done((f32[16,128,128]{2,1,0:T(8,128)S(1)}, f32[16,128,128]{2,1,0:T(8,128)S(1)}, u32[]{:S(2)}, u32[]{:S(2)}) %collective-permute-start.1) | collective-permute-done | bytes 1048608 | tf_op jit(solution)/shard_map/ppermute | solution.py:181
  83.8 0.0 copy-start
  83.8 1.1 broadcast_in_dim.11
  84.9 0.2 copy-done
  85.1 3.7 %all-to-all-start.3 = ((f32[16,8,16,128]{3,2,1,0:T(8,128)}), f32[16,8,16,128]{3,2,1,0:T(8,128)S(1)}, u32[]{:S(2)}, u32[]{:S(2)}) async-start(f32[16,8,16,128]{3,2,1,0:T(8,128)} %broadcast_in_dim.11), calls=%async_computation.3 | async-start | bytes 2097152 | tf_op jit(solution)/shard_map/all_to_all | solution.py:186
  88.8 0.0 copy-start.1
  88.8 1.2 copy-done.1
  90.0 23.3 %shard_map.76 = (f32[512,512]{1,0:T(8,128)S(1)}, f32[4,128,128]{2,1,0:T(8,128)S(1)}) custom-call(f32[16,128,128]{2,1,0:T(8,128)S(1)} %all_to_all.26.own_ref, f32[16,128,128]{2,1,0:T(8,128)S(1)} %copy-done.1), custom_call_target="tpu_custom_call" | custom-call | flops 24000000000 | bytes 72000000 | tf_op jit(solution)/shard_map/pallas_call | solution.py:169
  113.3 0.0 copy-start.6
  113.3 1.0 copy-done.6
  114.3 0.0 all-to-all-done.3.own2_ref
  114.3 0.4 collective-permute-start.2
  114.7 2.4 %reshape_squeeze.3 = f32[16,84,256]{2,1,0:T(8,128)} reshape(f32[1,1344,256]{2,1,0:T(8,128)} %param.7) | data formatting | bytes 2752512 | tf_op jit(solution)/shard_map/reshape;squeeze | solution.py:205
  117.1 6.9 %all-to-all-start.4 = ((f32[16,84,256]{2,1,0:T(8,128)}), f32[16,84,256]{2,1,0:T(8,128)}, u32[]{:S(2)}, u32[]{:S(2)}) async-start(f32[16,84,256]{2,1,0:T(8,128)} %reshape_squeeze.3), calls=%async_computation.4 | async-start | bytes 2883584 | tf_op jit(solution)/shard_map/all_to_all | solution.py:205
  124.0 0.0 collective-permute-done.2.other2_ref
  124.1 0.0 copy-start.2
  124.1 1.2 copy-done.2
  125.3 0.0 copy-start.7
  125.3 1.2 copy-done.7
  126.5 33.0 %shard_map.77 = (f32[512,128]{1,0:T(8,128)}, f32[256,512]{1,0:T(8,128)}, f32[84,128]{1,0:T(8,128)}, f32[84,256]{1,0:T(8,128)S(1)}) custom-call(f32[16,128,128]{2,1,0:T(8,128)S(1)} %all_to_all.26.own_ref, f32[16,128,128]{2,1,0:T(8,128)S(1)} %copy-done.2, f32[16,8,16,128]{3,2,1,0:T(8,128)S(1)} %all-to-all-done.3.own2_ref, ...), custom_call_target="tpu_custom_call" | custom-call | flops 30000001024 | bytes 90000000 | tf_op jit(solution)/shard_map/pallas_call | solution.py:169
  159.5 0.0 all-to-all-done.4
  159.5 1.5 reduce_sum.19
  160.9 0.7 sub.7
  (6 shorter events, 0.1 us)
Async XLA Ops:
  0.6 1.1 copy-start.3
  1.7 1.0 copy-start.4
  2.8 0.9 copy-start.5
  33.3 22.9 %all-to-all-start.1 = ((f32[8,116,128]{2,1,0:T(8,128)}), f32[8,116,128]{2,1,0:T(8,128)S(1)}, u32[]{:S(2)}, u32[]{:S(2)}) async-start(f32[8,116,128]{2,1,0:T(8,128)} %broadcast_in_dim.9), calls=%async_computation.1 | async-start | bytes 983040 | tf_op jit(solution)/shard_map/all_to_all | solution.py:186
  56.2 4.1 %collective-permute-start = (f32[8,16,128]{2,1,0:T(8,128)S(1)}, f32[8,16,128]{2,1,0:T(8,128)S(1)}, u32[]{:S(2)}, u32[]{:S(2)}) collective-permute-start(f32[8,16,128]{2,1,0:T(8,128)S(1)} %constant_dynamic-slice_fusion), channel_id=1, source_target_pairs={{0,128},{128,0},{1,129},{129,1},{2,130},{130,2},{3,131},{131,3},{4... | collective-permute-start | bytes 196616 | tf_op jit(solution)/shard_map/ppermute | solution.py:181
  79.8 4.0 %collective-permute-start.1 = (f32[16,128,128]{2,1,0:T(8,128)S(1)}, f32[16,128,128]{2,1,0:T(8,128)S(1)}, u32[]{:S(2)}, u32[]{:S(2)}) collective-permute-start(f32[16,128,128]{2,1,0:T(8,128)S(1)} %all_to_all.26.own_ref), channel_id=1, source_target_pairs={{0,128},{128,0},{1,129},{129,1},{2,130},{130,2},{3,131},{131,3},{4... | collective-permute-start | bytes 3145736 | tf_op jit(solution)/shard_map/ppermute | solution.py:181
  83.8 1.3 copy-start
  85.1 29.2 %all-to-all-start.3 = ((f32[16,8,16,128]{3,2,1,0:T(8,128)}), f32[16,8,16,128]{3,2,1,0:T(8,128)S(1)}, u32[]{:S(2)}, u32[]{:S(2)}) async-start(f32[16,8,16,128]{3,2,1,0:T(8,128)} %broadcast_in_dim.11), calls=%async_computation.3 | async-start | bytes 2097152 | tf_op jit(solution)/shard_map/all_to_all | solution.py:186
  88.8 1.2 copy-start.1
  113.3 1.0 copy-start.6
  114.3 9.8 %collective-permute-start.2 = (f32[16,8,16,128]{3,2,1,0:T(8,128)S(1)}, f32[16,8,16,128]{3,2,1,0:T(8,128)}, u32[]{:S(2)}, u32[]{:S(2)}) collective-permute-start(f32[16,8,16,128]{3,2,1,0:T(8,128)S(1)} %all-to-all-done.3.own2_ref), channel_id=1, source_target_pairs={{0,128},{128,0},{1,129},{129,1},{2,130},{130,2},{3,131},{131,3},{4... | collective-permute-start | bytes 3145736 | tf_op jit(solution)/shard_map/ppermute | solution.py:181
  117.1 42.4 %all-to-all-start.4 = ((f32[16,84,256]{2,1,0:T(8,128)}), f32[16,84,256]{2,1,0:T(8,128)}, u32[]{:S(2)}, u32[]{:S(2)}) async-start(f32[16,84,256]{2,1,0:T(8,128)} %reshape_squeeze.3), calls=%async_computation.4 | async-start | bytes 2883584 | tf_op jit(solution)/shard_map/all_to_all | solution.py:205
  124.1 1.2 copy-start.2
  125.3 1.2 copy-start.7

commit v3 on v2

--- a/solution.py
+++ b/solution.py
@@ -16,68 +16,83 @@
     d=lambda x,y: lax.dot_general(x,y,dims,preferred_element_type=f32)
     return d(ah,bh)+(d(ah,bl)+d(al,bh))
 
-def chol128(groups):
-    lane=lax.broadcasted_iota(jnp.int32,(8,128),1)
-    sub=lax.broadcasted_iota(jnp.int32,(8,128),0)
-    bc=lambda x: jnp.broadcast_to(x,(8,128))
-    S=list(groups); U=[]; W=[]
-    for t in range(16):
-        o=8*t
-        St=S[t]
-        inblk=(lane>=o)&(lane<o+8)
-        P=[bc(St[i:i+1,:]) for i in range(8)]
-        a=[[bc(P[i][:,o+j:o+j+1]) for j in range(i+1)] for i in range(8)]
-        C={g:[bc(S[g][:,o+m:o+m+1]) for m in range(8)] for g in range(t+1,16)}
-        P=[jnp.where(inblk,jnp.where(lane==o+i,1.0,0.0),P[i]) for i in range(8)]
-        r=[None]*8; R=[None]*8
-        for m in range(8):
-            r[m]=lax.rsqrt(a[m][m])
-            for i in range(m+1,8): a[i][m]=a[i][m]*r[m]
-            a[m][m]=a[m][m]*r[m]
-            for i in range(m+1,8):
-                for j in range(m+1,i+1):
-                    a[i][j]=a[i][j]-a[i][m]*a[j][m]
-            R[m]=P[m]*r[m]
-            for i in range(m+1,8): P[i]=P[i]-a[i][m]*R[m]
-        V=[None]*8
-        for m in range(7,-1,-1):
-            acc=R[m]
-            for j in range(7,m,-1): acc=acc-a[j][m]*V[j]
-            V[m]=acc*r[m]
-        for g in range(t+1,16):
-            x=jnp.where(inblk,0.0,S[g])
-            for m in range(8): x=x-C[g][m]*V[m]
-            S[g]=x
-        ut=jnp.zeros((8,128),f32); wt=ut
-        for m in range(8):
-            row=R[m]
-            wt=jnp.where(sub==m,row,wt)
-            for i in range(m,8): row=jnp.where(lane==o+i,a[i][m],row)
-            if m: row=jnp.where((lane>=o)&(lane<o+m),0.0,row)
-            ut=jnp.where(sub==m,row,ut)
-        U.append(jnp.where(lane>=o,ut,0.0)); W.append(jnp.where(lane<o+8,wt,0.0))
-    return U,W
+def block_inverse(block):
+    lane = lax.broadcasted_iota(jnp.int32, (8, 128), 1)
+    sub = lax.broadcasted_iota(jnp.int32, (8, 128), 0)
+    wide = lambda x: jnp.broadcast_to(x, (8, 128))
+    S = [block[8 * g : 8 * g + 8] for g in range(16)]
+    inverse = []
+    for t in range(8):
+        o = 16 * t
+        inside = (lane >= o) & (lane < o + 16)
+        mine = (2 * t, 2 * t + 1)
+        cols = [[wide(S[g][:, o + j : o + j + 1]) for g in mine] for j in range(16)]
+        P = [
+            jnp.where(inside, jnp.where(lane - o - 8 * k == sub, 1.0, 0.0), S[g])
+            for k, g in enumerate(mine)
+        ]
+        rows = [jnp.zeros((8, 128), f32)] * 2
+        pivots = [jnp.ones((8, 128), f32)] * 2
+        for m in range(16):
+            k, s = divmod(m, 8)
+            here = sub == s
+            pivot = wide(cols[m][k][s : s + 1])
+            scale = 1.0 / pivot
+            pivots[k] = jnp.where(here, pivot, pivots[k])
+            rows[k] = jnp.where(here, P[k], rows[k])
+            for j in range(m + 1, 16):
+                f = wide(cols[j][k][s : s + 1]) * scale
+                for i in range(2):
+                    x = cols[j][i] - cols[m][i] * f
+                    cols[j][i] = jnp.where(here, f, x) if i == k else x
+            f = wide(P[k][s : s + 1]) * scale
+            for i in range(2):
+                x = P[i] - cols[m][i] * f
+                P[i] = jnp.where(here, f, x) if i == k else x
+        V = [wide(P[m // 8][m % 8 : m % 8 + 1]) for m in range(16)]
+        for g in range(2 * t + 2, min(16, 2 * t + 4)):
+            x = jnp.where(inside, 0.0, S[g])
+            for m in range(16):
+                x = x - wide(S[g][:, o + m : o + m + 1]) * V[m]
+            S[g] = x
+        far = range(2 * t + 4, 16)
+        if far:
+            pads = [jnp.zeros((n, 128), bf16) for n in (o, 112 - o)]
+            full = lambda v: jnp.concatenate(
+                [x for x in (pads[0], v, pads[1]) if x.shape[0]], axis=0
+            )
+            vh, vl = (full(v) for v in split(jnp.concatenate(P, axis=0)))
+            xh, xl = split(jnp.concatenate([S[g] for g in far], axis=0))
+            d = lambda x, y: lax.dot_general(x, y, NN, preferred_element_type=f32)
+            y = d(xh, vh) + (d(xh, vl) + d(xl, vh))
+            for n, g in enumerate(far):
+                S[g] = jnp.where(inside, 0.0, S[g]) - y[8 * n : 8 * n + 8]
+        for k in range(2):
+            inverse.append(jnp.where(lane < o + 16, rows[k] * lax.rsqrt(pivots[k]), 0.0))
+    return jnp.concatenate(inverse, axis=0)
 
 
 def factor_loop(a_ref, u_ref, w_ref):
     n = a_ref.shape[0]
-
-    def body(k, _):
+    blocks = n // 128
+    ahead = lax.broadcasted_iota(jnp.int32, (128, n), 1) - lax.broadcasted_iota(
+        jnp.int32, (128, n), 0
+    )
+
+    def step(k, diagonal, first=False):
         o = pl.multiple_of(k * 128, 128)
-        rows = [pl.ds(pl.multiple_of(o + 8 * g, 8), 8) for g in range(16)]
-        upper, inverse = chol128([a_ref[rows[g], pl.ds(o, 128)] for g in range(16)])
-        for g in range(16):
-            w_ref[k, 8 * g : 8 * g + 8, :] = inverse[g]
-        panel = mm(w_ref[k], a_ref[pl.ds(o, 128), :])
-        col = lax.broadcasted_iota(jnp.int32, (128, n), 1)
-        panel = jnp.where(col >= o + 128, panel, 0.0)
-        u_ref[pl.ds(o, 128), :] = panel
-        for g in range(16):
-            u_ref[rows[g], pl.ds(o, 128)] = upper[g]
-        a_ref[...] = a_ref[...] - mm(panel, panel, TN)
-        return 0
-
-    lax.fori_loop(0, n // 128, body, 0)
+        inverse = block_inverse(diagonal)
+        if not first:
+            past = u_ref[pl.ds(pl.multiple_of(k * 128 - 128, 128), 128), :]
+            a_ref[...] = a_ref[...] - mm(past, past, TN)
+        w_ref[k] = inverse
+        panel = mm(inverse, a_ref[pl.ds(o, 128), :])
+        u_ref[pl.ds(o, 128), :] = jnp.where(ahead >= o, panel, 0.0)
+        following = pl.ds(pl.multiple_of(jnp.minimum(k + 1, blocks - 1) * 128, 128), 128)
+        corner = u_ref[pl.ds(o, 128), following]
+        return a_ref[following, following] - mm(corner, corner, TN)
+
+    lax.fori_loop(1, blocks, step, step(0, a_ref[0:128, 0:128], True))
 
 
 def solve_half(x_ref, first, lanes, u_ref, w_ref):

time: 162 us -> 142 us (0.88)
  Pallas kernels: 56.4 us -> 35.3 us
  waiting for transfers between devices: 17.9 us -> 19.8 us
    pallas_call x3, Pallas kernels: 56.4 us -> 35.3 us  [call(): pl.pallas_call(kernel, out_shape=tuple((shape(s) for s in outs)), scratch...]
    all_to_all x1, starting transfers between devices: 6.93 us -> 4.57 us  [per_device(): lax.all_to_all(trail_rest[0].reshape(16, 84, 256), 'layer', 0, 0)]
    all_to_all x2, waiting for transfers between devices: 14.7 us -> 16.7 us  [spread(): lax.all_to_all(jnp.broadcast_to(value, (n,) + value.shape), axis, 0, 0)]
  transfers between devices with their start and end apart: 6 -> 6, of which waited for: 3 -> 4; matrix products, arithmetic and copies ran while one was open for 2% -> 2% of each run, Pallas kernels for 35% -> 25%
where the time goes in v3:
time: 142 us; the launch traced here: 141 us
  blocking collectives  48 us (34%)
  Pallas kernels  35.3 us (25%)
  starting transfers between devices  23 us (16%)
  waiting for transfers between devices  19.8 us (14%)
  local copies, waits for them, and re-layouts  12.4 us (9%)
  other arithmetic  2.21 us (2%)
    pallas_call x3, Pallas kernels, call(): pl.pallas_call(kernel, out_shape=tuple((shape(s) for s in outs)), scratch...  35.3 us
    all_to_all x1, blocking collectives, per_device(): sums = jnp.sum(lax.all_to_all(pieces, 'layer', 0, 0), axis=0)  28.6 us
    all_to_all x1, blocking collectives, spread(): lax.all_to_all(jnp.broadcast_to(value, (n,) + value.shape), axis, 0, 0)  19.4 us
    all_to_all x2, waiting for transfers between devices, spread(): lax.all_to_all(jnp.broadcast_to(value, (n,) + value.shape), axis, 0, 0)  16.7 us
    all_to_all x2, starting transfers between devices, spread(): lax.all_to_all(jnp.broadcast_to(value, (n,) + value.shape), axis, 0, 0)  11.8 us
    unnamed x16, local copies, waits for them, and re-layouts  7.87 us
    ppermute x3, starting transfers between devices, swap_rows(): return lax.ppermute(value, 'row', [(0, 1), (1, 0)])  6.62 us
    all_to_all x1, starting transfers between devices, per_device(): lax.all_to_all(trail_rest[0].reshape(16, 84, 256), 'layer', 0, 0)  4.57 us
  transfers between devices with their start and end apart: 6, of which 4 were waited for; matrix products, arithmetic and copies ran while one was open for 2% of the time, Pallas kernels for 25%

profile of v3, /device:TPU:1, one launch (start us, length us, event | category | flops | bytes accessed | tf_op | source)
XLA Modules:
  0.0 141.5 jit_solution(1765192811209282005)
XLA Ops:
  0.6 0.0 copy-start.3
  0.6 1.1 copy-done.3
  1.7 0.0 copy-start.4
  1.7 1.0 copy-done.4
  2.8 0.0 copy-start.5
  2.8 0.9 copy-done.5
  3.7 0.1 shard_map.75
  3.8 28.6 %all_to_all.25 = f32[16,180,128]{2,1,0:T(8,128)S(1)} all-to-all(f32[16,180,128]{2,1,0:T(8,128)S(1)} %shard_map.75), channel_id=1, replica_groups=mesh['row'=2,'col'=8,'layer'=16] {'layer'}, dimensions={0} | all-to-all | bytes 2949120 | tf_op jit(solution)/shard_map/all_to_all | solution.py:207
  32.4 0.1 reduce_sum.18
  32.5 0.8 broadcast_in_dim.9
  33.3 8.2 %all-to-all-start.1 = ((f32[8,116,128]{2,1,0:T(8,128)}), f32[8,116,128]{2,1,0:T(8,128)S(1)}, u32[]{:S(2)}, u32[]{:S(2)}) async-start(f32[8,116,128]{2,1,0:T(8,128)} %broadcast_in_dim.9), calls=%async_computation.1 | async-start | bytes 983040 | tf_op jit(solution)/shard_map/all_to_all | solution.py:201
  41.5 14.7 %all-to-all-done.1.strips_ref = f32[8,116,128]{2,1,0:T(8,128)S(1)} async-done(((f32[8,116,128]{2,1,0:T(8,128)}), f32[8,116,128]{2,1,0:T(8,128)S(1)}, u32[]{:S(2)}, u32[]{:S(2)}) %all-to-all-start.1) | async-done | bytes 475168 | tf_op jit(solution)/shard_map/all_to_all | solution.py:201
  56.2 3.2 %collective-permute-start = (f32[8,16,128]{2,1,0:T(8,128)S(1)}, f32[8,16,128]{2,1,0:T(8,128)S(1)}, u32[]{:S(2)}, u32[]{:S(2)}) collective-permute-start(f32[8,16,128]{2,1,0:T(8,128)S(1)} %constant_dynamic-slice_fusion), channel_id=1, source_target_pairs={{0,128},{128,0},{1,129},{129,1},{2,130},{130,2},{3,131},{131,3},{4... | collective-permute-start | bytes 196616 | tf_op jit(solution)/shard_map/ppermute | solution.py:196
  59.4 0.9 collective-permute-done
  60.3 0.1 broadcast_in_dim.10
  60.4 19.4 %all_to_all.26.own_ref = f32[16,128,128]{2,1,0:T(8,128)S(1)} all-to-all(f32[16,128,128]{2,1,0:T(8,128)S(1)} %broadcast_in_dim.10), channel_id=1, replica_groups=mesh['row'=2,'col'=8,'layer'=16] {'layer'}, dimensions={0} | all-to-all | bytes 2097152 | tf_op jit(solution)/shard_map/all_to_all | solution.py:201
  79.8 1.8 %collective-permute-start.1 = (f32[16,128,128]{2,1,0:T(8,128)S(1)}, f32[16,128,128]{2,1,0:T(8,128)S(1)}, u32[]{:S(2)}, u32[]{:S(2)}) collective-permute-start(f32[16,128,128]{2,1,0:T(8,128)S(1)} %all_to_all.26.own_ref), channel_id=1, source_target_pairs={{0,128},{128,0},{1,129},{129,1},{2,130},{130,2},{3,131},{131,3},{4... | collective-permute-start | bytes 3145736 | tf_op jit(solution)/shard_map/ppermute | solution.py:196
  81.5 2.3 %collective-permute-done.1.other_ref = f32[16,128,128]{2,1,0:T(8,128)S(1)} collective-permute-done((f32[16,128,128]{2,1,0:T(8,128)S(1)}, f32[16,128,128]{2,1,0:T(8,128)S(1)}, u32[]{:S(2)}, u32[]{:S(2)}) %collective-permute-start.1) | collective-permute-done | bytes 1048608 | tf_op jit(solution)/shard_map/ppermute | solution.py:196
  83.8 0.0 copy-start
  83.8 1.1 broadcast_in_dim.11
  84.9 0.2 copy-done
  85.1 3.7 %all-to-all-start.3 = ((f32[16,8,16,128]{3,2,1,0:T(8,128)}), f32[16,8,16,128]{3,2,1,0:T(8,128)S(1)}, u32[]{:S(2)}, u32[]{:S(2)}) async-start(f32[16,8,16,128]{3,2,1,0:T(8,128)} %broadcast_in_dim.11), calls=%async_computation.3 | async-start | bytes 2097152 | tf_op jit(solution)/shard_map/all_to_all | solution.py:201
  88.8 0.0 copy-start.1
  88.8 1.2 copy-done.1
  90.0 12.8 %shard_map.76 = (f32[512,512]{1,0:T(8,128)S(1)}, f32[4,128,128]{2,1,0:T(8,128)S(1)}) custom-call(f32[16,128,128]{2,1,0:T(8,128)S(1)} %all_to_all.26.own_ref, f32[16,128,128]{2,1,0:T(8,128)S(1)} %copy-done.1), custom_call_target="tpu_custom_call" | custom-call | flops 24000000000 | bytes 72000000 | tf_op jit(solution)/shard_map/pallas_call | solution.py:184
  102.8 0.0 copy-start.6
  102.9 1.0 copy-done.6
  103.8 2.0 %all-to-all-done.3.own2_ref = f32[16,8,16,128]{3,2,1,0:T(8,128)S(1)} async-done(((f32[16,8,16,128]{3,2,1,0:T(8,128)}), f32[16,8,16,128]{3,2,1,0:T(8,128)S(1)}, u32[]{:S(2)}, u32[]{:S(2)}) %all-to-all-start.3) | async-done | bytes 1048608 | tf_op jit(solution)/shard_map/all_to_all | solution.py:201
  105.8 1.7 %collective-permute-start.2 = (f32[16,8,16,128]{3,2,1,0:T(8,128)S(1)}, f32[16,8,16,128]{3,2,1,0:T(8,128)}, u32[]{:S(2)}, u32[]{:S(2)}) collective-permute-start(f32[16,8,16,128]{3,2,1,0:T(8,128)S(1)} %all-to-all-done.3.own2_ref), channel_id=1, source_target_pairs={{0,128},{128,0},{1,129},{129,1},{2,130},{130,2},{3,131},{131,3},{4... | collective-permute-start | bytes 3145736 | tf_op jit(solution)/shard_map/ppermute | solution.py:196
  107.5 2.4 %reshape_squeeze.3 = f32[16,84,256]{2,1,0:T(8,128)} reshape(f32[1,1344,256]{2,1,0:T(8,128)} %param.7) | data formatting | bytes 2752512 | tf_op jit(solution)/shard_map/reshape;squeeze | solution.py:220
  110.0 4.6 %all-to-all-start.4 = ((f32[16,84,256]{2,1,0:T(8,128)}), f32[16,84,256]{2,1,0:T(8,128)}, u32[]{:S(2)}, u32[]{:S(2)}) async-start(f32[16,84,256]{2,1,0:T(8,128)} %reshape_squeeze.3), calls=%async_computation.4 | async-start | bytes 2883584 | tf_op jit(solution)/shard_map/all_to_all | solution.py:220
  114.5 0.0 collective-permute-done.2.other2_ref
  114.5 0.0 copy-start.2
  114.6 1.2 copy-done.2
  115.8 0.0 copy-start.7
  115.8 1.2 copy-done.7
  117.0 22.4 %shard_map.77 = (f32[512,128]{1,0:T(8,128)}, f32[256,512]{1,0:T(8,128)}, f32[84,128]{1,0:T(8,128)}, f32[84,256]{1,0:T(8,128)S(1)}) custom-call(f32[16,128,128]{2,1,0:T(8,128)S(1)} %all_to_all.26.own_ref, f32[16,128,128]{2,1,0:T(8,128)S(1)} %copy-done.2, f32[16,8,16,128]{3,2,1,0:T(8,128)S(1)} %all-to-all-done.3.own2_ref, ...), custom_call_target="tpu_custom_call" | custom-call | flops 30000001024 | bytes 90000000 | tf_op jit(solution)/shard_map/pallas_call | solution.py:184
  139.4 0.0 all-to-all-done.4
  139.4 1.5 %reduce_sum.19 = f32[84,256]{1,0:T(8,128)S(1)} reduce(f32[16,84,256]{2,1,0:T(8,128)} %all-to-all-done.4, f32[]{:T(128)} %constant.5.clone.1), dimensions={0}, to_apply=%region_1.2 | reduce | flops 322560 | bytes 1462276 | tf_op jit(solution)/shard_map/reduce_sum | solution.py:227
  140.8 0.7 sub.7
  (6 shorter events, 0.1 us)
Async XLA Ops:
  0.6 1.1 copy-start.3
  1.7 1.0 copy-start.4
  2.8 0.9 copy-start.5
  33.3 22.9 %all-to-all-start.1 = ((f32[8,116,128]{2,1,0:T(8,128)}), f32[8,116,128]{2,1,0:T(8,128)S(1)}, u32[]{:S(2)}, u32[]{:S(2)}) async-start(f32[8,116,128]{2,1,0:T(8,128)} %broadcast_in_dim.9), calls=%async_computation.1 | async-start | bytes 983040 | tf_op jit(solution)/shard_map/all_to_all | solution.py:201
  56.2 4.1 %collective-permute-start = (f32[8,16,128]{2,1,0:T(8,128)S(1)}, f32[8,16,128]{2,1,0:T(8,128)S(1)}, u32[]{:S(2)}, u32[]{:S(2)}) collective-permute-start(f32[8,16,128]{2,1,0:T(8,128)S(1)} %constant_dynamic-slice_fusion), channel_id=1, source_target_pairs={{0,128},{128,0},{1,129},{129,1},{2,130},{130,2},{3,131},{131,3},{4... | collective-permute-start | bytes 196616 | tf_op jit(solution)/shard_map/ppermute | solution.py:196
  79.8 4.0 %collective-permute-start.1 = (f32[16,128,128]{2,1,0:T(8,128)S(1)}, f32[16,128,128]{2,1,0:T(8,128)S(1)}, u32[]{:S(2)}, u32[]{:S(2)}) collective-permute-start(f32[16,128,128]{2,1,0:T(8,128)S(1)} %all_to_all.26.own_ref), channel_id=1, source_target_pairs={{0,128},{128,0},{1,129},{129,1},{2,130},{130,2},{3,131},{131,3},{4... | collective-permute-start | bytes 3145736 | tf_op jit(solution)/shard_map/ppermute | solution.py:196
  83.8 1.3 copy-start
  85.1 20.7 %all-to-all-start.3 = ((f32[16,8,16,128]{3,2,1,0:T(8,128)}), f32[16,8,16,128]{3,2,1,0:T(8,128)S(1)}, u32[]{:S(2)}, u32[]{:S(2)}) async-start(f32[16,8,16,128]{3,2,1,0:T(8,128)} %broadcast_in_dim.11), calls=%async_computation.3 | async-start | bytes 2097152 | tf_op jit(solution)/shard_map/all_to_all | solution.py:201
  88.8 1.2 copy-start.1
  102.8 1.0 copy-start.6
  105.8 8.7 %collective-permute-start.2 = (f32[16,8,16,128]{3,2,1,0:T(8,128)S(1)}, f32[16,8,16,128]{3,2,1,0:T(8,128)}, u32[]{:S(2)}, u32[]{:S(2)}) collective-permute-start(f32[16,8,16,128]{3,2,1,0:T(8,128)S(1)} %all-to-all-done.3.own2_ref), channel_id=1, source_target_pairs={{0,128},{128,0},{1,129},{129,1},{2,130},{130,2},{3,131},{131,3},{4... | collective-permute-start | bytes 3145736 | tf_op jit(solution)/shard_map/ppermute | solution.py:196
  110.0 29.4 %all-to-all-start.4 = ((f32[16,84,256]{2,1,0:T(8,128)}), f32[16,84,256]{2,1,0:T(8,128)}, u32[]{:S(2)}, u32[]{:S(2)}) async-start(f32[16,84,256]{2,1,0:T(8,128)} %reshape_squeeze.3), calls=%async_computation.4 | async-start | bytes 2883584 | tf_op jit(solution)/shard_map/all_to_all | solution.py:220
  114.5 1.2 copy-start.2
  115.8 1.2 copy-start.7

commit v4 on v3

v4 whole, which is shorter than its diff:
```python
import jax, jax.numpy as jnp
from jax import lax
from jax.sharding import PartitionSpec as P
from jax.experimental import pallas as pl
from jax.experimental.pallas import tpu as pltpu
HALF = 512
f32=jnp.float32; bf16=jnp.bfloat16
NN=(((1,),(0,)),((),())); NT=(((1,),(1,)),((),())); TN=(((0,),(0,)),((),()))

def split(a):
    hi=a.astype(bf16); lo=(a-hi.astype(f32)).astype(bf16)
    return hi,lo

def mm(a,b,dims=NN):
    ah,al=split(a); bh,bl=split(b)
    d=lambda x,y: lax.dot_general(x,y,dims,preferred_element_type=f32)
    return d(ah,bh)+(d(ah,bl)+d(al,bh))

def block_inverse(block):
    lane = lax.broadcasted_iota(jnp.int32, (8, 128), 1)
    sub = lax.broadcasted_iota(jnp.int32, (8, 128), 0)
    wide = lambda x: jnp.broadcast_to(x, (8, 128))
    S = [block[8 * g : 8 * g + 8] for g in range(16)]
    inverse = []
    for t in range(8):
        o = 16 * t
        inside = (lane >= o) & (lane < o + 16)
        mine = (2 * t, 2 * t + 1)
        cols = [[wide(S[g][:, o + j : o + j + 1]) for g in mine] for j in range(16)]
        P = [
            jnp.where(inside, jnp.where(lane - o - 8 * k == sub, 1.0, 0.0), S[g])
            for k, g in enumerate(mine)
        ]
        rows = [jnp.zeros((8, 128), f32)] * 2
        pivots = [jnp.ones((8, 128), f32)] * 2
        for m in range(16):
            k, s = divmod(m, 8)
            here = sub == s
            pivot = wide(cols[m][k][s : s + 1])
            scale = 1.0 / pivot
            pivots[k] = jnp.where(here, pivot, pivots[k])
            rows[k] = jnp.where(here, P[k], rows[k])
            for j in range(m + 1, 16):
                f = wide(cols[j][k][s : s + 1]) * scale
                for i in range(2):
                    x = cols[j][i] - cols[m][i] * f
                    cols[j][i] = jnp.where(here, f, x) if i == k else x
            f = wide(P[k][s : s + 1]) * scale
            for i in range(2):
                x = P[i] - cols[m][i] * f
                P[i] = jnp.where(here, f, x) if i == k else x
        V = [wide(P[m // 8][m % 8 : m % 8 + 1]) for m in range(16)]
        for g in range(2 * t + 2, min(16, 2 * t + 4)):
            x = jnp.where(inside, 0.0, S[g])
            for m in range(16):
                x = x - wide(S[g][:, o + m : o + m + 1]) * V[m]
            S[g] = x
        far = range(2 * t + 4, 16)
        if far:
            pads = [jnp.zeros((n, 128), bf16) for n in (o, 112 - o)]
            full = lambda v: jnp.concatenate(
                [x for x in (pads[0], v, pads[1]) if x.shape[0]], axis=0
            )
            vh, vl = (full(v) for v in split(jnp.concatenate(P, axis=0)))
            xh, xl = split(jnp.concatenate([S[g] for g in far], axis=0))
            d = lambda x, y: lax.dot_general(x, y, NN, preferred_element_type=f32)
            y = d(xh, vh) + (d(xh, vl) + d(xl, vh))
            for n, g in enumerate(far):
                S[g] = jnp.where(inside, 0.0, S[g]) - y[8 * n : 8 * n + 8]
        for k in range(2):
            inverse.append(jnp.where(lane < o + 16, rows[k] * lax.rsqrt(pivots[k]), 0.0))
    return jnp.concatenate(inverse, axis=0)


def factor_loop(a_ref, u_ref, w_ref, b_ref, beside=lambda: None):
    n = a_ref.shape[0]
    blocks = n // 128
    ahead = lax.broadcasted_iota(jnp.int32, (128, n), 1) - lax.broadcasted_iota(
        jnp.int32, (128, n), 0
    )

    def solve(k):
        here = pl.ds(pl.multiple_of(k * 128, 128), 128)
        return here, mm(b_ref[:, here], w_ref[k], NT)

    def step(k, diagonal, first=False):
        o = pl.multiple_of(k * 128, 128)
        inverse = block_inverse(diagonal)
        if first:
            beside()
        else:
            past = u_ref[pl.ds(pl.multiple_of(k * 128 - 128, 128), 128), :]
            a_ref[...] = a_ref[...] - mm(past, past, TN)
            before, solved = solve(k - 1)
            b_ref[...] = b_ref[...] - mm(solved, past)
            b_ref[:, before] = solved
        w_ref[k] = inverse
        panel = mm(inverse, a_ref[pl.ds(o, 128), :])
        u_ref[pl.ds(o, 128), :] = jnp.where(ahead >= o, panel, 0.0)
        following = pl.ds(pl.multiple_of(jnp.minimum(k + 1, blocks - 1) * 128, 128), 128)
        corner = u_ref[pl.ds(o, 128), following]
        return a_ref[following, following] - mm(corner, corner, TN)

    lax.fori_loop(1, blocks, step, step(0, a_ref[0:128, 0:128], True))
    last, solved = solve(blocks - 1)
    b_ref[:, last] = solved


def solve_rows(x_ref, u_ref, w_ref):
    for k in range(x_ref.shape[1] // 128):
        here = slice(128 * k, 128 * k + 128)
        value = x_ref[:, here]
        if k:
            value = value - mm(x_ref[:, : 128 * k], u_ref[0 : 128 * k, here])
        x_ref[:, here] = mm(value, w_ref[k], NT)


def aligned(index, step):
    return pl.ds(pl.multiple_of(index * step, step), step)


def pack_kernel(top_ref, win_ref, rest_ref, out_ref, whole_ref, sems):
    moves = [
        (win_ref.at[:, :, 128 * j : 128 * j + 128], out_ref.at[:, 8 * j : 8 * j + 8])
        for j in range(4)
    ] + [(top_ref, out_ref.at[:, 32:48]), (rest_ref, whole_ref)]
    copies = [pltpu.make_async_copy(*move, sems.at[n]) for n, move in enumerate(moves)]
    for copy in copies[::-1]:
        copy.start()
    for copy in copies[::-1]:
        copy.wait()
    for piece in range(out_ref.shape[0]):
        out_ref[piece, 48:90] = whole_ref[42 * piece : 42 * piece + 42]


def place_top(q, own_ref, other_ref, refs):
    for which, src in ((q, own_ref), (1 - q, other_ref)):
        for strip in range(src.shape[0]):
            for n, dst in enumerate(refs):
                for c in range(4):
                    first = 64 * n + 16 * c
                    dst[aligned(2 * strip + which, 16), 128 * c : 128 * c + 128] = src[
                        strip, first : first + 16
                    ]


def place_lower(q, half, own_ref, other_ref, rest_own_ref, rest_other_ref, b_ref):
    win = 16 * own_ref.shape[0]
    for which, src in ((q, own_ref), (1 - q, other_ref)):
        for strip in range(src.shape[0]):
            for j in range(4):
                first = 64 + 32 * half + 8 * j
                b_ref[aligned(2 * strip + which, 8), 128 * j : 128 * j + 128] = src[
                    strip, first : first + 8
                ]
    b_ref[win + 80 : win + 88, :] = jnp.zeros((8, b_ref.shape[1]), f32)
    for j in range(4):
        mine = rest_own_ref[4 * half + j]
        theirs = rest_other_ref[4 * half + j]
        lanes = slice(128 * j, 128 * j + 128)
        b_ref[win : win + 42, lanes] = jnp.where(q == 0, mine, theirs)
        b_ref[win + 42 : win + 84, lanes] = jnp.where(q == 0, theirs, mine)


def first_kernel(own_ref, other_ref, rest_own_ref, rest_other_ref, u_ref, w_ref, b_ref, a_ref):
    q = lax.axis_index("row")
    place_top(q, own_ref, other_ref, [a_ref])
    place_lower(q, 0, own_ref, other_ref, rest_own_ref, rest_other_ref, b_ref)
    factor_loop(a_ref, u_ref, w_ref, b_ref)


def second_kernel(
    own_ref, other_ref, own2_ref, other2_ref, rest_own_ref, rest_other_ref, u1_ref, w1_ref, b1_ref,
    top_out, win_out, rest_out, product_out, l_ref, a_ref, u2_ref, w2_ref, b_ref, sum_ref,
):
    q = lax.axis_index("row")
    c = lax.axis_index("col")
    n_win = win_out.shape[0]
    n_rest = rest_out.shape[0]
    place_top(q, own2_ref, other2_ref, [l_ref, a_ref])
    place_lower(q, 1, own_ref, other_ref, rest_own_ref, rest_other_ref, b_ref)
    solve_rows(l_ref, u1_ref, w1_ref)
    a_ref[...] = a_ref[...] - mm(l_ref[...], l_ref[...], NT)

    def beside():
        b_ref[...] = b_ref[...] - mm(b1_ref[...], l_ref[...], NT)
        sum_ref[...] = mm(b1_ref[n_win:, :], b1_ref[:n_win, :], NT)

    factor_loop(a_ref, u2_ref, w2_ref, b_ref, beside)
    product_out[...] = (sum_ref[...] + mm(b_ref[n_win:, :], b_ref[:n_win, :], NT))[:n_rest]
    left = c < 4

    @pl.when(q == 0)
    def _():
        win_out[...] = b1_ref[:n_win, :]

    @pl.when(q == 1)
    def _():
        win_out[...] = b_ref[:n_win, :]

    @pl.when(left)
    def _():
        rest_out[...] = b1_ref[n_win : n_win + n_rest, aligned(c, 128)]

    @pl.when(jnp.logical_not(left))
    def _():
        rest_out[...] = b_ref[n_win : n_win + n_rest, aligned(c - 4, 128)]

    @pl.when(left & (q == 0))
    def _():
        top_out[...] = u1_ref[aligned(c, 128), :].T

    @pl.when(jnp.logical_not(left) & (q == 0))
    def _():
        top_out[...] = jnp.zeros(top_out.shape, f32)

    @pl.when(left & (q == 1))
    def _():
        top_out[...] = l_ref[:, aligned(c, 128)]

    @pl.when(jnp.logical_not(left) & (q == 1))
    def _():
        top_out[...] = u2_ref[aligned(c - 4, 128), :].T


def call(kernel, outs, scratch, micros, limit, *args, **extra):
    shape = lambda s: jax.ShapeDtypeStruct(s, f32)
    return pl.pallas_call(
        kernel,
        out_shape=tuple(shape(s) for s in outs),
        scratch_shapes=[pltpu.VMEM(s, f32) if isinstance(s, tuple) else s for s in scratch],
        compiler_params=pltpu.CompilerParams(vmem_limit_bytes=limit << 20),
        cost_estimate=pl.CostEstimate(
            flops=int(micros * 1e9), transcendentals=0, bytes_accessed=int(micros * 3e6)
        ),
        **extra,
    )(*args)


def swap_rows(value):
    return lax.ppermute(value, "row", [(0, 1), (1, 0)])


def spread(value, axis):
    n = lax.axis_size(axis)
    return lax.all_to_all(jnp.broadcast_to(value, (n,) + value.shape), axis, 0, 0)


def per_device(panel_top, panel_win, panel_rest, trail_rest):
    q = lax.axis_index("row")
    (pieces,) = call(
        pack_kernel, [(32, 90, 128)], [(1344, 128), pltpu.SemaphoreType.DMA((6,))], 2, 4,
        panel_top[0].reshape(32, 16, 128), panel_win[0].reshape(32, 8, HALF), panel_rest[0],
        in_specs=[pl.BlockSpec(memory_space=pltpu.HBM)] * 3,
    )
    parts = lax.all_to_all(pieces, ("layer", "row"), 0, 0)
    sums = jnp.sum(parts.reshape(16, 2, 90, 128), axis=0)
    sums, trail = lax.optimization_barrier((sums, trail_rest[0].reshape(16, 84, 256)))
    strips = spread(sums[:, 32:], "col")
    own = spread(
        jnp.concatenate([strips[:4, 0, :16].reshape(64, 128), sums[:, :32].reshape(64, 128)], axis=0),
        "layer",
    )
    rest = strips[:, :, 16:]
    rest_own = lax.dynamic_index_in_dim(rest, q, 1, False)
    rest_other = swap_rows(lax.dynamic_index_in_dim(rest, 1 - q, 1, False))
    other = swap_rows(own)
    second = strips[:, 1, :16].reshape(128, 128)
    own, other, second = lax.optimization_barrier((own, other, second))
    own2 = spread(second, "layer")
    u1, w1, b1 = call(
        first_kernel, [(HALF, HALF), (4, 128, 128), (344, HALF)], [(HALF, HALF)], 14, 12,
        own, other, rest_own, rest_other,
    )
    own2, u1, trail = lax.optimization_barrier((own2, u1, trail))
    other2 = swap_rows(own2)
    trail_parts = lax.all_to_all(trail, "layer", 0, 0)
    top_block, win_block, rest_block, product = call(
        second_kernel,
        [(HALF, 128), (256, HALF), (84, 128), (84, 256)],
        [(HALF, HALF), (HALF, HALF), (HALF, HALF), (4, 128, 128), (344, HALF), (88, 256)], 20, 16,
        own, other, own2, other2, rest_own, rest_other, u1, w1, b1,
    )
    return top_block, win_block, rest_block, jnp.sum(trail_parts, axis=0) - product


def solution(mesh):
    return jax.shard_map(
        per_device,
        mesh=mesh,
        in_specs=(
            P("layer", "row", "col"),
            P("layer", "col", "row"),
            P("layer", "row", "col"),
            P("layer", "row", "col"),
        ),
        out_specs=(
            P("row", "col"),
            P("col", "row"),
            P(("row", "layer"), "col"),
            P(("row", "layer"), "col"),
        ),
        check_vma=False,
    )
```

time: 142 us -> 142 us (level)
  blocking collectives: 48 us -> 23.4 us
  waiting for transfers between devices: 19.8 us -> 38.4 us
  starting transfers between devices: 23 us -> 29.4 us
    all_to_all x1 -> x0, blocking collectives: 28.6 us -> none  [per_device(): sums = jnp.sum(lax.all_to_all(pieces, 'layer', 0, 0), axis=0)]
    all_to_all x1 -> x2, waiting for transfers between devices: 0.01 us -> 22.3 us  [the longest x1 20.9 us: per_device(): parts = lax.all_to_all(pieces, ('layer', 'row'), 0, 0)]
    all_to_all x1 -> x2, starting transfers between devices: 4.57 us -> 13.9 us  [the longest x1 8.73 us: per_device(): parts = lax.all_to_all(pieces, ('layer', 'row'), 0, 0)]
    all_to_all x1, blocking collectives: 19.4 us -> 23.4 us  [spread(): lax.all_to_all(jnp.broadcast_to(value, (n,) + value.shape), axis, 0, 0)]
    ppermute x3, starting transfers between devices: 6.62 us -> 3.62 us  [swap_rows(): return lax.ppermute(value, 'row', [(0, 1), (1, 0)])]
    all_to_all x2, waiting for transfers between devices: 16.7 us -> 14.3 us  [spread(): lax.all_to_all(jnp.broadcast_to(value, (n,) + value.shape), axis, 0, 0)]
    ppermute x3, waiting for transfers between devices: 3.17 us -> 1.73 us  [swap_rows(): return lax.ppermute(value, 'row', [(0, 1), (1, 0)])]
    unnamed x16 -> x20, local copies, waits for them, and re-layouts: 7.87 us -> 8.92 us
  transfers between devices with their start and end apart: 6 -> 7, of which waited for: 4 -> 5; matrix products, arithmetic and copies ran while one was open for 2% -> 2% of each run, Pallas kernels for 25% -> 23%
where the time goes in v4:
time: 142 us; the launch traced here: 141 us
  waiting for transfers between devices  38.4 us (27%)
  Pallas kernels  34.6 us (24%)
  starting transfers between devices  29.4 us (21%)
  blocking collectives  23.4 us (16%)
  local copies, waits for them, and re-layouts  12.7 us (9%)
  other arithmetic  2.2 us (2%)
    pallas_call x3, Pallas kernels, call(): pl.pallas_call(kernel, out_shape=tuple((shape(s) for s in outs)), scratch...  34.6 us
    all_to_all x1, blocking collectives, spread(): lax.all_to_all(jnp.broadcast_to(value, (n,) + value.shape), axis, 0, 0)  23.4 us
    all_to_all x1, waiting for transfers between devices, per_device(): parts = lax.all_to_all(pieces, ('layer', 'row'), 0, 0)  20.9 us
    all_to_all x2, waiting for transfers between devices, spread(): lax.all_to_all(jnp.broadcast_to(value, (n,) + value.shape), axis, 0, 0)  14.3 us
    all_to_all x2, starting transfers between devices, spread(): lax.all_to_all(jnp.broadcast_to(value, (n,) + value.shape), axis, 0, 0)  11.8 us
    unnamed x20, local copies, waits for them, and re-layouts  8.92 us
    all_to_all x1, starting transfers between devices, per_device(): parts = lax.all_to_all(pieces, ('layer', 'row'), 0, 0)  8.73 us
    all_to_all x1, starting transfers between devices, per_device(): trail_parts = lax.all_to_all(trail, 'layer', 0, 0)  5.18 us
  transfers between devices with their start and end apart: 7, of which 5 were waited for; matrix products, arithmetic and copies ran while one was open for 2% of the time, Pallas kernels for 23%

profile of v4, /device:TPU:1, one launch (start us, length us, event | category | flops | bytes accessed | tf_op | source)
XLA Modules:
  0.0 141.5 jit_solution(9720145304330244473)
XLA Ops:
  0.6 0.0 copy-start
  0.6 1.1 copy-done
  1.7 0.0 copy-start.1
  1.7 1.0 copy-done.1
  2.8 0.0 copy-start.2
  2.8 0.9 copy-done.2
  3.7 1.6 %shard_map.75 = f32[32,90,128]{2,1,0:T(8,128)} custom-call(f32[32,16,128]{2,1,0:T(8,128)S(1)} %bitcast.19, f32[32,8,512]{2,1,0:T(8,128)S(1)} %bitcast.18, f32[1344,128]{1,0:T(8,128)S(1)} %bitcast.17), custom_call_target="tpu_custom_call" | custom-call | flops 2000000000 | bytes 6000000 | tf_op jit(solution)/shard_map/pallas_call | solution.py:228
  5.3 0.0 copy-start.9
  5.3 8.7 %all-to-all-start = ((f32[32,90,128]{2,1,0:T(8,128)}), f32[32,90,128]{2,1,0:T(8,128)S(1)}, u32[]{:S(2)}, u32[]{:S(2)}) async-start(f32[32,90,128]{2,1,0:T(8,128)} %shard_map.75), calls=%async_computation | async-start | bytes 3145728 | tf_op jit(solution)/shard_map/all_to_all | solution.py:256
  14.1 0.0 copy-done.9
  14.1 1.2 reshape_squeeze.17
  15.3 20.9 %all-to-all-done = f32[32,90,128]{2,1,0:T(8,128)S(1)} async-done(((f32[32,90,128]{2,1,0:T(8,128)}), f32[32,90,128]{2,1,0:T(8,128)S(1)}, u32[]{:S(2)}, u32[]{:S(2)}) %all-to-all-start) | async-done | bytes 1474592 | tf_op jit(solution)/shard_map/all_to_all | solution.py:256
  36.3 0.1 reduce_sum.18
  36.4 0.9 broadcast_in_dim.9
  37.3 8.2 %all-to-all-start.1 = ((f32[8,2,58,128]{3,1,2,0:T(2,128)}), f32[8,2,58,128]{3,1,2,0:T(2,128)S(1)}, u32[]{:S(2)}, u32[]{:S(2)}) async-start(f32[8,2,58,128]{3,1,2,0:T(2,128)} %broadcast_in_dim.9), calls=%async_computation.1 | async-start | bytes 950272 | tf_op jit(solution)/shard_map/all_to_all | solution.py:246
  45.5 13.9 %all-to-all-done.1 = f32[8,2,58,128]{3,1,2,0:T(2,128)S(1)} async-done(((f32[8,2,58,128]{3,1,2,0:T(2,128)}), f32[8,2,58,128]{3,1,2,0:T(2,128)S(1)}, u32[]{:S(2)}, u32[]{:S(2)}) %all-to-all-start.1) | async-done | bytes 475168 | tf_op jit(solution)/shard_map/all_to_all | solution.py:246
  59.5 0.1 broadcast_in_dim.10
  59.6 23.4 %all_to_all.25.own_ref = f32[16,128,128]{2,1,0:T(8,128)S(1)} all-to-all(f32[16,128,128]{2,1,0:T(8,128)S(1)} %broadcast_in_dim.10), channel_id=1, replica_groups=mesh['row'=2,'col'=8,'layer'=16] {'layer'}, dimensions={0} | all-to-all | bytes 2097152 | tf_op jit(solution)/shard_map/all_to_all | solution.py:246
  82.9 1.8 %collective-permute-start = (f32[16,128,128]{2,1,0:T(8,128)S(1)}, f32[16,128,128]{2,1,0:T(8,128)S(1)}, u32[]{:S(2)}, u32[]{:S(2)}) collective-permute-start(f32[16,128,128]{2,1,0:T(8,128)S(1)} %all_to_all.25.own_ref), channel_id=1, source_target_pairs={{0,128},{128,0},{1,129},{129,1},{2,130},{130,2},{3,131},{131,3},{4... | collective-permute-start | bytes 3145736 | tf_op jit(solution)/shard_map/ppermute | solution.py:241
  84.8 0.3 constant_dynamic-slice_fusion
  85.1 0.1 collective-permute-start.1
  85.2 0.1 slice.21
  85.3 1.7 %collective-permute-done.other_ref = f32[16,128,128]{2,1,0:T(8,128)S(1)} collective-permute-done((f32[16,128,128]{2,1,0:T(8,128)S(1)}, f32[16,128,128]{2,1,0:T(8,128)S(1)}, u32[]{:S(2)}, u32[]{:S(2)}) %collective-permute-start) | collective-permute-done | bytes 1048608 | tf_op jit(solution)/shard_map/ppermute | solution.py:241
  87.0 1.1 broadcast_in_dim.11
  88.1 3.7 %all-to-all-start.3 = ((f32[16,128,128]{2,1,0:T(8,128)}), f32[16,128,128]{2,1,0:T(8,128)S(1)}, u32[]{:S(2)}, u32[]{:S(2)}) async-start(f32[16,128,128]{2,1,0:T(8,128)} %broadcast_in_dim.11), calls=%async_computation.3 | async-start | bytes 2097152 | tf_op jit(solution)/shard_map/all_to_all | solution.py:246
  91.8 0.0 collective-permute-done.1.rest_other_ref
  91.8 14.0 %shard_map.76 = (f32[512,512]{1,0:T(8,128)S(1)}, f32[4,128,128]{2,1,0:T(8,128)S(1)}, f32[344,512]{1,0:T(8,128)S(1)}) custom-call(f32[16,128,128]{2,1,0:T(8,128)S(1)} %all_to_all.25.own_ref, f32[16,128,128]{2,1,0:T(8,128)S(1)} %collective-permute-done.other_ref, f32[8,42,128]{2,1,0:T(8,128)S(1)} %bitcast.15, f32[8,42,128]{2,1,0:T(8,128)} %collective-permute-done.1.rest_other_ref), custom_call_target="tpu_custom_call" | custom-call | flops 14000000000 | bytes 42000000 | tf_op jit(solution)/shard_map/pallas_call | solution.py:228
  105.8 0.0 copy-start.3
  105.9 1.0 copy-done.3
  106.8 0.0 copy-start.5
  106.8 0.9 copy-done.5
  107.7 0.0 copy-start.7
  107.7 0.7 copy-done.7
  108.4 0.4 all-to-all-done.3.own2_ref
  108.8 1.7 %collective-permute-start.2 = (f32[16,128,128]{2,1,0:T(8,128)S(1)}, f32[16,128,128]{2,1,0:T(8,128)}, u32[]{:S(2)}, u32[]{:S(2)}) collective-permute-start(f32[16,128,128]{2,1,0:T(8,128)S(1)} %all-to-all-done.3.own2_ref), channel_id=1, source_target_pairs={{0,128},{128,0},{1,129},{129,1},{2,130},{130,2},{3,131},{131,3},{4... | collective-permute-start | bytes 3145736 | tf_op jit(solution)/shard_map/ppermute | solution.py:241
  110.5 5.2 %all-to-all-start.4 = ((f32[16,84,256]{2,1,0:T(8,128)}), f32[16,84,256]{2,1,0:T(8,128)}, u32[]{:S(2)}, u32[]{:S(2)}) async-start(f32[16,84,256]{2,1,0:T(8,128)} %reshape_squeeze.17), calls=%async_computation.4 | async-start | bytes 2883584 | tf_op jit(solution)/shard_map/all_to_all | solution.py:277
  115.7 0.0 collective-permute-done.2.other2_ref
  115.7 0.0 copy-start.4
  115.7 1.2 copy-done.4
  117.0 0.0 copy-start.6
  117.0 1.1 copy-done.6
  118.1 0.0 copy-start.8
  118.1 0.9 copy-done.8
  119.0 18.9 %shard_map.77 = (f32[512,128]{1,0:T(8,128)}, f32[256,512]{1,0:T(8,128)}, f32[84,128]{1,0:T(8,128)}, f32[84,256]{1,0:T(8,128)S(1)}) custom-call(f32[16,128,128]{2,1,0:T(8,128)S(1)} %all_to_all.25.own_ref, f32[16,128,128]{2,1,0:T(8,128)S(1)} %collective-permute-done.other_ref, f32[16,128,128]{2,1,0:T(8,128)S(1)} %all-to-all-done.3.own2_ref, ...), custom_call_target="tpu_custom_call" | custom-call | flops 20000000000 | bytes 60000000 | tf_op jit(solution)/shard_map/pallas_call | solution.py:228
  137.9 1.4 all-to-all-done.4
  139.4 1.5 %reduce_sum.19 = f32[84,256]{1,0:T(8,128)S(1)} reduce(f32[16,84,256]{2,1,0:T(8,128)} %all-to-all-done.4, f32[]{:T(128)} %constant.13.clone.1), dimensions={0}, to_apply=%region_1.2 | reduce | flops 322560 | bytes 1462276 | tf_op jit(solution)/shard_map/reduce_sum | solution.py:284
  140.8 0.7 sub.7
  (8 shorter events, 0.1 us)
Async XLA Ops:
  0.6 1.1 copy-start
  1.7 1.0 copy-start.1
  2.8 0.9 copy-start.2
  5.3 8.8 %copy-start.9 = (f32[1,1344,256]{2,1,0:T(8,128)S(1)}, f32[1,1344,256]{2,1,0:T(8,128)}, u32[]{:S(2)}) copy-start(f32[1,1344,256]{2,1,0:T(8,128)} %param.7) | copy-start | bytes 4128772
  5.3 30.9 %all-to-all-start = ((f32[32,90,128]{2,1,0:T(8,128)}), f32[32,90,128]{2,1,0:T(8,128)S(1)}, u32[]{:S(2)}, u32[]{:S(2)}) async-start(f32[32,90,128]{2,1,0:T(8,128)} %shard_map.75), calls=%async_computation | async-start | bytes 3145728 | tf_op jit(solution)/shard_map/all_to_all | solution.py:256
  37.3 22.1 %all-to-all-start.1 = ((f32[8,2,58,128]{3,1,2,0:T(2,128)}), f32[8,2,58,128]{3,1,2,0:T(2,128)S(1)}, u32[]{:S(2)}, u32[]{:S(2)}) async-start(f32[8,2,58,128]{3,1,2,0:T(2,128)} %broadcast_in_dim.9), calls=%async_computation.1 | async-start | bytes 950272 | tf_op jit(solution)/shard_map/all_to_all | solution.py:246
  82.9 4.1 %collective-permute-start = (f32[16,128,128]{2,1,0:T(8,128)S(1)}, f32[16,128,128]{2,1,0:T(8,128)S(1)}, u32[]{:S(2)}, u32[]{:S(2)}) collective-permute-start(f32[16,128,128]{2,1,0:T(8,128)S(1)} %all_to_all.25.own_ref), channel_id=1, source_target_pairs={{0,128},{128,0},{1,129},{129,1},{2,130},{130,2},{3,131},{131,3},{4... | collective-permute-start | bytes 3145736 | tf_op jit(solution)/shard_map/ppermute | solution.py:241
  85.1 6.7 %collective-permute-start.1 = (f32[8,42,128]{2,1,0:T(8,128)S(1)}, f32[8,42,128]{2,1,0:T(8,128)}, u32[]{:S(2)}, u32[]{:S(2)}) collective-permute-start(f32[8,42,128]{2,1,0:T(8,128)S(1)} %bitcast.22), channel_id=1, source_target_pairs={{0,128},{128,0},{1,129},{129,1},{2,130},{130,2},{3,131},{131,3},{4... | collective-permute-start | bytes 516104 | tf_op jit(solution)/shard_map/ppermute | solution.py:241
  88.1 20.7 %all-to-all-start.3 = ((f32[16,128,128]{2,1,0:T(8,128)}), f32[16,128,128]{2,1,0:T(8,128)S(1)}, u32[]{:S(2)}, u32[]{:S(2)}) async-start(f32[16,128,128]{2,1,0:T(8,128)} %broadcast_in_dim.11), calls=%async_computation.3 | async-start | bytes 2097152 | tf_op jit(solution)/shard_map/all_to_all | solution.py:246
  105.8 1.0 copy-start.3
  106.8 0.9 copy-start.5
  107.7 0.7 copy-start.7
  108.8 6.9 %collective-permute-start.2 = (f32[16,128,128]{2,1,0:T(8,128)S(1)}, f32[16,128,128]{2,1,0:T(8,128)}, u32[]{:S(2)}, u32[]{:S(2)}) collective-permute-start(f32[16,128,128]{2,1,0:T(8,128)S(1)} %all-to-all-done.3.own2_ref), channel_id=1, source_target_pairs={{0,128},{128,0},{1,129},{129,1},{2,130},{130,2},{3,131},{131,3},{4... | collective-permute-start | bytes 3145736 | tf_op jit(solution)/shard_map/ppermute | solution.py:241
  110.5 28.8 %all-to-all-start.4 = ((f32[16,84,256]{2,1,0:T(8,128)}), f32[16,84,256]{2,1,0:T(8,128)}, u32[]{:S(2)}, u32[]{:S(2)}) async-start(f32[16,84,256]{2,1,0:T(8,128)} %reshape_squeeze.17), calls=%async_computation.4 | async-start | bytes 2883584 | tf_op jit(solution)/shard_map/all_to_all | solution.py:277
  115.7 1.2 copy-start.4
  117.0 1.1 copy-start.6
  118.1 0.9 copy-start.8

commit v5 on v4

--- a/solution.py
+++ b/solution.py
@@ -162,23 +162,42 @@
         b_ref[win + 42 : win + 84, lanes] = jnp.where(q == 0, theirs, mine)
 
 
-def first_kernel(own_ref, other_ref, rest_own_ref, rest_other_ref, u_ref, w_ref, b_ref, a_ref):
+def start_all(sources, targets, sems):
+    copies = [
+        pltpu.make_async_copy(source, target, sems.at[n])
+        for n, (source, target) in enumerate(zip(sources, targets))
+    ]
+    for copy in copies:
+        copy.start()
+    return copies
+
+
+def first_kernel(
+    own_ref, other_ref, rest_own_ref, rest_other_ref, u_out, w_out, b_out,
+    u_ref, w_ref, b_ref, a_ref, sems,
+):
     q = lax.axis_index("row")
     place_top(q, own_ref, other_ref, [a_ref])
     place_lower(q, 0, own_ref, other_ref, rest_own_ref, rest_other_ref, b_ref)
     factor_loop(a_ref, u_ref, w_ref, b_ref)
+    for copy in start_all((u_ref, w_ref, b_ref), (u_out, w_out, b_out), sems):
+        copy.wait()
 
 
 def second_kernel(
-    own_ref, other_ref, own2_ref, other2_ref, rest_own_ref, rest_other_ref, u1_ref, w1_ref, b1_ref,
-    top_out, win_out, rest_out, product_out, l_ref, a_ref, u2_ref, w2_ref, b_ref, sum_ref,
+    own_ref, other_ref, own2_ref, other2_ref, rest_own_ref, rest_other_ref, u1_in, w1_in, b1_in,
+    top_out, win_out, rest_out, product_out, u1_ref, w1_ref, b1_ref, l_ref, a_ref, u2_ref, w2_ref,
+    b_ref, sum_ref, sems,
 ):
+    copies = start_all((u1_in, w1_in, b1_in), (u1_ref, w1_ref, b1_ref), sems)
     q = lax.axis_index("row")
     c = lax.axis_index("col")
     n_win = win_out.shape[0]
     n_rest = rest_out.shape[0]
     place_top(q, own2_ref, other2_ref, [l_ref, a_ref])
     place_lower(q, 1, own_ref, other_ref, rest_own_ref, rest_other_ref, b_ref)
+    for copy in copies:
+        copy.wait()
     solve_rows(l_ref, u1_ref, w1_ref)
     a_ref[...] = a_ref[...] - mm(l_ref[...], l_ref[...], NT)
 
@@ -224,7 +243,7 @@
 
 
 def call(kernel, outs, scratch, micros, limit, *args, **extra):
-    shape = lambda s: jax.ShapeDtypeStruct(s, f32)
+    shape = lambda s: jax.ShapeDtypeStruct(s, f32) if isinstance(s, tuple) else s
     return pl.pallas_call(
         kernel,
         out_shape=tuple(shape(s) for s in outs),
@@ -250,7 +269,12 @@
     q = lax.axis_index("row")
     (pieces,) = call(
         pack_kernel, [(32, 90, 128)], [(1344, 128), pltpu.SemaphoreType.DMA((6,))], 2, 4,
-        panel_top[0].reshape(32, 16, 128), panel_win[0].reshape(32, 8, HALF), panel_rest[0],
+        *(
+            pltpu.with_memory_space_constraint(x, pltpu.HBM)
+            for x in (
+                panel_top[0].reshape(32, 16, 128), panel_win[0].reshape(32, 8, HALF), panel_rest[0]
+            )
+        ),
         in_specs=[pl.BlockSpec(memory_space=pltpu.HBM)] * 3,
     )
     parts = lax.all_to_all(pieces, ("layer", "row"), 0, 0)
@@ -265,23 +289,34 @@
     rest_own = lax.dynamic_index_in_dim(rest, q, 1, False)
     rest_other = swap_rows(lax.dynamic_index_in_dim(rest, 1 - q, 1, False))
     other = swap_rows(own)
-    second = strips[:, 1, :16].reshape(128, 128)
+    second = jnp.broadcast_to(strips[:, 1, :16].reshape(128, 128), (16, 128, 128))
     own, other, second = lax.optimization_barrier((own, other, second))
-    own2 = spread(second, "layer")
+    own2 = lax.all_to_all(second, "layer", 0, 0)
+    carried = [(HALF, HALF), (4, 128, 128), (344, HALF)]
     u1, w1, b1 = call(
-        first_kernel, [(HALF, HALF), (4, 128, 128), (344, HALF)], [(HALF, HALF)], 14, 12,
-        own, other, rest_own, rest_other,
-    )
-    own2, u1, trail = lax.optimization_barrier((own2, u1, trail))
+        first_kernel, [pltpu.HBM(x, f32) for x in carried],
+        carried + [(HALF, HALF), pltpu.SemaphoreType.DMA((3,))], 14, 12,
+        own, other, rest_own, rest_other, out_specs=(pl.BlockSpec(memory_space=pltpu.HBM),) * 3,
+    )
+    u1, w1, b1 = (pltpu.with_memory_space_constraint(x, pltpu.HBM) for x in (u1, w1, b1))
+    own2, w1, trail = lax.optimization_barrier((own2, w1, trail))
     other2 = swap_rows(own2)
     trail_parts = lax.all_to_all(trail, "layer", 0, 0)
     top_block, win_block, rest_block, product = call(
         second_kernel,
         [(HALF, 128), (256, HALF), (84, 128), (84, 256)],
-        [(HALF, HALF), (HALF, HALF), (HALF, HALF), (4, 128, 128), (344, HALF), (88, 256)], 20, 16,
+        carried
+        + [(HALF, HALF), (HALF, HALF), (HALF, HALF), (4, 128, 128), (344, HALF), (88, 256)]
+        + [pltpu.SemaphoreType.DMA((3,))],
+        20, 20,
         own, other, own2, other2, rest_own, rest_other, u1, w1, b1,
-    )
-    return top_block, win_block, rest_block, jnp.sum(trail_parts, axis=0) - product
+        in_specs=[pl.BlockSpec(memory_space=pltpu.VMEM)] * 6
+        + [pl.BlockSpec(memory_space=pltpu.HBM)] * 3,
+    )
+    schur = trail_parts[0] - product
+    for part in range(1, 16):
+        schur = schur + trail_parts[part]
+    return top_block, win_block, rest_block, schur
 
 
 def solution(mesh):

time: 142 us -> 141 us (level)
  local copies, waits for them, and re-layouts: 12.7 us -> 3.87 us
  waiting for transfers between devices: 38.4 us -> 43 us
  Pallas kernels: 34.6 us -> 37.9 us
    unnamed x20 -> x2, local copies, waits for them, and re-layouts: 8.92 us -> 0.01 us
    all_to_all x0 -> x1, starting transfers between devices: none -> 3.65 us  [per_device(): own2 = lax.all_to_all(second, 'layer', 0, 0)]
    all_to_all x2 -> x1, starting transfers between devices: 11.8 us -> 8.19 us  [spread(): lax.all_to_all(jnp.broadcast_to(value, (n,) + value.shape), axis, 0, 0)]
    pallas_call x3, Pallas kernels: 34.6 us -> 37.9 us  [call(): pl.pallas_call(kernel, out_shape=tuple((shape(s) for s in outs)), scratch...]
    all_to_all x1, waiting for transfers between devices: 1.41 us -> 4.38 us  [per_device(): trail_parts = lax.all_to_all(trail, 'layer', 0, 0)]
    add x0 -> x1, other arithmetic: none -> 2.14 us  [per_device(): schur = schur + trail_parts[part]]
    all_to_all x0 -> x1, waiting for transfers between devices: none -> 2.09 us  [per_device(): own2 = lax.all_to_all(second, 'layer', 0, 0)]
    reduce_sum x1 -> x0, other arithmetic: 1.46 us -> none  [per_device(): jnp.sum(trail_parts, axis=0) - product]
  transfers between devices with their start and end apart: 7 -> 7, of which waited for: 5 -> 5; matrix products, arithmetic and copies ran while one was open for 2% -> 2% of each run, Pallas kernels for 23% -> 25%
where the time goes in v5:
time: 141 us; the launch traced here: 140 us
  waiting for transfers between devices  43 us (30%)
  Pallas kernels  37.9 us (27%)
  starting transfers between devices  28.8 us (20%)
  blocking collectives  23.4 us (17%)
  local copies, waits for them, and re-layouts  3.87 us (3%)
  other arithmetic  2.23 us (2%)
    pallas_call x3, Pallas kernels, call(): pl.pallas_call(kernel, out_shape=tuple((shape(s) for s in outs)), scratch...  37.9 us
    all_to_all x1, blocking collectives, spread(): lax.all_to_all(jnp.broadcast_to(value, (n,) + value.shape), axis, 0, 0)  23.4 us
    all_to_all x1, waiting for transfers between devices, per_device(): parts = lax.all_to_all(pieces, ('layer', 'row'), 0, 0)  20.9 us
    all_to_all x1, waiting for transfers between devices, spread(): lax.all_to_all(jnp.broadcast_to(value, (n,) + value.shape), axis, 0, 0)  13.9 us
    all_to_all x1, starting transfers between devices, per_device(): parts = lax.all_to_all(pieces, ('layer', 'row'), 0, 0)  8.73 us
    all_to_all x1, starting transfers between devices, spread(): lax.all_to_all(jnp.broadcast_to(value, (n,) + value.shape), axis, 0, 0)  8.19 us
    all_to_all x1, starting transfers between devices, per_device(): trail_parts = lax.all_to_all(trail, 'layer', 0, 0)  4.57 us
    all_to_all x1, waiting for transfers between devices, per_device(): trail_parts = lax.all_to_all(trail, 'layer', 0, 0)  4.38 us
  transfers between devices with their start and end apart: 7, of which 5 were waited for; matrix products, arithmetic and copies ran while one was open for 2% of the time, Pallas kernels for 25%

profile of v5, /device:TPU:1, one launch (start us, length us, event | category | flops | bytes accessed | tf_op | source)
XLA Modules:
  0.0 140.0 jit_solution(4922825759112567029)
XLA Ops:
  0.6 2.6 %shard_map.75 = f32[32,90,128]{2,1,0:T(8,128)} custom-call(f32[32,16,128]{2,1,0:T(8,128)} %bitcast.118, f32[32,8,512]{2,1,0:T(8,128)} %bitcast.117, f32[1344,128]{1,0:T(8,128)} %bitcast.116), custom_call_target="tpu_custom_call" | custom-call | flops 2000000000 | bytes 6000000 | tf_op jit(solution)/shard_map/pallas_call | solution.py:247
  3.2 0.0 copy-start
  3.2 8.7 %all-to-all-start = ((f32[32,90,128]{2,1,0:T(8,128)}), f32[32,90,128]{2,1,0:T(8,128)S(1)}, u32[]{:S(2)}, u32[]{:S(2)}) async-start(f32[32,90,128]{2,1,0:T(8,128)} %shard_map.75), calls=%async_computation | async-start | bytes 3145728 | tf_op jit(solution)/shard_map/all_to_all | solution.py:280
  12.0 0.0 copy-done
  12.0 1.3 reshape_squeeze.17
  13.2 20.9 %all-to-all-done = f32[32,90,128]{2,1,0:T(8,128)S(1)} async-done(((f32[32,90,128]{2,1,0:T(8,128)}), f32[32,90,128]{2,1,0:T(8,128)S(1)}, u32[]{:S(2)}, u32[]{:S(2)}) %all-to-all-start) | async-done | bytes 1474592 | tf_op jit(solution)/shard_map/all_to_all | solution.py:280
  34.1 0.1 reduce_sum.9
  34.3 0.9 broadcast_in_dim.9
  35.2 8.2 %all-to-all-start.1 = ((f32[8,2,58,128]{3,1,2,0:T(2,128)}), f32[8,2,58,128]{3,1,2,0:T(2,128)S(1)}, u32[]{:S(2)}, u32[]{:S(2)}) async-start(f32[8,2,58,128]{3,1,2,0:T(2,128)} %broadcast_in_dim.9), calls=%async_computation.1 | async-start | bytes 950272 | tf_op jit(solution)/shard_map/all_to_all | solution.py:265
  43.4 13.9 %all-to-all-done.1 = f32[8,2,58,128]{3,1,2,0:T(2,128)S(1)} async-done(((f32[8,2,58,128]{3,1,2,0:T(2,128)}), f32[8,2,58,128]{3,1,2,0:T(2,128)S(1)}, u32[]{:S(2)}, u32[]{:S(2)}) %all-to-all-start.1) | async-done | bytes 475168 | tf_op jit(solution)/shard_map/all_to_all | solution.py:265
  57.3 0.1 broadcast_in_dim.10
  57.4 23.4 %all_to_all.25.own_ref = f32[16,128,128]{2,1,0:T(8,128)S(1)} all-to-all(f32[16,128,128]{2,1,0:T(8,128)S(1)} %broadcast_in_dim.10), channel_id=1, replica_groups=mesh['row'=2,'col'=8,'layer'=16] {'layer'}, dimensions={0} | all-to-all | bytes 2097152 | tf_op jit(solution)/shard_map/all_to_all | solution.py:265
  80.8 1.8 %collective-permute-start = (f32[16,128,128]{2,1,0:T(8,128)S(1)}, f32[16,128,128]{2,1,0:T(8,128)S(1)}, u32[]{:S(2)}, u32[]{:S(2)}) collective-permute-start(f32[16,128,128]{2,1,0:T(8,128)S(1)} %all_to_all.25.own_ref), channel_id=1, source_target_pairs={{0,128},{128,0},{1,129},{129,1},{2,130},{130,2},{3,131},{131,3},{4... | collective-permute-start | bytes 3145736 | tf_op jit(solution)/shard_map/ppermute | solution.py:260
  82.7 0.3 constant_dynamic-slice_fusion
  83.0 0.1 collective-permute-start.1
  83.1 0.1 slice.85
  83.2 1.7 %collective-permute-done.other_ref = f32[16,128,128]{2,1,0:T(8,128)S(1)} collective-permute-done((f32[16,128,128]{2,1,0:T(8,128)S(1)}, f32[16,128,128]{2,1,0:T(8,128)S(1)}, u32[]{:S(2)}, u32[]{:S(2)}) %collective-permute-start) | collective-permute-done | bytes 1048608 | tf_op jit(solution)/shard_map/ppermute | solution.py:260
  84.9 1.1 broadcast_in_dim.11
  86.0 3.7 %all-to-all-start.3 = ((f32[16,128,128]{2,1,0:T(8,128)}), f32[16,128,128]{2,1,0:T(8,128)S(1)}, u32[]{:S(2)}, u32[]{:S(2)}) async-start(f32[16,128,128]{2,1,0:T(8,128)} %broadcast_in_dim.11), calls=%async_computation.3 | async-start | bytes 2097152 | tf_op jit(solution)/shard_map/all_to_all | solution.py:294
  89.7 0.0 collective-permute-done.1.rest_other_ref
  89.7 14.9 %shard_map.76 = (f32[512,512]{1,0:T(8,128)}, f32[4,128,128]{2,1,0:T(8,128)}, f32[344,512]{1,0:T(8,128)}) custom-call(f32[16,128,128]{2,1,0:T(8,128)S(1)} %all_to_all.25.own_ref, f32[16,128,128]{2,1,0:T(8,128)S(1)} %collective-permute-done.other_ref, f32[8,42,128]{2,1,0:T(8,128)S(1)} %bitcast.109, f32[8,42,128]{2,1,0:T(8,128)} %collective-permute-done.1.rest_other_ref), custom_call_target="tpu_custom_call" | custom-call | flops 14000000000 | bytes 42000000 | tf_op jit(solution)/shard_map/pallas_call | solution.py:247
  104.6 2.1 %all-to-all-done.3.own2_ref = f32[16,128,128]{2,1,0:T(8,128)S(1)} async-done(((f32[16,128,128]{2,1,0:T(8,128)}), f32[16,128,128]{2,1,0:T(8,128)S(1)}, u32[]{:S(2)}, u32[]{:S(2)}) %all-to-all-start.3) | async-done | bytes 1048608 | tf_op jit(solution)/shard_map/all_to_all | solution.py:294
  106.7 1.7 %collective-permute-start.2 = (f32[16,128,128]{2,1,0:T(8,128)S(1)}, f32[16,128,128]{2,1,0:T(8,128)}, u32[]{:S(2)}, u32[]{:S(2)}) collective-permute-start(f32[16,128,128]{2,1,0:T(8,128)S(1)} %all-to-all-done.3.own2_ref), channel_id=1, source_target_pairs={{0,128},{128,0},{1,129},{129,1},{2,130},{130,2},{3,131},{131,3},{4... | collective-permute-start | bytes 3145736 | tf_op jit(solution)/shard_map/ppermute | solution.py:260
  108.4 4.6 %all-to-all-start.4 = ((f32[16,84,256]{2,1,0:T(8,128)}), f32[16,84,256]{2,1,0:T(8,128)}, u32[]{:S(2)}, u32[]{:S(2)}) async-start(f32[16,84,256]{2,1,0:T(8,128)} %reshape_squeeze.17), calls=%async_computation.4 | async-start | bytes 2883584 | tf_op jit(solution)/shard_map/all_to_all | solution.py:304
  113.0 0.0 collective-permute-done.2.other2_ref
  113.0 20.4 %shard_map.77 = (f32[512,128]{1,0:T(8,128)}, f32[256,512]{1,0:T(8,128)}, f32[84,128]{1,0:T(8,128)}, f32[84,256]{1,0:T(8,128)S(1)}) custom-call(f32[16,128,128]{2,1,0:T(8,128)S(1)} %all_to_all.25.own_ref, f32[16,128,128]{2,1,0:T(8,128)S(1)} %collective-permute-done.other_ref, f32[16,128,128]{2,1,0:T(8,128)S(1)} %all-to-all-done.3.own2_ref, ...), custom_call_target="tpu_custom_call" | custom-call | flops 20000000000 | bytes 60000000 | tf_op jit(solution)/shard_map/pallas_call | solution.py:247
  133.5 4.4 %all-to-all-done.4 = f32[16,84,256]{2,1,0:T(8,128)} async-done(((f32[16,84,256]{2,1,0:T(8,128)}), f32[16,84,256]{2,1,0:T(8,128)}, u32[]{:S(2)}, u32[]{:S(2)}) %all-to-all-start.4) | async-done | bytes 1376288 | tf_op jit(solution)/shard_map/all_to_all | solution.py:304
  137.8 2.1 %fusion = f32[84,256]{1,0:T(8,128)} fusion(f32[16,84,256]{2,1,0:T(8,128)} %all-to-all-done.4, f32[84,256]{1,0:T(8,128)S(1)} %get-tuple-element.33), kind=kLoop, calls=%fused_computation.3 | loop fusion | flops 344064 | bytes 1548288 | tf_op jit(solution)/shard_map/add | solution.py:318
  (8 shorter events, 0.1 us)
Async XLA Ops:
  3.2 8.8 %copy-start = (f32[1,1344,256]{2,1,0:T(8,128)S(1)}, f32[1,1344,256]{2,1,0:T(8,128)}, u32[]{:S(2)}) copy-start(f32[1,1344,256]{2,1,0:T(8,128)} %param.7) | copy-start | bytes 4128772
  3.2 30.9 %all-to-all-start = ((f32[32,90,128]{2,1,0:T(8,128)}), f32[32,90,128]{2,1,0:T(8,128)S(1)}, u32[]{:S(2)}, u32[]{:S(2)}) async-start(f32[32,90,128]{2,1,0:T(8,128)} %shard_map.75), calls=%async_computation | async-start | bytes 3145728 | tf_op jit(solution)/shard_map/all_to_all | solution.py:280
  35.2 22.1 %all-to-all-start.1 = ((f32[8,2,58,128]{3,1,2,0:T(2,128)}), f32[8,2,58,128]{3,1,2,0:T(2,128)S(1)}, u32[]{:S(2)}, u32[]{:S(2)}) async-start(f32[8,2,58,128]{3,1,2,0:T(2,128)} %broadcast_in_dim.9), calls=%async_computation.1 | async-start | bytes 950272 | tf_op jit(solution)/shard_map/all_to_all | solution.py:265
  80.8 4.1 %collective-permute-start = (f32[16,128,128]{2,1,0:T(8,128)S(1)}, f32[16,128,128]{2,1,0:T(8,128)S(1)}, u32[]{:S(2)}, u32[]{:S(2)}) collective-permute-start(f32[16,128,128]{2,1,0:T(8,128)S(1)} %all_to_all.25.own_ref), channel_id=1, source_target_pairs={{0,128},{128,0},{1,129},{129,1},{2,130},{130,2},{3,131},{131,3},{4... | collective-permute-start | bytes 3145736 | tf_op jit(solution)/shard_map/ppermute | solution.py:260
  83.0 6.7 %collective-permute-start.1 = (f32[8,42,128]{2,1,0:T(8,128)S(1)}, f32[8,42,128]{2,1,0:T(8,128)}, u32[]{:S(2)}, u32[]{:S(2)}) collective-permute-start(f32[8,42,128]{2,1,0:T(8,128)S(1)} %bitcast.113), channel_id=1, source_target_pairs={{0,128},{128,0},{1,129},{129,1},{2,130},{130,2},{3,131},{131,3},{4... | collective-permute-start | bytes 516104 | tf_op jit(solution)/shard_map/ppermute | solution.py:260
  86.0 20.7 %all-to-all-start.3 = ((f32[16,128,128]{2,1,0:T(8,128)}), f32[16,128,128]{2,1,0:T(8,128)S(1)}, u32[]{:S(2)}, u32[]{:S(2)}) async-start(f32[16,128,128]{2,1,0:T(8,128)} %broadcast_in_dim.11), calls=%async_computation.3 | async-start | bytes 2097152 | tf_op jit(solution)/shard_map/all_to_all | solution.py:294
  106.7 6.3 %collective-permute-start.2 = (f32[16,128,128]{2,1,0:T(8,128)S(1)}, f32[16,128,128]{2,1,0:T(8,128)}, u32[]{:S(2)}, u32[]{:S(2)}) collective-permute-start(f32[16,128,128]{2,1,0:T(8,128)S(1)} %all-to-all-done.3.own2_ref), channel_id=1, source_target_pairs={{0,128},{128,0},{1,129},{129,1},{2,130},{130,2},{3,131},{131,3},{4... | collective-permute-start | bytes 3145736 | tf_op jit(solution)/shard_map/ppermute | solution.py:260
  108.4 29.4 %all-to-all-start.4 = ((f32[16,84,256]{2,1,0:T(8,128)}), f32[16,84,256]{2,1,0:T(8,128)}, u32[]{:S(2)}, u32[]{:S(2)}) async-start(f32[16,84,256]{2,1,0:T(8,128)} %reshape_squeeze.17), calls=%async_computation.4 | async-start | bytes 2883584 | tf_op jit(solution)/shard_map/all_to_all | solution.py:304

commit v6 on v5

--- a/solution.py
+++ b/solution.py
@@ -40,11 +40,12 @@
             scale = 1.0 / pivot
             pivots[k] = jnp.where(here, pivot, pivots[k])
             rows[k] = jnp.where(here, P[k], rows[k])
+            others = [jnp.where(here, 0.0, cols[m][i]) if i == k else cols[m][i] for i in range(2)]
             for j in range(m + 1, 16):
                 f = wide(cols[j][k][s : s + 1]) * scale
                 for i in range(2):
-                    x = cols[j][i] - cols[m][i] * f
-                    cols[j][i] = jnp.where(here, f, x) if i == k else x
+                    x = jnp.where(here, f, cols[j][i]) if i == k else cols[j][i]
+                    cols[j][i] = x - others[i] * f
             f = wide(P[k][s : s + 1]) * scale
             for i in range(2):
                 x = P[i] - cols[m][i] * f
@@ -52,8 +53,11 @@
         V = [wide(P[m // 8][m % 8 : m % 8 + 1]) for m in range(16)]
         for g in range(2 * t + 2, min(16, 2 * t + 4)):
             x = jnp.where(inside, 0.0, S[g])
-            for m in range(16):
-                x = x - wide(S[g][:, o + m : o + m + 1]) * V[m]
+            parts = [wide(S[g][:, o + m : o + m + 1]) * V[m] for m in range(16)]
+            while len(parts) > 4:
+                parts = [u + v for u, v in zip(parts[::2], parts[1::2])]
+            for part in parts:
+                x = x - part
             S[g] = x
         far = range(2 * t + 4, 16)
         if far:
@@ -130,7 +134,15 @@
     for copy in copies[::-1]:
         copy.wait()
     for piece in range(out_ref.shape[0]):
+        out_ref[piece, 88:96] = jnp.zeros((8, 128), f32)
         out_ref[piece, 48:90] = whole_ref[42 * piece : 42 * piece + 42]
+
+
+def fan_kernel(strips_ref, out_ref):
+    for c in range(8):
+        strip = strips_ref[c, 64:80]
+        for piece in range(out_ref.shape[0]):
+            out_ref[piece, 16 * c : 16 * c + 16] = strip
 
 
 def place_top(q, own_ref, other_ref, refs):
@@ -155,8 +167,8 @@
                 ]
     b_ref[win + 80 : win + 88, :] = jnp.zeros((8, b_ref.shape[1]), f32)
     for j in range(4):
-        mine = rest_own_ref[4 * half + j]
-        theirs = rest_other_ref[4 * half + j]
+        mine = rest_own_ref[4 * half + j, 0:42]
+        theirs = rest_other_ref[4 * half + j, 0:42]
         lanes = slice(128 * j, 128 * j + 128)
         b_ref[win : win + 42, lanes] = jnp.where(q == 0, mine, theirs)
         b_ref[win + 42 : win + 84, lanes] = jnp.where(q == 0, theirs, mine)
@@ -268,7 +280,7 @@
 def per_device(panel_top, panel_win, panel_rest, trail_rest):
     q = lax.axis_index("row")
     (pieces,) = call(
-        pack_kernel, [(32, 90, 128)], [(1344, 128), pltpu.SemaphoreType.DMA((6,))], 2, 4,
+        pack_kernel, [(32, 96, 128)], [(1344, 128), pltpu.SemaphoreType.DMA((6,))], 2, 4,
         *(
             pltpu.with_memory_space_constraint(x, pltpu.HBM)
             for x in (
@@ -278,19 +290,19 @@
         in_specs=[pl.BlockSpec(memory_space=pltpu.HBM)] * 3,
     )
     parts = lax.all_to_all(pieces, ("layer", "row"), 0, 0)
-    sums = jnp.sum(parts.reshape(16, 2, 90, 128), axis=0)
+    sums = jnp.sum(parts.reshape(16, 2, 96, 128), axis=0)
     sums, trail = lax.optimization_barrier((sums, trail_rest[0].reshape(16, 84, 256)))
-    strips = spread(sums[:, 32:], "col")
+    strips = spread(sums[:, 32:].reshape(128, 128), "col")
     own = spread(
-        jnp.concatenate([strips[:4, 0, :16].reshape(64, 128), sums[:, :32].reshape(64, 128)], axis=0),
+        jnp.concatenate([strips[:4, :16].reshape(64, 128), sums[:, :32].reshape(64, 128)], axis=0),
         "layer",
     )
-    rest = strips[:, :, 16:]
-    rest_own = lax.dynamic_index_in_dim(rest, q, 1, False)
-    rest_other = swap_rows(lax.dynamic_index_in_dim(rest, 1 - q, 1, False))
+    rest_own = lax.dynamic_slice_in_dim(strips, 64 * q + 16, 48, 1)
+    rest_sent = lax.dynamic_slice_in_dim(strips, 80 - 64 * q, 48, 1)
+    (second,) = call(fan_kernel, [(16, 128, 128)], [], 1, 4, strips)
+    own, second, rest_own, rest_sent = lax.optimization_barrier((own, second, rest_own, rest_sent))
     other = swap_rows(own)
-    second = jnp.broadcast_to(strips[:, 1, :16].reshape(128, 128), (16, 128, 128))
-    own, other, second = lax.optimization_barrier((own, other, second))
+    rest_other = swap_rows(rest_sent)
     own2 = lax.all_to_all(second, "layer", 0, 0)
     carried = [(HALF, HALF), (4, 128, 128), (344, HALF)]
     u1, w1, b1 = call(

time: 141 us -> 139 us (0.986)
  blocking collectives: 23.4 us -> 0 us
  waiting for transfers between devices: 43 us -> 57.4 us
  starting transfers between devices: 28.8 us -> 36.2 us
    all_to_all x1 -> x0, blocking collectives: 23.4 us -> none  [spread(): lax.all_to_all(jnp.broadcast_to(value, (n,) + value.shape), axis, 0, 0)]
    all_to_all x1 -> x2, waiting for transfers between devices: 13.9 us -> 29.8 us  [spread(): lax.all_to_all(jnp.broadcast_to(value, (n,) + value.shape), axis, 0, 0)]
    all_to_all x1 -> x2, starting transfers between devices: 8.19 us -> 15.1 us  [spread(): lax.all_to_all(jnp.broadcast_to(value, (n,) + value.shape), axis, 0, 0)]
    ppermute x3, waiting for transfers between devices: 1.73 us -> 0.01 us  [swap_rows(): return lax.ppermute(value, 'row', [(0, 1), (1, 0)])]
    pallas_call x3 -> x4, Pallas kernels: 37.9 us -> 38.3 us  [call(): pl.pallas_call(kernel, out_shape=tuple((shape(s) for s in outs)), scratch...]
  transfers between devices with their start and end apart: 7 -> 8, of which waited for: 5 -> 5; matrix products, arithmetic and copies ran while one was open for 2% -> 1% of each run, Pallas kernels for 25% -> 26%
where the time goes in v6:
time: 139 us
  waiting for transfers between devices  57.4 us (41%)
  Pallas kernels  38.3 us (28%)
  starting transfers between devices  36.2 us (26%)
  local copies, waits for them, and re-layouts  3.88 us (3%)
  other arithmetic  2.23 us (2%)
    pallas_call x4, Pallas kernels, call(): pl.pallas_call(kernel, out_shape=tuple((shape(s) for s in outs)), scratch...  38.3 us
    all_to_all x2, waiting for transfers between devices, spread(): lax.all_to_all(jnp.broadcast_to(value, (n,) + value.shape), axis, 0, 0)  29.8 us
    all_to_all x1, waiting for transfers between devices, per_device(): parts = lax.all_to_all(pieces, ('layer', 'row'), 0, 0)  20.9 us
    all_to_all x2, starting transfers between devices, spread(): lax.all_to_all(jnp.broadcast_to(value, (n,) + value.shape), axis, 0, 0)  15.1 us
    all_to_all x1, starting transfers between devices, per_device(): parts = lax.all_to_all(pieces, ('layer', 'row'), 0, 0)  8.73 us
    all_to_all x1, waiting for transfers between devices, per_device(): trail_parts = lax.all_to_all(trail, 'layer', 0, 0)  4.74 us
    all_to_all x1, starting transfers between devices, per_device(): trail_parts = lax.all_to_all(trail, 'layer', 0, 0)  4.59 us
    ppermute x3, starting transfers between devices, swap_rows(): return lax.ppermute(value, 'row', [(0, 1), (1, 0)])  4.09 us
  transfers between devices with their start and end apart: 8, of which 5 were waited for; matrix products, arithmetic and copies ran while one was open for 1% of the time, Pallas kernels for 26%

profile of v6, /device:TPU:1, one launch (start us, length us, event | category | flops | bytes accessed | tf_op | source)
XLA Modules:
  0.0 138.7 jit_solution(8880094885112292401)
XLA Ops:
  0.6 2.6 %shard_map.75 = f32[32,96,128]{2,1,0:T(8,128)} custom-call(f32[32,16,128]{2,1,0:T(8,128)} %bitcast.107, f32[32,8,512]{2,1,0:T(8,128)} %bitcast.106, f32[1344,128]{1,0:T(8,128)} %bitcast.105), custom_call_target="tpu_custom_call" | custom-call | flops 2000000000 | bytes 6000000 | tf_op jit(solution)/shard_map/pallas_call | solution.py:259
  3.2 0.0 copy-start
  3.2 8.7 %all-to-all-start = ((f32[32,96,128]{2,1,0:T(8,128)}), f32[32,96,128]{2,1,0:T(8,128)S(1)}, u32[]{:S(2)}, u32[]{:S(2)}) async-start(f32[32,96,128]{2,1,0:T(8,128)} %shard_map.75), calls=%async_computation | async-start | bytes 3145728 | tf_op jit(solution)/shard_map/all_to_all | solution.py:292
  12.0 0.0 copy-done
  12.0 1.2 reshape_squeeze.11
  13.2 20.9 %all-to-all-done = f32[32,96,128]{2,1,0:T(8,128)S(1)} async-done(((f32[32,96,128]{2,1,0:T(8,128)}), f32[32,96,128]{2,1,0:T(8,128)S(1)}, u32[]{:S(2)}, u32[]{:S(2)}) %all-to-all-start) | async-done | bytes 1572896 | tf_op jit(solution)/shard_map/all_to_all | solution.py:292
  34.2 0.1 reduce_sum.9
  34.3 0.8 broadcast_in_dim.6
  35.1 8.2 %all-to-all-start.1 = ((f32[8,128,128]{2,1,0:T(8,128)}), f32[8,128,128]{2,1,0:T(8,128)S(1)}, u32[]{:S(2)}, u32[]{:S(2)}) async-start(f32[8,128,128]{2,1,0:T(8,128)} %broadcast_in_dim.6), calls=%async_computation.1 | async-start | bytes 1048576 | tf_op jit(solution)/shard_map/all_to_all | solution.py:277
  43.3 15.3 %all-to-all-done.1.strips_ref = f32[8,128,128]{2,1,0:T(8,128)S(1)} async-done(((f32[8,128,128]{2,1,0:T(8,128)}), f32[8,128,128]{2,1,0:T(8,128)S(1)}, u32[]{:S(2)}, u32[]{:S(2)}) %all-to-all-start.1) | async-done | bytes 524320 | tf_op jit(solution)/shard_map/all_to_all | solution.py:277
  58.6 1.1 broadcast_in_dim.7
  59.7 6.9 %all-to-all-start.2 = ((f32[16,128,128]{2,1,0:T(8,128)}), f32[16,128,128]{2,1,0:T(8,128)S(1)}, u32[]{:S(2)}, u32[]{:S(2)}) async-start(f32[16,128,128]{2,1,0:T(8,128)} %broadcast_in_dim.7), calls=%async_computation.2 | async-start | bytes 2097152 | tf_op jit(solution)/shard_map/all_to_all | solution.py:277
  66.6 1.1 shard_map.76
  67.7 0.7 constant_dynamic-slice_fusion
  68.4 14.5 %all-to-all-done.2.own_ref = f32[16,128,128]{2,1,0:T(8,128)S(1)} async-done(((f32[16,128,128]{2,1,0:T(8,128)}), f32[16,128,128]{2,1,0:T(8,128)S(1)}, u32[]{:S(2)}, u32[]{:S(2)}) %all-to-all-start.2) | async-done | bytes 1048608 | tf_op jit(solution)/shard_map/all_to_all | solution.py:277
  82.9 2.2 %collective-permute-start = (f32[16,128,128]{2,1,0:T(8,128)S(1)}, f32[16,128,128]{2,1,0:T(8,128)S(1)}, u32[]{:S(2)}, u32[]{:S(2)}) collective-permute-start(f32[16,128,128]{2,1,0:T(8,128)S(1)} %all-to-all-done.2.own_ref), channel_id=1, source_target_pairs={{0,128},{128,0},{1,129},{129,1},{2,130},{130,2},{3,131},{131,3},{4... | collective-permute-start | bytes 3145736 | tf_op jit(solution)/shard_map/ppermute | solution.py:272
  85.1 0.0 collective-permute-start.1
  85.1 3.7 %all-to-all-start.3 = ((f32[16,128,128]{2,1,0:T(8,128)}), f32[16,128,128]{2,1,0:T(8,128)S(1)}, u32[]{:S(2)}, u32[]{:S(2)}) async-start(f32[16,128,128]{2,1,0:T(8,128)} %shard_map.76), calls=%async_computation.3 | async-start | bytes 2097152 | tf_op jit(solution)/shard_map/all_to_all | solution.py:306
  88.8 0.0 collective-permute-done.1.rest_other_ref
  88.8 0.0 collective-permute-done.other_ref
  88.8 14.6 %shard_map.77 = (f32[512,512]{1,0:T(8,128)}, f32[4,128,128]{2,1,0:T(8,128)}, f32[344,512]{1,0:T(8,128)}) custom-call(f32[16,128,128]{2,1,0:T(8,128)S(1)} %all-to-all-done.2.own_ref, f32[16,128,128]{2,1,0:T(8,128)S(1)} %collective-permute-done.other_ref, f32[8,48,128]{2,1,0:T(8,128)S(1)} %get-tuple-element.23.rest_own_ref, ...), custom_call_target="tpu_custom_call" | custom-call | flops 14000000000 | bytes 42000000 | tf_op jit(solution)/shard_map/pallas_call | solution.py:259
  103.4 1.9 %all-to-all-done.3.own2_ref = f32[16,128,128]{2,1,0:T(8,128)S(1)} async-done(((f32[16,128,128]{2,1,0:T(8,128)}), f32[16,128,128]{2,1,0:T(8,128)S(1)}, u32[]{:S(2)}, u32[]{:S(2)}) %all-to-all-start.3) | async-done | bytes 1048608 | tf_op jit(solution)/shard_map/all_to_all | solution.py:306
  105.3 1.9 %collective-permute-start.2 = (f32[16,128,128]{2,1,0:T(8,128)S(1)}, f32[16,128,128]{2,1,0:T(8,128)}, u32[]{:S(2)}, u32[]{:S(2)}) collective-permute-start(f32[16,128,128]{2,1,0:T(8,128)S(1)} %all-to-all-done.3.own2_ref), channel_id=1, source_target_pairs={{0,128},{128,0},{1,129},{129,1},{2,130},{130,2},{3,131},{131,3},{4... | collective-permute-start | bytes 3145736 | tf_op jit(solution)/shard_map/ppermute | solution.py:272
  107.2 4.6 %all-to-all-start.4 = ((f32[16,84,256]{2,1,0:T(8,128)}), f32[16,84,256]{2,1,0:T(8,128)}, u32[]{:S(2)}, u32[]{:S(2)}) async-start(f32[16,84,256]{2,1,0:T(8,128)} %reshape_squeeze.11), calls=%async_computation.4 | async-start | bytes 2883584 | tf_op jit(solution)/shard_map/all_to_all | solution.py:316
  111.8 0.0 collective-permute-done.2.other2_ref
  111.8 20.1 %shard_map.78 = (f32[512,128]{1,0:T(8,128)}, f32[256,512]{1,0:T(8,128)}, f32[84,128]{1,0:T(8,128)}, f32[84,256]{1,0:T(8,128)S(1)}) custom-call(f32[16,128,128]{2,1,0:T(8,128)S(1)} %all-to-all-done.2.own_ref, f32[16,128,128]{2,1,0:T(8,128)S(1)} %collective-permute-done.other_ref, f32[16,128,128]{2,1,0:T(8,128)S(1)} %all-to-all-done.3.own2_ref, ...), custom_call_target="tpu_custom_call" | custom-call | flops 20000000000 | bytes 60000000 | tf_op jit(solution)/shard_map/pallas_call | solution.py:259
  131.8 4.7 %all-to-all-done.4 = f32[16,84,256]{2,1,0:T(8,128)} async-done(((f32[16,84,256]{2,1,0:T(8,128)}), f32[16,84,256]{2,1,0:T(8,128)}, u32[]{:S(2)}, u32[]{:S(2)}) %all-to-all-start.4) | async-done | bytes 1376288 | tf_op jit(solution)/shard_map/all_to_all | solution.py:316
  136.6 2.1 %fusion = f32[84,256]{1,0:T(8,128)} fusion(f32[16,84,256]{2,1,0:T(8,128)} %all-to-all-done.4, f32[84,256]{1,0:T(8,128)S(1)} %get-tuple-element.35), kind=kLoop, calls=%fused_computation.1 | loop fusion | flops 344064 | bytes 1548288 | tf_op jit(solution)/shard_map/add | solution.py:330
  (4 shorter events, 0.0 us)
Async XLA Ops:
  3.2 8.8 %copy-start = (f32[1,1344,256]{2,1,0:T(8,128)S(1)}, f32[1,1344,256]{2,1,0:T(8,128)}, u32[]{:S(2)}) copy-start(f32[1,1344,256]{2,1,0:T(8,128)} %param.7) | copy-start | bytes 4128772
  3.2 30.9 %all-to-all-start = ((f32[32,96,128]{2,1,0:T(8,128)}), f32[32,96,128]{2,1,0:T(8,128)S(1)}, u32[]{:S(2)}, u32[]{:S(2)}) async-start(f32[32,96,128]{2,1,0:T(8,128)} %shard_map.75), calls=%async_computation | async-start | bytes 3145728 | tf_op jit(solution)/shard_map/all_to_all | solution.py:292
  35.1 23.5 %all-to-all-start.1 = ((f32[8,128,128]{2,1,0:T(8,128)}), f32[8,128,128]{2,1,0:T(8,128)S(1)}, u32[]{:S(2)}, u32[]{:S(2)}) async-start(f32[8,128,128]{2,1,0:T(8,128)} %broadcast_in_dim.6), calls=%async_computation.1 | async-start | bytes 1048576 | tf_op jit(solution)/shard_map/all_to_all | solution.py:277
  59.7 23.2 %all-to-all-start.2 = ((f32[16,128,128]{2,1,0:T(8,128)}), f32[16,128,128]{2,1,0:T(8,128)S(1)}, u32[]{:S(2)}, u32[]{:S(2)}) async-start(f32[16,128,128]{2,1,0:T(8,128)} %broadcast_in_dim.7), calls=%async_computation.2 | async-start | bytes 2097152 | tf_op jit(solution)/shard_map/all_to_all | solution.py:277
  82.9 5.9 %collective-permute-start = (f32[16,128,128]{2,1,0:T(8,128)S(1)}, f32[16,128,128]{2,1,0:T(8,128)S(1)}, u32[]{:S(2)}, u32[]{:S(2)}) collective-permute-start(f32[16,128,128]{2,1,0:T(8,128)S(1)} %all-to-all-done.2.own_ref), channel_id=1, source_target_pairs={{0,128},{128,0},{1,129},{129,1},{2,130},{130,2},{3,131},{131,3},{4... | collective-permute-start | bytes 3145736 | tf_op jit(solution)/shard_map/ppermute | solution.py:272
  85.1 3.7 %collective-permute-start.1 = (f32[8,48,128]{2,1,0:T(8,128)}, f32[8,48,128]{2,1,0:T(8,128)}, u32[]{:S(2)}, u32[]{:S(2)}) collective-permute-start(f32[8,48,128]{2,1,0:T(8,128)} %get-tuple-element.24), channel_id=1, source_target_pairs={{0,128},{128,0},{1,129},{129,1},{2,130},{130,2},{3,131},{131,3},{4... | collective-permute-start | bytes 589832 | tf_op jit(solution)/shard_map/ppermute | solution.py:272
  85.1 20.1 %all-to-all-start.3 = ((f32[16,128,128]{2,1,0:T(8,128)}), f32[16,128,128]{2,1,0:T(8,128)S(1)}, u32[]{:S(2)}, u32[]{:S(2)}) async-start(f32[16,128,128]{2,1,0:T(8,128)} %shard_map.76), calls=%async_computation.3 | async-start | bytes 2097152 | tf_op jit(solution)/shard_map/all_to_all | solution.py:306
  105.3 6.5 %collective-permute-start.2 = (f32[16,128,128]{2,1,0:T(8,128)S(1)}, f32[16,128,128]{2,1,0:T(8,128)}, u32[]{:S(2)}, u32[]{:S(2)}) collective-permute-start(f32[16,128,128]{2,1,0:T(8,128)S(1)} %all-to-all-done.3.own2_ref), channel_id=1, source_target_pairs={{0,128},{128,0},{1,129},{129,1},{2,130},{130,2},{3,131},{131,3},{4... | collective-permute-start | bytes 3145736 | tf_op jit(solution)/shard_map/ppermute | solution.py:272
  107.2 29.4 %all-to-all-start.4 = ((f32[16,84,256]{2,1,0:T(8,128)}), f32[16,84,256]{2,1,0:T(8,128)}, u32[]{:S(2)}, u32[]{:S(2)}) async-start(f32[16,84,256]{2,1,0:T(8,128)} %reshape_squeeze.11), calls=%async_computation.4 | async-start | bytes 2883584 | tf_op jit(solution)/shard_map/all_to_all | solution.py:316

commit v7 on v6

--- a/solution.py
+++ b/solution.py
@@ -76,7 +76,7 @@
     return jnp.concatenate(inverse, axis=0)
 
 
-def factor_loop(a_ref, u_ref, w_ref, b_ref, beside=lambda: None):
+def factor_loop(a_ref, u_ref, w_ref, b_ref, first_diagonal, beside=lambda: None):
     n = a_ref.shape[0]
     blocks = n // 128
     ahead = lax.broadcasted_iota(jnp.int32, (128, n), 1) - lax.broadcasted_iota(
@@ -105,18 +105,18 @@
         corner = u_ref[pl.ds(o, 128), following]
         return a_ref[following, following] - mm(corner, corner, TN)
 
-    lax.fori_loop(1, blocks, step, step(0, a_ref[0:128, 0:128], True))
+    lax.fori_loop(1, blocks, step, step(0, first_diagonal, True))
     last, solved = solve(blocks - 1)
     b_ref[:, last] = solved
 
 
-def solve_rows(x_ref, u_ref, w_ref):
+def solve_rows(x_ref, rows, u_ref, w_ref):
     for k in range(x_ref.shape[1] // 128):
         here = slice(128 * k, 128 * k + 128)
-        value = x_ref[:, here]
+        value = x_ref[rows, here]
         if k:
-            value = value - mm(x_ref[:, : 128 * k], u_ref[0 : 128 * k, here])
-        x_ref[:, here] = mm(value, w_ref[k], NT)
+            value = value - mm(x_ref[rows, : 128 * k], u_ref[0 : 128 * k, here])
+        x_ref[rows, here] = mm(value, w_ref[k], NT)
 
 
 def aligned(index, step):
@@ -191,7 +191,7 @@
     q = lax.axis_index("row")
     place_top(q, own_ref, other_ref, [a_ref])
     place_lower(q, 0, own_ref, other_ref, rest_own_ref, rest_other_ref, b_ref)
-    factor_loop(a_ref, u_ref, w_ref, b_ref)
+    factor_loop(a_ref, u_ref, w_ref, b_ref, a_ref[0:128, 0:128])
     for copy in start_all((u_ref, w_ref, b_ref), (u_out, w_out, b_out), sems):
         copy.wait()
 
@@ -210,14 +210,16 @@
     place_lower(q, 1, own_ref, other_ref, rest_own_ref, rest_other_ref, b_ref)
     for copy in copies:
         copy.wait()
-    solve_rows(l_ref, u1_ref, w1_ref)
-    a_ref[...] = a_ref[...] - mm(l_ref[...], l_ref[...], NT)
+    solve_rows(l_ref, slice(0, 128), u1_ref, w1_ref)
+    diagonal = a_ref[0:128, 0:128] - mm(l_ref[0:128], l_ref[0:128], NT)
 
     def beside():
+        solve_rows(l_ref, slice(128, HALF), u1_ref, w1_ref)
+        a_ref[...] = a_ref[...] - mm(l_ref[...], l_ref[...], NT)
         b_ref[...] = b_ref[...] - mm(b1_ref[...], l_ref[...], NT)
         sum_ref[...] = mm(b1_ref[n_win:, :], b1_ref[:n_win, :], NT)
 
-    factor_loop(a_ref, u2_ref, w2_ref, b_ref, beside)
+    factor_loop(a_ref, u2_ref, w2_ref, b_ref, diagonal, beside)
     product_out[...] = (sum_ref[...] + mm(b_ref[n_win:, :], b_ref[:n_win, :], NT))[:n_rest]
     left = c < 4
 

time: 139 us -> 139 us (level)
  transfers between devices with their start and end apart: 8 -> 8, of which waited for: 5 -> 5; matrix products, arithmetic and copies ran while one was open for 1% -> 1% of each run, Pallas kernels for 26% -> 27%
where the time goes in v7:
time: 139 us
  waiting for transfers between devices  56.2 us (40%)
  Pallas kernels  39.5 us (28%)
  starting transfers between devices  36.2 us (26%)
  local copies, waits for them, and re-layouts  3.88 us (3%)
  other arithmetic  2.23 us (2%)
    pallas_call x4, Pallas kernels, call(): pl.pallas_call(kernel, out_shape=tuple((shape(s) for s in outs)), scratch...  39.5 us
    all_to_all x2, waiting for transfers between devices, spread(): lax.all_to_all(jnp.broadcast_to(value, (n,) + value.shape), axis, 0, 0)  29.8 us
    all_to_all x1, waiting for transfers between devices, per_device(): parts = lax.all_to_all(pieces, ('layer', 'row'), 0, 0)  20.9 us
    all_to_all x2, starting transfers between devices, spread(): lax.all_to_all(jnp.broadcast_to(value, (n,) + value.shape), axis, 0, 0)  15.1 us
    all_to_all x1, starting transfers between devices, per_device(): parts = lax.all_to_all(pieces, ('layer', 'row'), 0, 0)  8.73 us
    all_to_all x1, starting transfers between devices, per_device(): trail_parts = lax.all_to_all(trail, 'layer', 0, 0)  4.59 us
    ppermute x3, starting transfers between devices, swap_rows(): return lax.ppermute(value, 'row', [(0, 1), (1, 0)])  4.09 us
    all_to_all x1, starting transfers between devices, per_device(): own2 = lax.all_to_all(second, 'layer', 0, 0)  3.65 us
  transfers between devices with their start and end apart: 8, of which 5 were waited for; matrix products, arithmetic and copies ran while one was open for 1% of the time, Pallas kernels for 27%

profile of v7, /device:TPU:1, one launch (start us, length us, event | category | flops | bytes accessed | tf_op | source)
XLA Modules:
  0.0 138.7 jit_solution(4225183483391497738)
XLA Ops:
  0.6 2.6 %shard_map.75 = f32[32,96,128]{2,1,0:T(8,128)} custom-call(f32[32,16,128]{2,1,0:T(8,128)} %bitcast.107, f32[32,8,512]{2,1,0:T(8,128)} %bitcast.106, f32[1344,128]{1,0:T(8,128)} %bitcast.105), custom_call_target="tpu_custom_call" | custom-call | flops 2000000000 | bytes 6000000 | tf_op jit(solution)/shard_map/pallas_call | solution.py:261
  3.2 0.0 copy-start
  3.2 8.7 %all-to-all-start = ((f32[32,96,128]{2,1,0:T(8,128)}), f32[32,96,128]{2,1,0:T(8,128)S(1)}, u32[]{:S(2)}, u32[]{:S(2)}) async-start(f32[32,96,128]{2,1,0:T(8,128)} %shard_map.75), calls=%async_computation | async-start | bytes 3145728 | tf_op jit(solution)/shard_map/all_to_all | solution.py:294
  12.0 0.0 copy-done
  12.0 1.2 reshape_squeeze.11
  13.2 20.9 %all-to-all-done = f32[32,96,128]{2,1,0:T(8,128)S(1)} async-done(((f32[32,96,128]{2,1,0:T(8,128)}), f32[32,96,128]{2,1,0:T(8,128)S(1)}, u32[]{:S(2)}, u32[]{:S(2)}) %all-to-all-start) | async-done | bytes 1572896 | tf_op jit(solution)/shard_map/all_to_all | solution.py:294
  34.2 0.1 reduce_sum.9
  34.3 0.8 broadcast_in_dim.6
  35.1 8.2 %all-to-all-start.1 = ((f32[8,128,128]{2,1,0:T(8,128)}), f32[8,128,128]{2,1,0:T(8,128)S(1)}, u32[]{:S(2)}, u32[]{:S(2)}) async-start(f32[8,128,128]{2,1,0:T(8,128)} %broadcast_in_dim.6), calls=%async_computation.1 | async-start | bytes 1048576 | tf_op jit(solution)/shard_map/all_to_all | solution.py:279
  43.3 15.3 %all-to-all-done.1.strips_ref = f32[8,128,128]{2,1,0:T(8,128)S(1)} async-done(((f32[8,128,128]{2,1,0:T(8,128)}), f32[8,128,128]{2,1,0:T(8,128)S(1)}, u32[]{:S(2)}, u32[]{:S(2)}) %all-to-all-start.1) | async-done | bytes 524320 | tf_op jit(solution)/shard_map/all_to_all | solution.py:279
  58.6 1.1 broadcast_in_dim.7
  59.7 6.9 %all-to-all-start.2 = ((f32[16,128,128]{2,1,0:T(8,128)}), f32[16,128,128]{2,1,0:T(8,128)S(1)}, u32[]{:S(2)}, u32[]{:S(2)}) async-start(f32[16,128,128]{2,1,0:T(8,128)} %broadcast_in_dim.7), calls=%async_computation.2 | async-start | bytes 2097152 | tf_op jit(solution)/shard_map/all_to_all | solution.py:279
  66.6 1.1 shard_map.76
  67.7 0.7 constant_dynamic-slice_fusion
  68.4 14.5 %all-to-all-done.2.own_ref = f32[16,128,128]{2,1,0:T(8,128)S(1)} async-done(((f32[16,128,128]{2,1,0:T(8,128)}), f32[16,128,128]{2,1,0:T(8,128)S(1)}, u32[]{:S(2)}, u32[]{:S(2)}) %all-to-all-start.2) | async-done | bytes 1048608 | tf_op jit(solution)/shard_map/all_to_all | solution.py:279
  82.9 2.2 %collective-permute-start = (f32[16,128,128]{2,1,0:T(8,128)S(1)}, f32[16,128,128]{2,1,0:T(8,128)S(1)}, u32[]{:S(2)}, u32[]{:S(2)}) collective-permute-start(f32[16,128,128]{2,1,0:T(8,128)S(1)} %all-to-all-done.2.own_ref), channel_id=1, source_target_pairs={{0,128},{128,0},{1,129},{129,1},{2,130},{130,2},{3,131},{131,3},{4... | collective-permute-start | bytes 3145736 | tf_op jit(solution)/shard_map/ppermute | solution.py:274
  85.1 0.0 collective-permute-start.1
  85.1 3.7 %all-to-all-start.3 = ((f32[16,128,128]{2,1,0:T(8,128)}), f32[16,128,128]{2,1,0:T(8,128)S(1)}, u32[]{:S(2)}, u32[]{:S(2)}) async-start(f32[16,128,128]{2,1,0:T(8,128)} %shard_map.76), calls=%async_computation.3 | async-start | bytes 2097152 | tf_op jit(solution)/shard_map/all_to_all | solution.py:308
  88.8 0.0 collective-permute-done.1.rest_other_ref
  88.8 0.0 collective-permute-done.other_ref
  88.8 14.6 %shard_map.77 = (f32[512,512]{1,0:T(8,128)}, f32[4,128,128]{2,1,0:T(8,128)}, f32[344,512]{1,0:T(8,128)}) custom-call(f32[16,128,128]{2,1,0:T(8,128)S(1)} %all-to-all-done.2.own_ref, f32[16,128,128]{2,1,0:T(8,128)S(1)} %collective-permute-done.other_ref, f32[8,48,128]{2,1,0:T(8,128)S(1)} %get-tuple-element.23.rest_own_ref, ...), custom_call_target="tpu_custom_call" | custom-call | flops 14000000000 | bytes 42000000 | tf_op jit(solution)/shard_map/pallas_call | solution.py:261
  103.4 1.9 %all-to-all-done.3.own2_ref = f32[16,128,128]{2,1,0:T(8,128)S(1)} async-done(((f32[16,128,128]{2,1,0:T(8,128)}), f32[16,128,128]{2,1,0:T(8,128)S(1)}, u32[]{:S(2)}, u32[]{:S(2)}) %all-to-all-start.3) | async-done | bytes 1048608 | tf_op jit(solution)/shard_map/all_to_all | solution.py:308
  105.3 1.9 %collective-permute-start.2 = (f32[16,128,128]{2,1,0:T(8,128)S(1)}, f32[16,128,128]{2,1,0:T(8,128)}, u32[]{:S(2)}, u32[]{:S(2)}) collective-permute-start(f32[16,128,128]{2,1,0:T(8,128)S(1)} %all-to-all-done.3.own2_ref), channel_id=1, source_target_pairs={{0,128},{128,0},{1,129},{129,1},{2,130},{130,2},{3,131},{131,3},{4... | collective-permute-start | bytes 3145736 | tf_op jit(solution)/shard_map/ppermute | solution.py:274
  107.2 4.6 %all-to-all-start.4 = ((f32[16,84,256]{2,1,0:T(8,128)}), f32[16,84,256]{2,1,0:T(8,128)}, u32[]{:S(2)}, u32[]{:S(2)}) async-start(f32[16,84,256]{2,1,0:T(8,128)} %reshape_squeeze.11), calls=%async_computation.4 | async-start | bytes 2883584 | tf_op jit(solution)/shard_map/all_to_all | solution.py:318
  111.8 0.0 collective-permute-done.2.other2_ref
  111.8 21.2 %shard_map.78 = (f32[512,128]{1,0:T(8,128)}, f32[256,512]{1,0:T(8,128)}, f32[84,128]{1,0:T(8,128)}, f32[84,256]{1,0:T(8,128)S(1)}) custom-call(f32[16,128,128]{2,1,0:T(8,128)S(1)} %all-to-all-done.2.own_ref, f32[16,128,128]{2,1,0:T(8,128)S(1)} %collective-permute-done.other_ref, f32[16,128,128]{2,1,0:T(8,128)S(1)} %all-to-all-done.3.own2_ref, ...), custom_call_target="tpu_custom_call" | custom-call | flops 20000000000 | bytes 60000000 | tf_op jit(solution)/shard_map/pallas_call | solution.py:261
  133.0 3.6 %all-to-all-done.4 = f32[16,84,256]{2,1,0:T(8,128)} async-done(((f32[16,84,256]{2,1,0:T(8,128)}), f32[16,84,256]{2,1,0:T(8,128)}, u32[]{:S(2)}, u32[]{:S(2)}) %all-to-all-start.4) | async-done | bytes 1376288 | tf_op jit(solution)/shard_map/all_to_all | solution.py:318
  136.6 2.1 %fusion = f32[84,256]{1,0:T(8,128)} fusion(f32[16,84,256]{2,1,0:T(8,128)} %all-to-all-done.4, f32[84,256]{1,0:T(8,128)S(1)} %get-tuple-element.35), kind=kLoop, calls=%fused_computation.1 | loop fusion | flops 344064 | bytes 1548288 | tf_op jit(solution)/shard_map/add | solution.py:332
  (4 shorter events, 0.0 us)
Async XLA Ops:
  3.2 8.8 %copy-start = (f32[1,1344,256]{2,1,0:T(8,128)S(1)}, f32[1,1344,256]{2,1,0:T(8,128)}, u32[]{:S(2)}) copy-start(f32[1,1344,256]{2,1,0:T(8,128)} %param.7) | copy-start | bytes 4128772
  3.2 30.9 %all-to-all-start = ((f32[32,96,128]{2,1,0:T(8,128)}), f32[32,96,128]{2,1,0:T(8,128)S(1)}, u32[]{:S(2)}, u32[]{:S(2)}) async-start(f32[32,96,128]{2,1,0:T(8,128)} %shard_map.75), calls=%async_computation | async-start | bytes 3145728 | tf_op jit(solution)/shard_map/all_to_all | solution.py:294
  35.1 23.5 %all-to-all-start.1 = ((f32[8,128,128]{2,1,0:T(8,128)}), f32[8,128,128]{2,1,0:T(8,128)S(1)}, u32[]{:S(2)}, u32[]{:S(2)}) async-start(f32[8,128,128]{2,1,0:T(8,128)} %broadcast_in_dim.6), calls=%async_computation.1 | async-start | bytes 1048576 | tf_op jit(solution)/shard_map/all_to_all | solution.py:279
  59.7 23.2 %all-to-all-start.2 = ((f32[16,128,128]{2,1,0:T(8,128)}), f32[16,128,128]{2,1,0:T(8,128)S(1)}, u32[]{:S(2)}, u32[]{:S(2)}) async-start(f32[16,128,128]{2,1,0:T(8,128)} %broadcast_in_dim.7), calls=%async_computation.2 | async-start | bytes 2097152 | tf_op jit(solution)/shard_map/all_to_all | solution.py:279
  82.9 5.9 %collective-permute-start = (f32[16,128,128]{2,1,0:T(8,128)S(1)}, f32[16,128,128]{2,1,0:T(8,128)S(1)}, u32[]{:S(2)}, u32[]{:S(2)}) collective-permute-start(f32[16,128,128]{2,1,0:T(8,128)S(1)} %all-to-all-done.2.own_ref), channel_id=1, source_target_pairs={{0,128},{128,0},{1,129},{129,1},{2,130},{130,2},{3,131},{131,3},{4... | collective-permute-start | bytes 3145736 | tf_op jit(solution)/shard_map/ppermute | solution.py:274
  85.1 3.7 %collective-permute-start.1 = (f32[8,48,128]{2,1,0:T(8,128)}, f32[8,48,128]{2,1,0:T(8,128)}, u32[]{:S(2)}, u32[]{:S(2)}) collective-permute-start(f32[8,48,128]{2,1,0:T(8,128)} %get-tuple-element.24), channel_id=1, source_target_pairs={{0,128},{128,0},{1,129},{129,1},{2,130},{130,2},{3,131},{131,3},{4... | collective-permute-start | bytes 589832 | tf_op jit(solution)/shard_map/ppermute | solution.py:274
  85.1 20.1 %all-to-all-start.3 = ((f32[16,128,128]{2,1,0:T(8,128)}), f32[16,128,128]{2,1,0:T(8,128)S(1)}, u32[]{:S(2)}, u32[]{:S(2)}) async-start(f32[16,128,128]{2,1,0:T(8,128)} %shard_map.76), calls=%async_computation.3 | async-start | bytes 2097152 | tf_op jit(solution)/shard_map/all_to_all | solution.py:308
  105.3 6.5 %collective-permute-start.2 = (f32[16,128,128]{2,1,0:T(8,128)S(1)}, f32[16,128,128]{2,1,0:T(8,128)}, u32[]{:S(2)}, u32[]{:S(2)}) collective-permute-start(f32[16,128,128]{2,1,0:T(8,128)S(1)} %all-to-all-done.3.own2_ref), channel_id=1, source_target_pairs={{0,128},{128,0},{1,129},{129,1},{2,130},{130,2},{3,131},{131,3},{4... | collective-permute-start | bytes 3145736 | tf_op jit(solution)/shard_map/ppermute | solution.py:274
  107.2 29.4 %all-to-all-start.4 = ((f32[16,84,256]{2,1,0:T(8,128)}), f32[16,84,256]{2,1,0:T(8,128)}, u32[]{:S(2)}, u32[]{:S(2)}) async-start(f32[16,84,256]{2,1,0:T(8,128)} %reshape_squeeze.11), calls=%async_computation.4 | async-start | bytes 2883584 | tf_op jit(solution)/shard_map/all_to_all | solution.py:318

commit v8 on v6

--- a/solution.py
+++ b/solution.py
@@ -76,7 +76,7 @@
     return jnp.concatenate(inverse, axis=0)
 
 
-def factor_loop(a_ref, u_ref, w_ref, b_ref, beside=lambda: None):
+def factor_loop(a_ref, u_ref, w_ref, b_ref=None, beside=lambda: None):
     n = a_ref.shape[0]
     blocks = n // 128
     ahead = lax.broadcasted_iota(jnp.int32, (128, n), 1) - lax.broadcasted_iota(
@@ -95,9 +95,10 @@
         else:
             past = u_ref[pl.ds(pl.multiple_of(k * 128 - 128, 128), 128), :]
             a_ref[...] = a_ref[...] - mm(past, past, TN)
-            before, solved = solve(k - 1)
-            b_ref[...] = b_ref[...] - mm(solved, past)
-            b_ref[:, before] = solved
+            if b_ref is not None:
+                before, solved = solve(k - 1)
+                b_ref[...] = b_ref[...] - mm(solved, past)
+                b_ref[:, before] = solved
         w_ref[k] = inverse
         panel = mm(inverse, a_ref[pl.ds(o, 128), :])
         u_ref[pl.ds(o, 128), :] = jnp.where(ahead >= o, panel, 0.0)
@@ -106,8 +107,9 @@
         return a_ref[following, following] - mm(corner, corner, TN)
 
     lax.fori_loop(1, blocks, step, step(0, a_ref[0:128, 0:128], True))
-    last, solved = solve(blocks - 1)
-    b_ref[:, last] = solved
+    if b_ref is not None:
+        last, solved = solve(blocks - 1)
+        b_ref[:, last] = solved
 
 
 def solve_rows(x_ref, u_ref, w_ref):
@@ -138,7 +140,10 @@
         out_ref[piece, 48:90] = whole_ref[42 * piece : 42 * piece + 42]
 
 
-def fan_kernel(strips_ref, out_ref):
+def fan_kernel(strips_ref, win_ref, out_ref):
+    for piece in range(out_ref.shape[0]):
+        for half in range(2):
+            out_ref[piece, 128 + 32 * half : 160 + 32 * half] = win_ref[half]
     for c in range(8):
         strip = strips_ref[c, 64:80]
         for piece in range(out_ref.shape[0]):
@@ -161,7 +166,7 @@
     for which, src in ((q, own_ref), (1 - q, other_ref)):
         for strip in range(src.shape[0]):
             for j in range(4):
-                first = 64 + 32 * half + 8 * j
+                first = 128 + 32 * half + 8 * j
                 b_ref[aligned(2 * strip + which, 8), 128 * j : 128 * j + 128] = src[
                     strip, first : first + 8
                 ]
@@ -184,36 +189,34 @@
     return copies
 
 
-def first_kernel(
-    own_ref, other_ref, rest_own_ref, rest_other_ref, u_out, w_out, b_out,
-    u_ref, w_ref, b_ref, a_ref, sems,
-):
+def first_kernel(own_ref, other_ref, u_out, w_out, u_ref, w_ref, a_ref, sems):
     q = lax.axis_index("row")
     place_top(q, own_ref, other_ref, [a_ref])
-    place_lower(q, 0, own_ref, other_ref, rest_own_ref, rest_other_ref, b_ref)
-    factor_loop(a_ref, u_ref, w_ref, b_ref)
-    for copy in start_all((u_ref, w_ref, b_ref), (u_out, w_out, b_out), sems):
+    factor_loop(a_ref, u_ref, w_ref)
+    for copy in start_all((u_ref, w_ref), (u_out, w_out), sems):
         copy.wait()
 
 
 def second_kernel(
-    own_ref, other_ref, own2_ref, other2_ref, rest_own_ref, rest_other_ref, u1_in, w1_in, b1_in,
+    own_ref, other_ref, rest_own_ref, rest_other_ref, u1_in, w1_in,
     top_out, win_out, rest_out, product_out, u1_ref, w1_ref, b1_ref, l_ref, a_ref, u2_ref, w2_ref,
     b_ref, sum_ref, sems,
 ):
-    copies = start_all((u1_in, w1_in, b1_in), (u1_ref, w1_ref, b1_ref), sems)
+    copies = start_all((u1_in, w1_in), (u1_ref, w1_ref), sems)
     q = lax.axis_index("row")
     c = lax.axis_index("col")
     n_win = win_out.shape[0]
     n_rest = rest_out.shape[0]
-    place_top(q, own2_ref, other2_ref, [l_ref, a_ref])
-    place_lower(q, 1, own_ref, other_ref, rest_own_ref, rest_other_ref, b_ref)
+    place_top(q, own_ref, other_ref, [l_ref, a_ref])
+    for half, dst in enumerate((b1_ref, b_ref)):
+        place_lower(q, half, own_ref, other_ref, rest_own_ref, rest_other_ref, dst)
     for copy in copies:
         copy.wait()
     solve_rows(l_ref, u1_ref, w1_ref)
     a_ref[...] = a_ref[...] - mm(l_ref[...], l_ref[...], NT)
 
     def beside():
+        solve_rows(b1_ref, u1_ref, w1_ref)
         b_ref[...] = b_ref[...] - mm(b1_ref[...], l_ref[...], NT)
         sum_ref[...] = mm(b1_ref[n_win:, :], b1_ref[:n_win, :], NT)
 
@@ -293,24 +296,21 @@
     sums = jnp.sum(parts.reshape(16, 2, 96, 128), axis=0)
     sums, trail = lax.optimization_barrier((sums, trail_rest[0].reshape(16, 84, 256)))
     strips = spread(sums[:, 32:].reshape(128, 128), "col")
-    own = spread(
-        jnp.concatenate([strips[:4, :16].reshape(64, 128), sums[:, :32].reshape(64, 128)], axis=0),
-        "layer",
-    )
+    own = spread(strips[:4, :16].reshape(64, 128), "layer")
     rest_own = lax.dynamic_slice_in_dim(strips, 64 * q + 16, 48, 1)
     rest_sent = lax.dynamic_slice_in_dim(strips, 80 - 64 * q, 48, 1)
-    (second,) = call(fan_kernel, [(16, 128, 128)], [], 1, 4, strips)
+    (second,) = call(fan_kernel, [(16, 192, 128)], [], 1, 6, strips, sums[:, :32])
     own, second, rest_own, rest_sent = lax.optimization_barrier((own, second, rest_own, rest_sent))
     other = swap_rows(own)
     rest_other = swap_rows(rest_sent)
     own2 = lax.all_to_all(second, "layer", 0, 0)
-    carried = [(HALF, HALF), (4, 128, 128), (344, HALF)]
-    u1, w1, b1 = call(
+    carried = [(HALF, HALF), (4, 128, 128)]
+    u1, w1 = call(
         first_kernel, [pltpu.HBM(x, f32) for x in carried],
-        carried + [(HALF, HALF), pltpu.SemaphoreType.DMA((3,))], 14, 12,
-        own, other, rest_own, rest_other, out_specs=(pl.BlockSpec(memory_space=pltpu.HBM),) * 3,
-    )
-    u1, w1, b1 = (pltpu.with_memory_space_constraint(x, pltpu.HBM) for x in (u1, w1, b1))
+        carried + [(HALF, HALF), pltpu.SemaphoreType.DMA((2,))], 14, 12,
+        own, other, out_specs=(pl.BlockSpec(memory_space=pltpu.HBM),) * 2,
+    )
+    u1, w1 = (pltpu.with_memory_space_constraint(x, pltpu.HBM) for x in (u1, w1))
     own2, w1, trail = lax.optimization_barrier((own2, w1, trail))
     other2 = swap_rows(own2)
     trail_parts = lax.all_to_all(trail, "layer", 0, 0)
@@ -318,12 +318,12 @@
         second_kernel,
         [(HALF, 128), (256, HALF), (84, 128), (84, 256)],
         carried
-        + [(HALF, HALF), (HALF, HALF), (HALF, HALF), (4, 128, 128), (344, HALF), (88, 256)]
-        + [pltpu.SemaphoreType.DMA((3,))],
+        + [(344, HALF), (HALF, HALF), (HALF, HALF), (HALF, HALF), (4, 128, 128), (344, HALF)]
+        + [(88, 256), pltpu.SemaphoreType.DMA((2,))],
         20, 20,
-        own, other, own2, other2, rest_own, rest_other, u1, w1, b1,
-        in_specs=[pl.BlockSpec(memory_space=pltpu.VMEM)] * 6
-        + [pl.BlockSpec(memory_space=pltpu.HBM)] * 3,
+        own2, other2, rest_own, rest_other, u1, w1,
+        in_specs=[pl.BlockSpec(memory_space=pltpu.VMEM)] * 4
+        + [pl.BlockSpec(memory_space=pltpu.HBM)] * 2,
     )
     schur = trail_parts[0] - product
     for part in range(1, 16):

time: 139 us -> 139 us (level)
  blocking collectives: 0 us -> 22.4 us
  waiting for transfers between devices: 57.4 us -> 44.6 us
  starting transfers between devices: 36.2 us -> 27.4 us
  local copies, waits for them, and re-layouts: 3.88 us -> 2.18 us
    all_to_all x0 -> x1, blocking collectives: none -> 22.4 us  [spread(): lax.all_to_all(jnp.broadcast_to(value, (n,) + value.shape), axis, 0, 0)]
    all_to_all x2 -> x1, waiting for transfers between devices: 29.8 us -> 9.32 us  [spread(): lax.all_to_all(jnp.broadcast_to(value, (n,) + value.shape), axis, 0, 0)]
    all_to_all x1, waiting for transfers between devices: 1.88 us -> 13.2 us  [per_device(): own2 = lax.all_to_all(second, 'layer', 0, 0)]
    all_to_all x2 -> x1, starting transfers between devices: 15.1 us -> 7.76 us  [spread(): lax.all_to_all(jnp.broadcast_to(value, (n,) + value.shape), axis, 0, 0)]
    all_to_all x1, waiting for transfers between devices: 4.74 us -> 1.19 us  [per_device(): trail_parts = lax.all_to_all(trail, 'layer', 0, 0)]
    ppermute x3, starting transfers between devices: 4.09 us -> 2.61 us  [swap_rows(): return lax.ppermute(value, 'row', [(0, 1), (1, 0)])]
  transfers between devices with their start and end apart: 8 -> 7, of which waited for: 5 -> 4; matrix products, arithmetic and copies ran while one was open for 1% -> 1% of each run, Pallas kernels for 26% -> 26%
where the time goes in v8:
time: 139 us; the launch traced here: 138 us
  waiting for transfers between devices  44.6 us (32%)
  Pallas kernels  38.8 us (28%)
  starting transfers between devices  27.4 us (20%)
  blocking collectives  22.4 us (16%)
  other arithmetic  2.22 us (2%)
  local copies, waits for them, and re-layouts  2.18 us (2%)
    pallas_call x4, Pallas kernels, call(): pl.pallas_call(kernel, out_shape=tuple((shape(s) for s in outs)), scratch...  38.8 us
    all_to_all x1, blocking collectives, spread(): lax.all_to_all(jnp.broadcast_to(value, (n,) + value.shape), axis, 0, 0)  22.4 us
    all_to_all x1, waiting for transfers between devices, per_device(): parts = lax.all_to_all(pieces, ('layer', 'row'), 0, 0)  20.9 us
    all_to_all x1, waiting for transfers between devices, per_device(): own2 = lax.all_to_all(second, 'layer', 0, 0)  13.2 us
    all_to_all x1, waiting for transfers between devices, spread(): lax.all_to_all(jnp.broadcast_to(value, (n,) + value.shape), axis, 0, 0)  9.32 us
    all_to_all x1, starting transfers between devices, per_device(): parts = lax.all_to_all(pieces, ('layer', 'row'), 0, 0)  8.73 us
    all_to_all x1, starting transfers between devices, spread(): lax.all_to_all(jnp.broadcast_to(value, (n,) + value.shape), axis, 0, 0)  7.76 us
    all_to_all x1, starting transfers between devices, per_device(): trail_parts = lax.all_to_all(trail, 'layer', 0, 0)  4.58 us
  transfers between devices with their start and end apart: 7, of which 4 were waited for; matrix products, arithmetic and copies ran while one was open for 1% of the time, Pallas kernels for 26%

profile of v8, /device:TPU:1, one launch (start us, length us, event | category | flops | bytes accessed | tf_op | source)
XLA Modules:
  0.0 138.4 jit_solution(10143022658386554139)
XLA Ops:
  0.6 2.6 %shard_map.75 = f32[32,96,128]{2,1,0:T(8,128)} custom-call(f32[32,16,128]{2,1,0:T(8,128)} %bitcast.105, f32[32,8,512]{2,1,0:T(8,128)} %bitcast.104, f32[1344,128]{1,0:T(8,128)} %bitcast.103), custom_call_target="tpu_custom_call" | custom-call | flops 2000000000 | bytes 6000000 | tf_op jit(solution)/shard_map/pallas_call | solution.py:262
  3.2 0.0 copy-start
  3.3 8.7 %all-to-all-start = ((f32[32,96,128]{2,1,0:T(8,128)}), f32[32,96,128]{2,1,0:T(8,128)S(1)}, u32[]{:S(2)}, u32[]{:S(2)}) async-start(f32[32,96,128]{2,1,0:T(8,128)} %shard_map.75), calls=%async_computation | async-start | bytes 3145728 | tf_op jit(solution)/shard_map/all_to_all | solution.py:295
  12.0 0.0 copy-done
  12.0 1.2 reshape_squeeze.11
  13.3 20.9 %all-to-all-done = f32[32,96,128]{2,1,0:T(8,128)S(1)} async-done(((f32[32,96,128]{2,1,0:T(8,128)}), f32[32,96,128]{2,1,0:T(8,128)S(1)}, u32[]{:S(2)}, u32[]{:S(2)}) %all-to-all-start) | async-done | bytes 1572896 | tf_op jit(solution)/shard_map/all_to_all | solution.py:295
  34.2 0.1 reduce_sum.9
  34.3 22.4 %all_to_all.25.strips_ref = f32[8,128,128]{2,1,0:T(8,128)S(1)} all-to-all(f32[8,128,128]{2,1,0:T(8,128)S(1)} %broadcast_in_dim.6), channel_id=1, replica_groups=mesh['row'=2,'col'=8,'layer'=16] {'col'}, dimensions={0} | all-to-all | bytes 1048576 | tf_op jit(solution)/shard_map/all_to_all | solution.py:280
  56.8 0.8 broadcast_in_dim.7
  57.6 7.8 %all-to-all-start.2 = ((f32[16,64,128]{2,1,0:T(8,128)}), f32[16,64,128]{2,1,0:T(8,128)S(1)}, u32[]{:S(2)}, u32[]{:S(2)}) async-start(f32[16,64,128]{2,1,0:T(8,128)} %broadcast_in_dim.7), calls=%async_computation.2 | async-start | bytes 1048576 | tf_op jit(solution)/shard_map/all_to_all | solution.py:280
  65.4 1.3 shard_map.76
  66.7 9.3 %all-to-all-done.2.own_ref = f32[16,64,128]{2,1,0:T(8,128)S(1)} async-done(((f32[16,64,128]{2,1,0:T(8,128)}), f32[16,64,128]{2,1,0:T(8,128)S(1)}, u32[]{:S(2)}, u32[]{:S(2)}) %all-to-all-start.2) | async-done | bytes 524320 | tf_op jit(solution)/shard_map/all_to_all | solution.py:280
  76.0 1.8 %collective-permute-start = (f32[16,64,128]{2,1,0:T(8,128)S(1)}, f32[16,64,128]{2,1,0:T(8,128)S(1)}, u32[]{:S(2)}, u32[]{:S(2)}) collective-permute-start(f32[16,64,128]{2,1,0:T(8,128)S(1)} %all-to-all-done.2.own_ref), channel_id=1, source_target_pairs={{0,128},{128,0},{1,129},{129,1},{2,130},{130,2},{3,131},{131,3},{4... | collective-permute-start | bytes 1572872 | tf_op jit(solution)/shard_map/ppermute | solution.py:275
  77.9 3.7 %all-to-all-start.3 = ((f32[16,192,128]{2,1,0:T(8,128)}), f32[16,192,128]{2,1,0:T(8,128)S(1)}, u32[]{:S(2)}, u32[]{:S(2)}) async-start(f32[16,192,128]{2,1,0:T(8,128)} %shard_map.76), calls=%async_computation.3 | async-start | bytes 3145728 | tf_op jit(solution)/shard_map/all_to_all | solution.py:306
  81.6 0.0 collective-permute-done.other_ref
  81.6 13.5 %shard_map.77 = (f32[512,512]{1,0:T(8,128)}, f32[4,128,128]{2,1,0:T(8,128)}) custom-call(f32[16,64,128]{2,1,0:T(8,128)S(1)} %all-to-all-done.2.own_ref, f32[16,64,128]{2,1,0:T(8,128)S(1)} %collective-permute-done.other_ref), custom_call_target="tpu_custom_call" | custom-call | flops 14000000000 | bytes 42000000 | tf_op jit(solution)/shard_map/pallas_call | solution.py:262
  95.1 13.2 %all-to-all-done.3.own_ref = f32[16,192,128]{2,1,0:T(8,128)S(1)} async-done(((f32[16,192,128]{2,1,0:T(8,128)}), f32[16,192,128]{2,1,0:T(8,128)S(1)}, u32[]{:S(2)}, u32[]{:S(2)}) %all-to-all-start.3) | async-done | bytes 1572896 | tf_op jit(solution)/shard_map/all_to_all | solution.py:306
  108.3 0.8 collective-permute-start.1
  109.1 0.0 collective-permute-start.2
  109.1 4.6 %all-to-all-start.4 = ((f32[16,84,256]{2,1,0:T(8,128)}), f32[16,84,256]{2,1,0:T(8,128)}, u32[]{:S(2)}, u32[]{:S(2)}) async-start(f32[16,84,256]{2,1,0:T(8,128)} %reshape_squeeze.11), calls=%async_computation.4 | async-start | bytes 2883584 | tf_op jit(solution)/shard_map/all_to_all | solution.py:316
  113.7 0.0 collective-permute-done.2.rest_other_ref
  113.7 0.0 collective-permute-done.1.other_ref
  113.7 21.4 %shard_map.78 = (f32[512,128]{1,0:T(8,128)}, f32[256,512]{1,0:T(8,128)}, f32[84,128]{1,0:T(8,128)}, f32[84,256]{1,0:T(8,128)S(1)}) custom-call(f32[16,192,128]{2,1,0:T(8,128)S(1)} %all-to-all-done.3.own_ref, f32[16,192,128]{2,1,0:T(8,128)} %collective-permute-done.1.other_ref, f32[8,48,128]{2,1,0:T(8,128)S(1)} %get-tuple-element.25.rest_own_ref, ...), custom_call_target="tpu_custom_call" | custom-call | flops 20000000000 | bytes 60000000 | tf_op jit(solution)/shard_map/pallas_call | solution.py:262
  135.0 1.2 all-to-all-done.4
  136.2 2.1 %fusion = f32[84,256]{1,0:T(8,128)} fusion(f32[16,84,256]{2,1,0:T(8,128)} %all-to-all-done.4, f32[84,256]{1,0:T(8,128)S(1)} %get-tuple-element.33), kind=kLoop, calls=%fused_computation.1 | loop fusion | flops 344064 | bytes 1548288 | tf_op jit(solution)/shard_map/add | solution.py:330
  (5 shorter events, 0.1 us)
Async XLA Ops:
  3.2 8.8 %copy-start = (f32[1,1344,256]{2,1,0:T(8,128)S(1)}, f32[1,1344,256]{2,1,0:T(8,128)}, u32[]{:S(2)}) copy-start(f32[1,1344,256]{2,1,0:T(8,128)} %param.7) | copy-start | bytes 4128772
  3.3 30.9 %all-to-all-start = ((f32[32,96,128]{2,1,0:T(8,128)}), f32[32,96,128]{2,1,0:T(8,128)S(1)}, u32[]{:S(2)}, u32[]{:S(2)}) async-start(f32[32,96,128]{2,1,0:T(8,128)} %shard_map.75), calls=%async_computation | async-start | bytes 3145728 | tf_op jit(solution)/shard_map/all_to_all | solution.py:295
  57.6 18.4 %all-to-all-start.2 = ((f32[16,64,128]{2,1,0:T(8,128)}), f32[16,64,128]{2,1,0:T(8,128)S(1)}, u32[]{:S(2)}, u32[]{:S(2)}) async-start(f32[16,64,128]{2,1,0:T(8,128)} %broadcast_in_dim.7), calls=%async_computation.2 | async-start | bytes 1048576 | tf_op jit(solution)/shard_map/all_to_all | solution.py:280
  76.0 5.5 %collective-permute-start = (f32[16,64,128]{2,1,0:T(8,128)S(1)}, f32[16,64,128]{2,1,0:T(8,128)S(1)}, u32[]{:S(2)}, u32[]{:S(2)}) collective-permute-start(f32[16,64,128]{2,1,0:T(8,128)S(1)} %all-to-all-done.2.own_ref), channel_id=1, source_target_pairs={{0,128},{128,0},{1,129},{129,1},{2,130},{130,2},{3,131},{131,3},{4... | collective-permute-start | bytes 1572872 | tf_op jit(solution)/shard_map/ppermute | solution.py:275
  77.9 30.4 %all-to-all-start.3 = ((f32[16,192,128]{2,1,0:T(8,128)}), f32[16,192,128]{2,1,0:T(8,128)S(1)}, u32[]{:S(2)}, u32[]{:S(2)}) async-start(f32[16,192,128]{2,1,0:T(8,128)} %shard_map.76), calls=%async_computation.3 | async-start | bytes 3145728 | tf_op jit(solution)/shard_map/all_to_all | solution.py:306
  108.3 5.4 %collective-permute-start.1 = (f32[16,192,128]{2,1,0:T(8,128)S(1)}, f32[16,192,128]{2,1,0:T(8,128)}, u32[]{:S(2)}, u32[]{:S(2)}) collective-permute-start(f32[16,192,128]{2,1,0:T(8,128)S(1)} %all-to-all-done.3.own_ref), channel_id=1, source_target_pairs={{0,128},{128,0},{1,129},{129,1},{2,130},{130,2},{3,131},{131,3},{4... | collective-permute-start | bytes 4718600 | tf_op jit(solution)/shard_map/ppermute | solution.py:275
  109.1 4.6 %collective-permute-start.2 = (f32[8,48,128]{2,1,0:T(8,128)S(1)}, f32[8,48,128]{2,1,0:T(8,128)S(1)}, u32[]{:S(2)}, u32[]{:S(2)}) collective-permute-start(f32[8,48,128]{2,1,0:T(8,128)S(1)} %get-tuple-element.26), channel_id=1, source_target_pairs={{0,128},{128,0},{1,129},{129,1},{2,130},{130,2},{3,131},{131,3},{4... | collective-permute-start | bytes 589832 | tf_op jit(solution)/shard_map/ppermute | solution.py:275
  109.1 27.2 %all-to-all-start.4 = ((f32[16,84,256]{2,1,0:T(8,128)}), f32[16,84,256]{2,1,0:T(8,128)}, u32[]{:S(2)}, u32[]{:S(2)}) async-start(f32[16,84,256]{2,1,0:T(8,128)} %reshape_squeeze.11), calls=%async_computation.4 | async-start | bytes 2883584 | tf_op jit(solution)/shard_map/all_to_all | solution.py:316

commit v9 on v6

--- a/solution.py
+++ b/solution.py
@@ -123,19 +123,41 @@
     return pl.ds(pl.multiple_of(index * step, step), step)
 
 
-def pack_kernel(top_ref, win_ref, rest_ref, out_ref, whole_ref, sems):
-    moves = [
+def pack_kernel(top_ref, win_ref, rest_ref, out_ref, whole_ref, pieces_ref, sems):
+    moves = [(rest_ref, whole_ref), (top_ref, out_ref.at[:, 32:48])] + [
         (win_ref.at[:, :, 128 * j : 128 * j + 128], out_ref.at[:, 8 * j : 8 * j + 8])
         for j in range(4)
-    ] + [(top_ref, out_ref.at[:, 32:48]), (rest_ref, whole_ref)]
+    ]
     copies = [pltpu.make_async_copy(*move, sems.at[n]) for n, move in enumerate(moves)]
-    for copy in copies[::-1]:
+    for copy in copies:
         copy.start()
-    for copy in copies[::-1]:
+    copies[0].wait()
+    for piece in range(pieces_ref.shape[0]):
+        pieces_ref[piece, 40:48] = jnp.zeros((8, 128), f32)
+        pieces_ref[piece, 0:42] = whole_ref[42 * piece : 42 * piece + 42]
+    last = pltpu.make_async_copy(pieces_ref, out_ref.at[:, 48:96], sems.at[6])
+    last.start()
+    for copy in copies[1:] + [last]:
         copy.wait()
-    for piece in range(out_ref.shape[0]):
-        out_ref[piece, 88:96] = jnp.zeros((8, 128), f32)
-        out_ref[piece, 48:90] = whole_ref[42 * piece : 42 * piece + 42]
+
+
+def finish_kernel(parts_ref, product_ref, out_ref, held_ref, sems):
+    n = sems.shape[0]
+    each = parts_ref.shape[0] // n
+    copies = [
+        pltpu.make_async_copy(
+            parts_ref.at[each * i : each * i + each], held_ref.at[each * i : each * i + each], sems.at[i]
+        )
+        for i in range(n)
+    ]
+    for copy in copies:
+        copy.start()
+    total = -product_ref[...]
+    for i, copy in enumerate(copies):
+        copy.wait()
+        for part in range(each * i, each * i + each):
+            total = total + held_ref[part]
+    out_ref[...] = total
 
 
 def fan_kernel(strips_ref, out_ref):
@@ -280,7 +302,8 @@
 def per_device(panel_top, panel_win, panel_rest, trail_rest):
     q = lax.axis_index("row")
     (pieces,) = call(
-        pack_kernel, [(32, 96, 128)], [(1344, 128), pltpu.SemaphoreType.DMA((6,))], 2, 4,
+        pack_kernel, [pltpu.HBM((32, 96, 128), f32)],
+        [(1344, 128), (32, 48, 128), pltpu.SemaphoreType.DMA((7,))], 2, 4,
         *(
             pltpu.with_memory_space_constraint(x, pltpu.HBM)
             for x in (
@@ -288,6 +311,7 @@
             )
         ),
         in_specs=[pl.BlockSpec(memory_space=pltpu.HBM)] * 3,
+        out_specs=(pl.BlockSpec(memory_space=pltpu.HBM),),
     )
     parts = lax.all_to_all(pieces, ("layer", "row"), 0, 0)
     sums = jnp.sum(parts.reshape(16, 2, 96, 128), axis=0)
@@ -325,9 +349,11 @@
         in_specs=[pl.BlockSpec(memory_space=pltpu.VMEM)] * 6
         + [pl.BlockSpec(memory_space=pltpu.HBM)] * 3,
     )
-    schur = trail_parts[0] - product
-    for part in range(1, 16):
-        schur = schur + trail_parts[part]
+    (schur,) = call(
+        finish_kernel, [(84, 256)], [(16, 84, 256), pltpu.SemaphoreType.DMA((4,))], 1, 4,
+        pltpu.with_memory_space_constraint(trail_parts, pltpu.HBM), product,
+        in_specs=[pl.BlockSpec(memory_space=pltpu.HBM), pl.BlockSpec(memory_space=pltpu.VMEM)],
+    )
     return top_block, win_block, rest_block, schur
 
 

time: 139 us -> 163 us (1.17)
  Pallas kernels: 38.3 us -> 61.8 us
  other arithmetic: 2.23 us -> 0.09 us
    pallas_call x4 -> x5, Pallas kernels: 38.3 us -> 61.8 us  [call(): pl.pallas_call(kernel, out_shape=tuple((shape(s) for s in outs)), scratch...]
    add x1 -> x0, other arithmetic: 2.14 us -> none  [per_device(): schur = schur + trail_parts[part]]
  transfers between devices with their start and end apart: 8 -> 8, of which waited for: 5 -> 5; matrix products, arithmetic and copies ran while one was open for 1% -> 1% of each run, Pallas kernels for 26% -> 21%
where the time goes in v9:
time: 163 us; the launch traced here: 162 us
  Pallas kernels  61.8 us (38%)
  waiting for transfers between devices  57.7 us (35%)
  starting transfers between devices  36.2 us (22%)
  local copies, waits for them, and re-layouts  5.39 us (3%)
    pallas_call x5, Pallas kernels, call(): pl.pallas_call(kernel, out_shape=tuple((shape(s) for s in outs)), scratch...  61.8 us
    all_to_all x2, waiting for transfers between devices, spread(): lax.all_to_all(jnp.broadcast_to(value, (n,) + value.shape), axis, 0, 0)  29.8 us
    all_to_all x1, waiting for transfers between devices, per_device(): parts = lax.all_to_all(pieces, ('layer', 'row'), 0, 0)  20.9 us
    all_to_all x2, starting transfers between devices, spread(): lax.all_to_all(jnp.broadcast_to(value, (n,) + value.shape), axis, 0, 0)  15.1 us
    all_to_all x1, starting transfers between devices, per_device(): parts = lax.all_to_all(pieces, ('layer', 'row'), 0, 0)  8.73 us
    all_to_all x1, starting transfers between devices, per_device(): trail_parts = lax.all_to_all(trail, 'layer', 0, 0)  4.59 us
    all_to_all x1, waiting for transfers between devices, per_device(): trail_parts = lax.all_to_all(trail, 'layer', 0, 0)  4.12 us
    ppermute x3, starting transfers between devices, swap_rows(): return lax.ppermute(value, 'row', [(0, 1), (1, 0)])  4.09 us
  transfers between devices with their start and end apart: 8, of which 5 were waited for; matrix products, arithmetic and copies ran while one was open for 1% of the time, Pallas kernels for 21%

profile of v9, /device:TPU:1, one launch (start us, length us, event | category | flops | bytes accessed | tf_op | source)
XLA Modules:
  0.0 162.0 jit_solution(16214435654665447036)
XLA Ops:
  0.6 25.0 %shard_map.75 = f32[32,96,128]{2,1,0:T(8,128)} custom-call(f32[32,16,128]{2,1,0:T(8,128)} %bitcast.13, f32[32,8,512]{2,1,0:T(8,128)} %bitcast.12, f32[1344,128]{1,0:T(8,128)} %bitcast.11), custom_call_target="tpu_custom_call" | custom-call | flops 2000000000 | bytes 6000000 | tf_op jit(solution)/shard_map/pallas_call | solution.py:281
  25.6 0.0 copy-start.2
  25.6 8.7 %all-to-all-start = ((f32[32,96,128]{2,1,0:T(8,128)}), f32[32,96,128]{2,1,0:T(8,128)S(1)}, u32[]{:S(2)}, u32[]{:S(2)}) async-start(f32[32,96,128]{2,1,0:T(8,128)} %shard_map.75), calls=%async_computation | async-start | bytes 3145728 | tf_op jit(solution)/shard_map/all_to_all | solution.py:316
  34.4 0.0 copy-done.2
  34.4 1.2 reshape_squeeze.11
  35.6 20.9 %all-to-all-done = f32[32,96,128]{2,1,0:T(8,128)S(1)} async-done(((f32[32,96,128]{2,1,0:T(8,128)}), f32[32,96,128]{2,1,0:T(8,128)S(1)}, u32[]{:S(2)}, u32[]{:S(2)}) %all-to-all-start) | async-done | bytes 1572896 | tf_op jit(solution)/shard_map/all_to_all | solution.py:316
  56.6 0.1 reduce_sum.9
  56.7 0.8 broadcast_in_dim.6
  57.5 8.2 %all-to-all-start.1 = ((f32[8,128,128]{2,1,0:T(8,128)}), f32[8,128,128]{2,1,0:T(8,128)S(1)}, u32[]{:S(2)}, u32[]{:S(2)}) async-start(f32[8,128,128]{2,1,0:T(8,128)} %broadcast_in_dim.6), calls=%async_computation.1 | async-start | bytes 1048576 | tf_op jit(solution)/shard_map/all_to_all | solution.py:299
  65.7 15.3 %all-to-all-done.1.strips_ref = f32[8,128,128]{2,1,0:T(8,128)S(1)} async-done(((f32[8,128,128]{2,1,0:T(8,128)}), f32[8,128,128]{2,1,0:T(8,128)S(1)}, u32[]{:S(2)}, u32[]{:S(2)}) %all-to-all-start.1) | async-done | bytes 524320 | tf_op jit(solution)/shard_map/all_to_all | solution.py:299
  81.0 1.1 broadcast_in_dim.7
  82.1 6.9 %all-to-all-start.2 = ((f32[16,128,128]{2,1,0:T(8,128)}), f32[16,128,128]{2,1,0:T(8,128)S(1)}, u32[]{:S(2)}, u32[]{:S(2)}) async-start(f32[16,128,128]{2,1,0:T(8,128)} %broadcast_in_dim.7), calls=%async_computation.2 | async-start | bytes 2097152 | tf_op jit(solution)/shard_map/all_to_all | solution.py:299
  89.0 1.1 shard_map.76
  90.1 0.7 constant_dynamic-slice_fusion
  90.8 14.5 %all-to-all-done.2.own_ref = f32[16,128,128]{2,1,0:T(8,128)S(1)} async-done(((f32[16,128,128]{2,1,0:T(8,128)}), f32[16,128,128]{2,1,0:T(8,128)S(1)}, u32[]{:S(2)}, u32[]{:S(2)}) %all-to-all-start.2) | async-done | bytes 1048608 | tf_op jit(solution)/shard_map/all_to_all | solution.py:299
  105.3 2.2 %collective-permute-start = (f32[16,128,128]{2,1,0:T(8,128)S(1)}, f32[16,128,128]{2,1,0:T(8,128)S(1)}, u32[]{:S(2)}, u32[]{:S(2)}) collective-permute-start(f32[16,128,128]{2,1,0:T(8,128)S(1)} %all-to-all-done.2.own_ref), channel_id=1, source_target_pairs={{0,128},{128,0},{1,129},{129,1},{2,130},{130,2},{3,131},{131,3},{4... | collective-permute-start | bytes 3145736 | tf_op jit(solution)/shard_map/ppermute | solution.py:294
  107.5 0.0 collective-permute-start.1
  107.5 3.7 %all-to-all-start.3 = ((f32[16,128,128]{2,1,0:T(8,128)}), f32[16,128,128]{2,1,0:T(8,128)S(1)}, u32[]{:S(2)}, u32[]{:S(2)}) async-start(f32[16,128,128]{2,1,0:T(8,128)} %shard_map.76), calls=%async_computation.3 | async-start | bytes 2097152 | tf_op jit(solution)/shard_map/all_to_all | solution.py:330
  111.2 0.0 collective-permute-done.1.rest_other_ref
  111.2 0.0 collective-permute-done.other_ref
  111.2 13.7 %shard_map.77 = (f32[512,512]{1,0:T(8,128)}, f32[4,128,128]{2,1,0:T(8,128)}, f32[344,512]{1,0:T(8,128)}) custom-call(f32[16,128,128]{2,1,0:T(8,128)S(1)} %all-to-all-done.2.own_ref, f32[16,128,128]{2,1,0:T(8,128)S(1)} %collective-permute-done.other_ref, f32[8,48,128]{2,1,0:T(8,128)S(1)} %get-tuple-element.23.rest_own_ref, ...), custom_call_target="tpu_custom_call" | custom-call | flops 14000000000 | bytes 42000000 | tf_op jit(solution)/shard_map/pallas_call | solution.py:281
  124.9 2.8 %all-to-all-done.3.own2_ref = f32[16,128,128]{2,1,0:T(8,128)S(1)} async-done(((f32[16,128,128]{2,1,0:T(8,128)}), f32[16,128,128]{2,1,0:T(8,128)S(1)}, u32[]{:S(2)}, u32[]{:S(2)}) %all-to-all-start.3) | async-done | bytes 1048608 | tf_op jit(solution)/shard_map/all_to_all | solution.py:330
  127.7 1.9 %collective-permute-start.2 = (f32[16,128,128]{2,1,0:T(8,128)S(1)}, f32[16,128,128]{2,1,0:T(8,128)}, u32[]{:S(2)}, u32[]{:S(2)}) collective-permute-start(f32[16,128,128]{2,1,0:T(8,128)S(1)} %all-to-all-done.3.own2_ref), channel_id=1, source_target_pairs={{0,128},{128,0},{1,129},{129,1},{2,130},{130,2},{3,131},{131,3},{4... | collective-permute-start | bytes 3145736 | tf_op jit(solution)/shard_map/ppermute | solution.py:294
  129.6 4.6 %all-to-all-start.4 = ((f32[16,84,256]{2,1,0:T(8,128)}), f32[16,84,256]{2,1,0:T(8,128)}, u32[]{:S(2)}, u32[]{:S(2)}) async-start(f32[16,84,256]{2,1,0:T(8,128)} %reshape_squeeze.11), calls=%async_computation.4 | async-start | bytes 2883584 | tf_op jit(solution)/shard_map/all_to_all | solution.py:340
  134.2 0.0 collective-permute-done.2.other2_ref
  134.2 20.1 %shard_map.78 = (f32[512,128]{1,0:T(8,128)}, f32[256,512]{1,0:T(8,128)}, f32[84,128]{1,0:T(8,128)}, f32[84,256]{1,0:T(8,128)S(1)}) custom-call(f32[16,128,128]{2,1,0:T(8,128)S(1)} %all-to-all-done.2.own_ref, f32[16,128,128]{2,1,0:T(8,128)S(1)} %collective-permute-done.other_ref, f32[16,128,128]{2,1,0:T(8,128)S(1)} %all-to-all-done.3.own2_ref, ...), custom_call_target="tpu_custom_call" | custom-call | flops 20000000000 | bytes 60000000 | tf_op jit(solution)/shard_map/pallas_call | solution.py:281
  154.2 0.0 copy-start
  154.2 0.6 copy-done
  154.9 4.1 %all-to-all-done.4.parts_ref = f32[16,84,256]{2,1,0:T(8,128)} async-done(((f32[16,84,256]{2,1,0:T(8,128)}), f32[16,84,256]{2,1,0:T(8,128)}, u32[]{:S(2)}, u32[]{:S(2)}) %all-to-all-start.4) | async-done | bytes 1376288 | tf_op jit(solution)/shard_map/all_to_all | solution.py:340
  159.0 0.0 copy-start.1
  159.0 0.9 copy-done.1
  159.9 2.0 %shard_map.79 = f32[84,256]{1,0:T(8,128)} custom-call(f32[16,84,256]{2,1,0:T(8,128)} %all-to-all-done.4.parts_ref, f32[84,256]{1,0:T(8,128)S(1)} %copy-done.1), custom_call_target="tpu_custom_call" | custom-call | flops 1000000000 | bytes 3000000 | tf_op jit(solution)/shard_map/pallas_call | solution.py:281
  (4 shorter events, 0.0 us)
Async XLA Ops:
  25.6 8.8 %copy-start.2 = (f32[1,1344,256]{2,1,0:T(8,128)S(1)}, f32[1,1344,256]{2,1,0:T(8,128)}, u32[]{:S(2)}) copy-start(f32[1,1344,256]{2,1,0:T(8,128)} %param.7) | copy-start | bytes 4128772
  25.6 30.9 %all-to-all-start = ((f32[32,96,128]{2,1,0:T(8,128)}), f32[32,96,128]{2,1,0:T(8,128)S(1)}, u32[]{:S(2)}, u32[]{:S(2)}) async-start(f32[32,96,128]{2,1,0:T(8,128)} %shard_map.75), calls=%async_computation | async-start | bytes 3145728 | tf_op jit(solution)/shard_map/all_to_all | solution.py:316
  57.5 23.5 %all-to-all-start.1 = ((f32[8,128,128]{2,1,0:T(8,128)}), f32[8,128,128]{2,1,0:T(8,128)S(1)}, u32[]{:S(2)}, u32[]{:S(2)}) async-start(f32[8,128,128]{2,1,0:T(8,128)} %broadcast_in_dim.6), calls=%async_computation.1 | async-start | bytes 1048576 | tf_op jit(solution)/shard_map/all_to_all | solution.py:299
  82.1 23.2 %all-to-all-start.2 = ((f32[16,128,128]{2,1,0:T(8,128)}), f32[16,128,128]{2,1,0:T(8,128)S(1)}, u32[]{:S(2)}, u32[]{:S(2)}) async-start(f32[16,128,128]{2,1,0:T(8,128)} %broadcast_in_dim.7), calls=%async_computation.2 | async-start | bytes 2097152 | tf_op jit(solution)/shard_map/all_to_all | solution.py:299
  105.3 5.9 %collective-permute-start = (f32[16,128,128]{2,1,0:T(8,128)S(1)}, f32[16,128,128]{2,1,0:T(8,128)S(1)}, u32[]{:S(2)}, u32[]{:S(2)}) collective-permute-start(f32[16,128,128]{2,1,0:T(8,128)S(1)} %all-to-all-done.2.own_ref), channel_id=1, source_target_pairs={{0,128},{128,0},{1,129},{129,1},{2,130},{130,2},{3,131},{131,3},{4... | collective-permute-start | bytes 3145736 | tf_op jit(solution)/shard_map/ppermute | solution.py:294
  107.5 3.7 %collective-permute-start.1 = (f32[8,48,128]{2,1,0:T(8,128)}, f32[8,48,128]{2,1,0:T(8,128)S(1)}, u32[]{:S(2)}, u32[]{:S(2)}) collective-permute-start(f32[8,48,128]{2,1,0:T(8,128)} %get-tuple-element.24), channel_id=1, source_target_pairs={{0,128},{128,0},{1,129},{129,1},{2,130},{130,2},{3,131},{131,3},{4... | collective-permute-start | bytes 589832 | tf_op jit(solution)/shard_map/ppermute | solution.py:294
  107.5 20.1 %all-to-all-start.3 = ((f32[16,128,128]{2,1,0:T(8,128)}), f32[16,128,128]{2,1,0:T(8,128)S(1)}, u32[]{:S(2)}, u32[]{:S(2)}) async-start(f32[16,128,128]{2,1,0:T(8,128)} %shard_map.76), calls=%async_computation.3 | async-start | bytes 2097152 | tf_op jit(solution)/shard_map/all_to_all | solution.py:330
  127.7 6.5 %collective-permute-start.2 = (f32[16,128,128]{2,1,0:T(8,128)S(1)}, f32[16,128,128]{2,1,0:T(8,128)}, u32[]{:S(2)}, u32[]{:S(2)}) collective-permute-start(f32[16,128,128]{2,1,0:T(8,128)S(1)} %all-to-all-done.3.own2_ref), channel_id=1, source_target_pairs={{0,128},{128,0},{1,129},{129,1},{2,130},{130,2},{3,131},{131,3},{4... | collective-permute-start | bytes 3145736 | tf_op jit(solution)/shard_map/ppermute | solution.py:294
  129.6 29.4 %all-to-all-start.4 = ((f32[16,84,256]{2,1,0:T(8,128)}), f32[16,84,256]{2,1,0:T(8,128)}, u32[]{:S(2)}, u32[]{:S(2)}) async-start(f32[16,84,256]{2,1,0:T(8,128)} %reshape_squeeze.11), calls=%async_computation.4 | async-start | bytes 2883584 | tf_op jit(solution)/shard_map/all_to_all | solution.py:340
  154.2 0.6 copy-start
  159.0 0.9 copy-start.1
